TPU v7x, 128 devices: a whole 4x4x4 slice. The times are simulated.
128 devices in a mesh: row: 8 (over z_lo, y), col: 16 (over z_hi, x, core).
Axes of the slice: x: 4, y: 4, z: 4 (z_hi: 2, z_lo: 2; z = z_hi * 2 + z_lo), core: 2. Of those that a mesh axis runs over, the one named last changes fastest.
Arguments:
- init_temp: float32 [4, 2048, 8192], P(None, 'row', 'col'), may hold values from -6 to 6
- power: float32 [8192, 64, 64], P(('row', 'col')), may hold values from 0 to 3
- die_owner: int32 [8192, 1], P(('row', 'col')), may hold values from 0 to 127; in each aligned block of 64 rows (0 to 63, 64 to 127, ...) at most 2 rows name the same one
- die_tile: int32 [8192], P(('row', 'col')), may hold values from 0 to 31
- classes: int32 [4, 2048, 8192], P(None, 'row', 'col'), may hold values from 0 to 7
- cond_table: float32 [4, 8], replicated, may hold values from 0.2 to 1.5
- target: float32 [2048, 8192], P('row', 'col'), may hold values from -6 to 6
Outputs:
- final_temp: float32 [4, 2048, 8192], P(None, 'row', 'col')
- init_grad: float32 [4, 2048, 8192], P(None, 'row', 'col')
- die_grad: float32 [8192, 64, 64], P(('row', 'col'))
Inputs may be any that keep to these rules, and one draw needn't show every extreme that they name: `die_owner`: among the dies of one device (aligned blocks of 64 dies), at most 2 have the same owner.
All inputs are finite; a program needn't handle non-finite values.
Results may differ from a plain program's by a relative error of at most 0.000088.
Values sent between devices are 32-bit elements; how exact they have to be, the bound alone decides.
A program may use at most 128 MiB of HBM per device.

v0:
```python
import jax
import jax.numpy as jnp
from jax import lax
from jax.sharding import PartitionSpec as P

TILE = 64
CLASSES = 8
STEPS = 6
CAP = 2


RATE = 0.1
AMBIENT_LOSS = 0.3


def extended(cells, sides, width):
    for axis, dim in sides:
        count = lax.axis_size(axis)
        ends = count - 1
        head = lax.slice_in_dim(cells, 0, width, axis=dim)
        tail = lax.slice_in_dim(cells, cells.shape[dim] - width, cells.shape[dim], axis=dim)
        cells = jnp.concatenate(
            [
                lax.ppermute(tail, axis, [(i, (i + 1) % count) for i in range(ends)]),
                cells,
                lax.ppermute(head, axis, [((i + 1) % count, i) for i in range(ends)]),
            ],
            axis=dim,
        )
    return cells


def conduct_root(classes, cond_table):
    conduct = jnp.zeros(classes.shape, cond_table.dtype)
    for label in range(CLASSES):
        conduct = conduct + jnp.where(classes == label, cond_table[:, label][:, None, None], 0.0)
    return jnp.sqrt(conduct)


def advance(field, root_cond, source):
    middle = field[:, 1:-1, 1:-1]
    roots = root_cond[:, 1:-1, 1:-1]
    inflow = roots * root_cond[:, :-2, 1:-1] * (field[:, :-2, 1:-1] - middle)
    inflow = inflow + roots * root_cond[:, 2:, 1:-1] * (field[:, 2:, 1:-1] - middle)
    inflow = inflow + roots * root_cond[:, 1:-1, :-2] * (field[:, 1:-1, :-2] - middle)
    inflow = inflow + roots * root_cond[:, 1:-1, 2:] * (field[:, 1:-1, 2:] - middle)
    vertical = roots[1:] * roots[:-1] * (middle[1:] - middle[:-1])
    zero_layer = jnp.zeros_like(middle[:1])
    inflow = (
        inflow
        + jnp.concatenate([vertical, zero_layer], 0)
        - jnp.concatenate([zero_layer, vertical], 0)
    )
    inflow = inflow - AMBIENT_LOSS * jnp.concatenate([jnp.zeros_like(middle[:-1]), middle[-1:]], 0)
    if source is not None:
        inflow = inflow + jnp.concatenate([source[None], jnp.zeros_like(middle[1:])], 0)
    return middle + RATE * inflow


def step_rim(field):
    return extended(field, (("row", 1), ("col", 2)), 1)


def send_dies(outbound, tile_ids, row_count, col_count):
    received, recv_tiles = (
        lax.all_to_all(
            outbound.reshape(row_count * col_count, CAP, -1),
            ("row", "col"),
            split_axis=0,
            concat_axis=0,
            tiled=True,
        ),
        lax.all_to_all(
            tile_ids.reshape(row_count * col_count, CAP),
            ("row", "col"),
            split_axis=0,
            concat_axis=0,
            tiled=True,
        ),
    )
    return (
        received.reshape(row_count * col_count * CAP, -1),
        recv_tiles.reshape(row_count * col_count * CAP),
    )


def return_grads(backward, row_count, col_count):
    returned = lax.all_to_all(
        backward.reshape(row_count * col_count, CAP, -1),
        ("row", "col"),
        split_axis=0,
        concat_axis=0,
        tiled=True,
    )
    return returned.reshape(row_count * col_count * CAP, -1)


def on_device(init_temp, power, die_owner, die_tile, classes, cond_table, target):
    row_count = lax.axis_size("row")
    col_count = lax.axis_size("col")
    devices_all = row_count * col_count
    layers, height, breadth = init_temp.shape
    tile_rows = height // TILE
    tile_cols = breadth // TILE
    die_count = power.shape[0]
    highest = lax.Precision.HIGHEST
    power_flat = power.reshape(die_count, TILE * TILE)
    owners = die_owner[:, 0]
    ordinal = jnp.arange(die_count, dtype=jnp.int32)
    same_owner = (owners[:, None] == owners[None, :]) & (ordinal[:, None] < ordinal[None, :])
    ranking = jnp.sum(same_owner.astype(jnp.int32), axis=0)
    slot_index = owners * CAP + ranking
    all_slots = jnp.arange(devices_all * CAP, dtype=jnp.int32)
    matched = all_slots[:, None] == slot_index[None, :]
    send_hot = matched.astype(jnp.float32)
    outbound = jnp.dot(send_hot, power_flat, precision=highest)
    tile_ids = jnp.sum(jnp.where(matched, die_tile[None, :] + 1, 0), axis=1) - 1
    received, recv_tiles = send_dies(outbound, tile_ids, row_count, col_count)
    tile_range = jnp.arange(tile_rows * tile_cols, dtype=jnp.int32)
    recv_hot = (tile_range[:, None] == recv_tiles[None, :]).astype(jnp.float32)
    source_tiles = jnp.dot(recv_hot, received, precision=highest)
    source = (
        source_tiles.reshape(tile_rows, tile_cols, TILE, TILE)
        .transpose(0, 2, 1, 3)
        .reshape(height, breadth)
    )
    root_cond = conduct_root(classes, cond_table)
    padded_roots = extended(root_cond, (("row", 1), ("col", 2)), 1)
    heat_field = init_temp
    for step_index in range(STEPS):
        heat_field = advance(step_rim(heat_field), padded_roots, source)
    adjoint = jnp.concatenate([(heat_field[0] - target)[None], jnp.zeros_like(heat_field[1:])], 0)
    grad_sum = jnp.zeros_like(target)
    for step_index in range(STEPS):
        grad_sum = grad_sum + adjoint[0]
        adjoint = advance(step_rim(adjoint), padded_roots, None)
    grad_tiles = (
        grad_sum.reshape(tile_rows, TILE, tile_cols, TILE)
        .transpose(0, 2, 1, 3)
        .reshape(tile_rows * tile_cols, TILE * TILE)
    )
    backward = jnp.dot(recv_hot.T, grad_tiles, precision=highest)
    returned = return_grads(backward, row_count, col_count)
    die_grad = (RATE * jnp.dot(send_hot.T, returned, precision=highest)).reshape(
        die_count, TILE, TILE
    )
    return (heat_field, adjoint, die_grad)


def solution(mesh):
    in_specs = (
        P(None, "row", "col"),
        P(("row", "col"), None, None),
        P(("row", "col"), None),
        P(("row", "col")),
        P(None, "row", "col"),
        P(),
        P("row", "col"),
    )
    out_specs = (P(None, "row", "col"), P(None, "row", "col"), P(("row", "col"), None, None))
    return jax.shard_map(
        on_device, mesh=mesh, in_specs=in_specs, out_specs=out_specs, check_vma=False
    )
```

profile of v0, /device:TPU:15, one launch (start us, length us, event | category | flops | bytes accessed | tf_op | source)
XLA Modules:
  0.0 618.8 jit_solution(14175289675788893918)
XLA Ops:
  3.0 10.6 %all-to-all-start = ((s32[128,1,2]{2,1,0:T(1,128)}), s32[128,1,2]{2,1,0:T(1,128)S(1)}, u32[]{:S(2)}, u32[]{:S(2)}) async-start(s32[128,1,2]{2,1,0:T(1,128)} %bitcast.1), calls=%async_computation | async-start | bytes 131072 | tf_op jit(solution)/shard_map/all_to_all | solution.py:73
  17.7 5.2 copy.499
  23.0 10.2 %all-to-all-start.1 = ((f32[128,2,4096]{2,1,0:T(2,128)}), f32[128,2,4096]{2,1,0:T(2,128)}, u32[]{:S(2)}, u32[]{:S(2)}) async-start(f32[128,2,4096]{2,1,0:T(2,128)} %copy.499), calls=%async_computation.1 | async-start | bytes 8388608 | tf_op jit(solution)/shard_map/all_to_all | solution.py:66
  33.5 3.8 add_sqrt_fusion
  50.5 28.1 %collective-permute-done = f32[4,1,512]{2,0,1:T(4,128)S(1)} collective-permute-done((f32[4,1,512]{2,0,1:T(4,128)S(1)}, f32[4,1,512]{2,0,1:T(4,128)S(1)}, u32[]{:S(2)}, u32[]{:S(2)}) %collective-permute-start) | collective-permute-done | bytes 8224 | tf_op jit(solution)/shard_map/ppermute | solution.py:24
  79.1 8.9 %collective-permute-start.4 = (f32[4,258,1]{1,0,2:T(4,128)S(1)}, f32[4,258,1]{1,0,2:T(4,128)S(1)}, u32[]{:S(2)}, u32[]{:S(2)}) collective-permute-start(f32[4,258,1]{1,0,2:T(4,128)S(1)} %copy.488), channel_id=1, source_target_pairs={{0,1},{1,2},{2,3},{3,4},{4,5},{5,6},{6,7},{7,8},{8,9},{9,10},{10,1... | collective-permute-start | bytes 12392 | tf_op jit(solution)/shard_map/ppermute | solution.py:24
  92.0 7.3 %collective-permute-start.5 = (f32[4,258,1]{1,0,2:T(4,128)S(1)}, f32[4,258,1]{1,0,2:T(4,128)S(1)}, u32[]{:S(2)}, u32[]{:S(2)}) collective-permute-start(f32[4,258,1]{1,0,2:T(4,128)S(1)} %copy.492), channel_id=1, source_target_pairs={{0,1},{1,2},{2,3},{3,4},{4,5},{5,6},{6,7},{7,8},{8,9},{9,10},{10,1... | collective-permute-start | bytes 12392 | tf_op jit(solution)/shard_map/ppermute | solution.py:24
  109.1 6.1 reshape.130
  115.2 5.6 copy.500
  120.8 6.3 %convolution_bitcast_fusion = f32[4,64,8,64]{3,2,1,0:T(8,128)} fusion(f32[64,64,256,1]{2,1,0,3:T(8,128)} %bitcast.61, s32[256]{0:T(256)S(1)} %eq.158, s32[4,8]{1,0:T(4,128)S(1)} %multiply_add_fusion), kind=kOutput, calls=%fused_computation.335 | convolution fusion | flops 402661376 | bytes 4719744 | tf_op jit(solution)/shard_map/dot_general | solution.py:121
  128.6 11.5 %fusion.12 = (f32[4,256,512]{2,1,0:T(8,128)S(1)}, f32[4,256,512]{2,1,0:T(8,128)}, f32[4,256,512]{2,1,0:T(8,128)}) fusion(f32[4,256,512]{2,1,0:T(8,128)} %param.7, f32[1,256,512]{2,1,0:T(8,128)S(1)} %broadcast_in_dim_reshape.2, f32[4,258,1]{2,1,0:T(8,128)} %copy.497, f32[4,1,512]{2,1,0:T(1,128)S(1)} %copy.485, f32[4,1,512]{2,1,0:T(1,128)S(1)} %copy.481, ...), kind=kLoop, calls=%fused_computation.27 | loop fusion | flops 19922944 | bytes 13156480 | tf_op jit(solution)/shard_map/add | solution.py:57
  149.0 6.9 %collective-permute-start.10 = (f32[4,258,1]{1,0,2:T(4,128)S(1)}, f32[4,258,1]{1,0,2:T(4,128)S(1)}, u32[]{:S(2)}, u32[]{:S(2)}) collective-permute-start(f32[4,258,1]{1,0,2:T(4,128)S(1)} %copy.507), channel_id=1, source_target_pairs={{0,1},{1,2},{2,3},{3,4},{4,5},{5,6},{6,7},{7,8},{8,9},{9,10},{10,1... | collective-permute-start | bytes 12392 | tf_op jit(solution)/shard_map/ppermute | solution.py:24
  159.1 4.1 fusion.202
  166.8 9.5 %fusion.14 = f32[4,256,512]{2,1,0:T(8,128)S(1)} fusion(f32[4,256,512]{2,1,0:T(8,128)} %copy-done.13, f32[1,256,512]{2,1,0:T(8,128)S(1)} %broadcast_in_dim_reshape.2, f32[4,256,512]{2,1,0:T(8,128)} %get-tuple-element.22, f32[4,258,1]{2,1,0:T(8,128)} %copy.510, f32[4,1,512]{2,1,0:T(1,128)S(1)} %copy.504, f32[4,1,512]{2,1,0:T(1,128)S(1)} %copy.502, ...), kind=kLoop, calls=%fused_computation.29 | loop fusion | flops 15728640 | bytes 13148224 | tf_op jit(solution)/shard_map/add | solution.py:57
  186.8 8.0 %collective-permute-start.14 = (f32[4,258,1]{1,0,2:T(4,128)S(1)}, f32[4,258,1]{1,0,2:T(4,128)S(1)}, u32[]{:S(2)}, u32[]{:S(2)}) collective-permute-start(f32[4,258,1]{1,0,2:T(4,128)S(1)} %copy.517), channel_id=1, source_target_pairs={{0,1},{1,2},{2,3},{3,4},{4,5},{5,6},{6,7},{7,8},{8,9},{9,10},{10,1... | collective-permute-start | bytes 12392 | tf_op jit(solution)/shard_map/ppermute | solution.py:24
  198.0 4.1 fusion.201
  205.7 9.5 %fusion.16 = f32[4,256,512]{2,1,0:T(8,128)S(1)} fusion(f32[4,256,512]{2,1,0:T(8,128)} %copy-done.10, f32[1,256,512]{2,1,0:T(8,128)S(1)} %broadcast_in_dim_reshape.2, f32[4,256,512]{2,1,0:T(8,128)} %get-tuple-element.22, f32[4,258,1]{2,1,0:T(8,128)} %copy.520, f32[4,1,512]{2,1,0:T(1,128)S(1)} %copy.514, f32[4,1,512]{2,1,0:T(1,128)S(1)} %copy.512, ...), kind=kLoop, calls=%fused_computation.31 | loop fusion | flops 15728640 | bytes 13148224 | tf_op jit(solution)/shard_map/add | solution.py:57
  226.2 6.9 %collective-permute-start.18 = (f32[4,258,1]{1,0,2:T(4,128)S(1)}, f32[4,258,1]{1,0,2:T(4,128)S(1)}, u32[]{:S(2)}, u32[]{:S(2)}) collective-permute-start(f32[4,258,1]{1,0,2:T(4,128)S(1)} %copy.527), channel_id=1, source_target_pairs={{0,1},{1,2},{2,3},{3,4},{4,5},{5,6},{6,7},{7,8},{8,9},{9,10},{10,1... | collective-permute-start | bytes 12392 | tf_op jit(solution)/shard_map/ppermute | solution.py:24
  236.3 4.1 fusion.200
  244.0 9.5 %fusion.18 = f32[4,256,512]{2,1,0:T(8,128)S(1)} fusion(f32[4,256,512]{2,1,0:T(8,128)} %copy-done.11, f32[1,256,512]{2,1,0:T(8,128)S(1)} %broadcast_in_dim_reshape.2, f32[4,256,512]{2,1,0:T(8,128)} %get-tuple-element.22, f32[4,258,1]{2,1,0:T(8,128)} %copy.530, f32[4,1,512]{2,1,0:T(1,128)S(1)} %copy.524, f32[4,1,512]{2,1,0:T(1,128)S(1)} %copy.522, ...), kind=kLoop, calls=%fused_computation.33 | loop fusion | flops 15728640 | bytes 13148224 | tf_op jit(solution)/shard_map/add | solution.py:57
  264.4 6.9 %collective-permute-start.22 = (f32[4,258,1]{1,0,2:T(4,128)S(1)}, f32[4,258,1]{1,0,2:T(4,128)S(1)}, u32[]{:S(2)}, u32[]{:S(2)}) collective-permute-start(f32[4,258,1]{1,0,2:T(4,128)S(1)} %copy.537), channel_id=1, source_target_pairs={{0,1},{1,2},{2,3},{3,4},{4,5},{5,6},{6,7},{7,8},{8,9},{9,10},{10,1... | collective-permute-start | bytes 12392 | tf_op jit(solution)/shard_map/ppermute | solution.py:24
  274.8 4.1 fusion.199
  282.2 9.5 %fusion.20 = f32[4,256,512]{2,1,0:T(8,128)S(1)} fusion(f32[4,256,512]{2,1,0:T(8,128)} %copy-done.12, f32[1,256,512]{2,1,0:T(8,128)S(1)} %broadcast_in_dim_reshape.2, f32[4,256,512]{2,1,0:T(8,128)} %get-tuple-element.22, f32[4,258,1]{2,1,0:T(8,128)} %copy.540, f32[4,1,512]{2,1,0:T(1,128)S(1)} %copy.534, f32[4,1,512]{2,1,0:T(1,128)S(1)} %copy.532, ...), kind=kLoop, calls=%fused_computation.35 | loop fusion | flops 15728640 | bytes 13148224 | tf_op jit(solution)/shard_map/add | solution.py:57
  302.7 7.1 %collective-permute-start.26 = (f32[4,258,1]{1,0,2:T(4,128)S(1)}, f32[4,258,1]{1,0,2:T(4,128)S(1)}, u32[]{:S(2)}, u32[]{:S(2)}) collective-permute-start(f32[4,258,1]{1,0,2:T(4,128)S(1)} %copy.547), channel_id=1, source_target_pairs={{0,1},{1,2},{2,3},{3,4},{4,5},{5,6},{6,7},{7,8},{8,9},{9,10},{10,1... | collective-permute-start | bytes 12392 | tf_op jit(solution)/shard_map/ppermute | solution.py:24
  313.0 4.1 fusion.198
  320.7 9.5 %fusion.22 = f32[4,256,512]{2,1,0:T(8,128)S(1)} fusion(f32[4,256,512]{2,1,0:T(8,128)} %copy-done.9, f32[1,256,512]{2,1,0:T(8,128)S(1)} %broadcast_in_dim_reshape.2, f32[4,256,512]{2,1,0:T(8,128)} %get-tuple-element.22, f32[4,258,1]{2,1,0:T(8,128)} %copy.550, f32[4,1,512]{2,1,0:T(1,128)S(1)} %copy.544, f32[4,1,512]{2,1,0:T(1,128)S(1)} %copy.542, ...), kind=kLoop, calls=%fused_computation.37 | loop fusion | flops 15728640 | bytes 13148224 | tf_op jit(solution)/shard_map/add | solution.py:57
  341.2 6.9 %collective-permute-start.30 = (f32[4,258,1]{1,0,2:T(4,128)S(1)}, f32[4,258,1]{1,0,2:T(4,128)S(1)}, u32[]{:S(2)}, u32[]{:S(2)}) collective-permute-start(f32[4,258,1]{1,0,2:T(4,128)S(1)} %copy.557), channel_id=1, source_target_pairs={{0,1},{1,2},{2,3},{3,4},{4,5},{5,6},{6,7},{7,8},{8,9},{9,10},{10,1... | collective-permute-start | bytes 12392 | tf_op jit(solution)/shard_map/ppermute | solution.py:24
  359.3 7.7 %pad_add_fusion.6 = f32[4,256,512]{2,1,0:T(8,128)S(1)} fusion(f32[1,256,512]{2,1,0:T(8,128)S(1)} %fusion.209, f32[4,256,512]{2,1,0:T(8,128)} %get-tuple-element.21, f32[4,256,512]{2,1,0:T(8,128)} %get-tuple-element.22, f32[4,258,1]{2,1,0:T(8,128)} %copy.560, f32[4,1,512]{2,1,0:T(1,128)S(1)} %copy.554, f32[4,256,512]{2,1,0:T(8,128)} %copy-done.15, ...), kind=kLoop, calls=%fused_computation.6 | loop fusion | flops 15204352 | bytes 14196800 | tf_op jit(solution)/shard_map/add | solution.py:57
  376.1 5.3 collective-permute-start.34
  383.6 4.1 fusion.197
  391.3 9.4 %fusion.94 = f32[4,256,512]{2,1,0:T(8,128)S(1)} fusion(f32[4,256,512]{2,1,0:T(8,128)} %copy-done, f32[4,256,512]{2,1,0:T(8,128)} %get-tuple-element.22, f32[4,258,1]{2,1,0:T(8,128)} %copy.570, f32[4,1,512]{2,1,0:T(1,128)S(1)} %copy.564, f32[4,1,512]{2,1,0:T(1,128)S(1)} %copy.562, f32[4,256,512]{2,1,0:T(8,128)} %get-tuple-element.21, ...), kind=kLoop, calls=%fused_computation.142 | loop fusion | flops 15204352 | bytes 12623936 | tf_op jit(solution)/shard_map/add | solution.py:57
  409.7 6.1 collective-permute-start.38
  418.0 4.1 fusion.196
  425.6 9.7 %fusion.78 = f32[4,256,512]{2,1,0:T(8,128)S(1)} fusion(f32[4,256,512]{2,1,0:T(8,128)} %copy-done.2, f32[4,256,512]{2,1,0:T(8,128)} %get-tuple-element.22, f32[4,258,1]{2,1,0:T(8,128)} %copy.580, f32[4,1,512]{2,1,0:T(1,128)S(1)} %copy.574, f32[4,1,512]{2,1,0:T(1,128)S(1)} %copy.572, f32[4,256,512]{2,1,0:T(8,128)} %get-tuple-element.21, ...), kind=kLoop, calls=%fused_computation.118 | loop fusion | flops 15204352 | bytes 12623936 | tf_op jit(solution)/shard_map/add | solution.py:57
  444.4 6.1 collective-permute-start.42
  452.7 4.1 fusion.195
  460.4 9.2 %fusion.62 = f32[4,256,512]{2,1,0:T(8,128)S(1)} fusion(f32[4,256,512]{2,1,0:T(8,128)} %copy-done.4, f32[4,256,512]{2,1,0:T(8,128)} %get-tuple-element.22, f32[4,258,1]{2,1,0:T(8,128)} %copy.590, f32[4,1,512]{2,1,0:T(1,128)S(1)} %copy.584, f32[4,1,512]{2,1,0:T(1,128)S(1)} %copy.582, f32[4,256,512]{2,1,0:T(8,128)} %get-tuple-element.21, ...), kind=kLoop, calls=%fused_computation.94 | loop fusion | flops 15204352 | bytes 12623936 | tf_op jit(solution)/shard_map/add | solution.py:57
  481.2 6.2 collective-permute-start.46
  489.5 4.1 fusion.194
  497.3 9.6 %fusion.46 = f32[4,256,512]{2,1,0:T(8,128)S(1)} fusion(f32[4,256,512]{2,1,0:T(8,128)} %copy-done.7, f32[4,256,512]{2,1,0:T(8,128)} %get-tuple-element.22, f32[4,258,1]{2,1,0:T(8,128)} %copy.600, f32[4,1,512]{2,1,0:T(1,128)S(1)} %copy.594, f32[4,1,512]{2,1,0:T(1,128)S(1)} %copy.592, f32[4,256,512]{2,1,0:T(8,128)} %get-tuple-element.21, ...), kind=kLoop, calls=%fused_computation.70 | loop fusion | flops 15204352 | bytes 12623936 | tf_op jit(solution)/shard_map/add | solution.py:57
  516.3 5.2 copy.613
  521.6 8.5 %all-to-all-start.2 = ((f32[128,2,4096]{2,1,0:T(2,128)}), f32[128,2,4096]{2,1,0:T(2,128)}, u32[]{:S(2)}, u32[]{:S(2)}) async-start(f32[128,2,4096]{2,1,0:T(2,128)} %copy.613), calls=%async_computation.2 | async-start | bytes 8388608 | tf_op jit(solution)/shard_map/all_to_all | solution.py:88
  536.3 39.1 %collective-permute-done.48 = f32[4,1,512]{2,0,1:T(4,128)S(1)} collective-permute-done((f32[4,1,512]{2,0,1:T(4,128)S(1)}, f32[4,1,512]{2,0,1:T(4,128)S(1)}, u32[]{:S(2)}, u32[]{:S(2)}) %collective-permute-start.48) | collective-permute-done | bytes 8224 | tf_op jit(solution)/shard_map/ppermute | solution.py:24
  577.3 8.9 %collective-permute-start.50 = (f32[4,258,1]{1,0,2:T(4,128)S(1)}, f32[4,258,1]{1,0,2:T(4,128)S(1)}, u32[]{:S(2)}, u32[]{:S(2)}) collective-permute-start(f32[4,258,1]{1,0,2:T(4,128)S(1)} %copy.607), channel_id=1, source_target_pairs={{0,1},{1,2},{2,3},{3,4},{4,5},{5,6},{6,7},{7,8},{8,9},{9,10},{10,1... | collective-permute-start | bytes 12392 | tf_op jit(solution)/shard_map/ppermute | solution.py:24
  588.6 4.1 fusion.193
  596.0 10.3 %fusion.30 = f32[4,256,512]{2,1,0:T(8,128)} fusion(f32[4,256,512]{2,1,0:T(8,128)} %copy-done.6, f32[4,256,512]{2,1,0:T(8,128)} %get-tuple-element.22, f32[4,258,1]{2,1,0:T(8,128)} %copy.610, f32[4,1,512]{2,1,0:T(1,128)S(1)} %copy.604, f32[4,1,512]{2,1,0:T(1,128)S(1)} %copy.602, f32[4,256,512]{2,1,0:T(8,128)} %get-tuple-element.21, ...), kind=kLoop, calls=%fused_computation.46 | loop fusion | flops 15204352 | bytes 12623936 | tf_op jit(solution)/shard_map/add | solution.py:57
  606.3 6.1 reshape.133
  612.4 3.9 convolution_multiply_fusion
  (312 shorter events, 230.5 us)
Async XLA Ops:
  3.0 20.0 %all-to-all-start = ((s32[128,1,2]{2,1,0:T(1,128)}), s32[128,1,2]{2,1,0:T(1,128)S(1)}, u32[]{:S(2)}, u32[]{:S(2)}) async-start(s32[128,1,2]{2,1,0:T(1,128)} %bitcast.1), calls=%async_computation | async-start | bytes 131072 | tf_op jit(solution)/shard_map/all_to_all | solution.py:73
  23.0 86.1 %all-to-all-start.1 = ((f32[128,2,4096]{2,1,0:T(2,128)}), f32[128,2,4096]{2,1,0:T(2,128)}, u32[]{:S(2)}, u32[]{:S(2)}) async-start(f32[128,2,4096]{2,1,0:T(2,128)} %copy.499), calls=%async_computation.1 | async-start | bytes 8388608 | tf_op jit(solution)/shard_map/all_to_all | solution.py:66
  37.4 41.2 %collective-permute-start = (f32[4,1,512]{2,0,1:T(4,128)S(1)}, f32[4,1,512]{2,0,1:T(4,128)S(1)}, u32[]{:S(2)}, u32[]{:S(2)}) collective-permute-start(f32[4,1,512]{2,0,1:T(4,128)S(1)} %copy.478), channel_id=1, source_target_pairs={{0,16},{16,32},{32,48},{48,64},{64,80},{80,96},{96,112},{1,17},{17... | collective-permute-start | bytes 24584 | tf_op jit(solution)/shard_map/ppermute | solution.py:24
  40.6 38.0 %collective-permute-start.2 = (f32[4,1,512]{2,0,1:T(4,128)S(1)}, f32[4,1,512]{2,0,1:T(4,128)S(1)}, u32[]{:S(2)}, u32[]{:S(2)}) collective-permute-start(f32[4,1,512]{2,0,1:T(4,128)S(1)} %copy.482), channel_id=1, source_target_pairs={{16,0},{32,16},{48,32},{64,48},{80,64},{96,80},{112,96},{17,1},{33... | collective-permute-start | bytes 24584 | tf_op jit(solution)/shard_map/ppermute | solution.py:26
  42.8 47.4 %collective-permute-start.1 = (f32[4,1,512]{2,0,1:T(4,128)S(1)}, f32[4,1,512]{2,0,1:T(4,128)S(1)}, u32[]{:S(2)}, u32[]{:S(2)}) collective-permute-start(f32[4,1,512]{2,0,1:T(4,128)S(1)} %copy.615), channel_id=1, source_target_pairs={{0,16},{16,32},{32,48},{48,64},{64,80},{80,96},{96,112},{1,17},{17... | collective-permute-start | bytes 24584 | tf_op jit(solution)/shard_map/ppermute | solution.py:24
  45.9 44.3 %collective-permute-start.3 = (f32[4,1,512]{2,0,1:T(4,128)S(1)}, f32[4,1,512]{2,0,1:T(4,128)S(1)}, u32[]{:S(2)}, u32[]{:S(2)}) collective-permute-start(f32[4,1,512]{2,0,1:T(4,128)S(1)} %copy.616), channel_id=1, source_target_pairs={{16,0},{32,16},{48,32},{64,48},{80,64},{96,80},{112,96},{17,1},{33... | collective-permute-start | bytes 24584 | tf_op jit(solution)/shard_map/ppermute | solution.py:26
  79.1 24.2 %collective-permute-start.4 = (f32[4,258,1]{1,0,2:T(4,128)S(1)}, f32[4,258,1]{1,0,2:T(4,128)S(1)}, u32[]{:S(2)}, u32[]{:S(2)}) collective-permute-start(f32[4,258,1]{1,0,2:T(4,128)S(1)} %copy.488), channel_id=1, source_target_pairs={{0,1},{1,2},{2,3},{3,4},{4,5},{5,6},{6,7},{7,8},{8,9},{9,10},{10,1... | collective-permute-start | bytes 12392 | tf_op jit(solution)/shard_map/ppermute | solution.py:24
  88.2 16.2 %collective-permute-start.6 = (f32[4,258,1]{1,0,2:T(4,128)S(1)}, f32[4,258,1]{1,0,2:T(4,128)S(1)}, u32[]{:S(2)}, u32[]{:S(2)}) collective-permute-start(f32[4,258,1]{1,0,2:T(4,128)S(1)} %copy.494), channel_id=1, source_target_pairs={{1,0},{2,1},{3,2},{4,3},{5,4},{6,5},{7,6},{8,7},{9,8},{10,9},{11,1... | collective-permute-start | bytes 12392 | tf_op jit(solution)/shard_map/ppermute | solution.py:26
  92.0 13.5 %collective-permute-start.5 = (f32[4,258,1]{1,0,2:T(4,128)S(1)}, f32[4,258,1]{1,0,2:T(4,128)S(1)}, u32[]{:S(2)}, u32[]{:S(2)}) collective-permute-start(f32[4,258,1]{1,0,2:T(4,128)S(1)} %copy.492), channel_id=1, source_target_pairs={{0,1},{1,2},{2,3},{3,4},{4,5},{5,6},{6,7},{7,8},{8,9},{9,10},{10,1... | collective-permute-start | bytes 12392 | tf_op jit(solution)/shard_map/ppermute | solution.py:24
  99.5 8.6 %collective-permute-start.7 = (f32[4,258,1]{1,0,2:T(4,128)S(1)}, f32[4,258,1]{1,0,2:T(4,128)S(1)}, u32[]{:S(2)}, u32[]{:S(2)}) collective-permute-start(f32[4,258,1]{1,0,2:T(4,128)S(1)} %copy.496), channel_id=1, source_target_pairs={{1,0},{2,1},{3,2},{4,3},{5,4},{6,5},{7,6},{8,7},{9,8},{10,9},{11,1... | collective-permute-start | bytes 12392 | tf_op jit(solution)/shard_map/ppermute | solution.py:26
  140.1 5.3 collective-permute-start.8
  149.0 15.3 %collective-permute-start.10 = (f32[4,258,1]{1,0,2:T(4,128)S(1)}, f32[4,258,1]{1,0,2:T(4,128)S(1)}, u32[]{:S(2)}, u32[]{:S(2)}) collective-permute-start(f32[4,258,1]{1,0,2:T(4,128)S(1)} %copy.507), channel_id=1, source_target_pairs={{0,1},{1,2},{2,3},{3,4},{4,5},{5,6},{6,7},{7,8},{8,9},{9,10},{10,1... | collective-permute-start | bytes 12392 | tf_op jit(solution)/shard_map/ppermute | solution.py:24
  157.2 8.6 %collective-permute-start.11 = (f32[4,258,1]{1,0,2:T(4,128)S(1)}, f32[4,258,1]{1,0,2:T(4,128)S(1)}, u32[]{:S(2)}, u32[]{:S(2)}) collective-permute-start(f32[4,258,1]{1,0,2:T(4,128)S(1)} %copy.509), channel_id=1, source_target_pairs={{1,0},{2,1},{3,2},{4,3},{5,4},{6,5},{7,6},{8,7},{9,8},{10,9},{11,1... | collective-permute-start | bytes 12392 | tf_op jit(solution)/shard_map/ppermute | solution.py:26
  176.3 5.5 collective-permute-start.12
  178.5 5.9 collective-permute-start.13
  186.8 15.3 %collective-permute-start.14 = (f32[4,258,1]{1,0,2:T(4,128)S(1)}, f32[4,258,1]{1,0,2:T(4,128)S(1)}, u32[]{:S(2)}, u32[]{:S(2)}) collective-permute-start(f32[4,258,1]{1,0,2:T(4,128)S(1)} %copy.517), channel_id=1, source_target_pairs={{0,1},{1,2},{2,3},{3,4},{4,5},{5,6},{6,7},{7,8},{8,9},{9,10},{10,1... | collective-permute-start | bytes 12392 | tf_op jit(solution)/shard_map/ppermute | solution.py:24
  196.1 8.6 %collective-permute-start.15 = (f32[4,258,1]{1,0,2:T(4,128)S(1)}, f32[4,258,1]{1,0,2:T(4,128)S(1)}, u32[]{:S(2)}, u32[]{:S(2)}) collective-permute-start(f32[4,258,1]{1,0,2:T(4,128)S(1)} %copy.519), channel_id=1, source_target_pairs={{1,0},{2,1},{3,2},{4,3},{5,4},{6,5},{7,6},{8,7},{9,8},{10,9},{11,1... | collective-permute-start | bytes 12392 | tf_op jit(solution)/shard_map/ppermute | solution.py:26
  215.2 5.6 collective-permute-start.16
  218.9 4.8 collective-permute-start.17
  226.2 14.2 %collective-permute-start.18 = (f32[4,258,1]{1,0,2:T(4,128)S(1)}, f32[4,258,1]{1,0,2:T(4,128)S(1)}, u32[]{:S(2)}, u32[]{:S(2)}) collective-permute-start(f32[4,258,1]{1,0,2:T(4,128)S(1)} %copy.527), channel_id=1, source_target_pairs={{0,1},{1,2},{2,3},{3,4},{4,5},{5,6},{6,7},{7,8},{8,9},{9,10},{10,1... | collective-permute-start | bytes 12392 | tf_op jit(solution)/shard_map/ppermute | solution.py:24
  234.4 8.6 %collective-permute-start.19 = (f32[4,258,1]{1,0,2:T(4,128)S(1)}, f32[4,258,1]{1,0,2:T(4,128)S(1)}, u32[]{:S(2)}, u32[]{:S(2)}) collective-permute-start(f32[4,258,1]{1,0,2:T(4,128)S(1)} %copy.529), channel_id=1, source_target_pairs={{1,0},{2,1},{3,2},{4,3},{5,4},{6,5},{7,6},{8,7},{9,8},{10,9},{11,1... | collective-permute-start | bytes 12392 | tf_op jit(solution)/shard_map/ppermute | solution.py:26
  253.5 5.6 collective-permute-start.20
  257.2 4.8 collective-permute-start.21
  264.4 14.4 %collective-permute-start.22 = (f32[4,258,1]{1,0,2:T(4,128)S(1)}, f32[4,258,1]{1,0,2:T(4,128)S(1)}, u32[]{:S(2)}, u32[]{:S(2)}) collective-permute-start(f32[4,258,1]{1,0,2:T(4,128)S(1)} %copy.537), channel_id=1, source_target_pairs={{0,1},{1,2},{2,3},{3,4},{4,5},{5,6},{6,7},{7,8},{8,9},{9,10},{10,1... | collective-permute-start | bytes 12392 | tf_op jit(solution)/shard_map/ppermute | solution.py:24
  272.6 8.6 %collective-permute-start.23 = (f32[4,258,1]{1,0,2:T(4,128)S(1)}, f32[4,258,1]{1,0,2:T(4,128)S(1)}, u32[]{:S(2)}, u32[]{:S(2)}) collective-permute-start(f32[4,258,1]{1,0,2:T(4,128)S(1)} %copy.539), channel_id=1, source_target_pairs={{1,0},{2,1},{3,2},{4,3},{5,4},{6,5},{7,6},{8,7},{9,8},{10,9},{11,1... | collective-permute-start | bytes 12392 | tf_op jit(solution)/shard_map/ppermute | solution.py:26
  291.8 5.6 collective-permute-start.24
  302.7 14.4 %collective-permute-start.26 = (f32[4,258,1]{1,0,2:T(4,128)S(1)}, f32[4,258,1]{1,0,2:T(4,128)S(1)}, u32[]{:S(2)}, u32[]{:S(2)}) collective-permute-start(f32[4,258,1]{1,0,2:T(4,128)S(1)} %copy.547), channel_id=1, source_target_pairs={{0,1},{1,2},{2,3},{3,4},{4,5},{5,6},{6,7},{7,8},{8,9},{9,10},{10,1... | collective-permute-start | bytes 12392 | tf_op jit(solution)/shard_map/ppermute | solution.py:24
  311.1 8.6 %collective-permute-start.27 = (f32[4,258,1]{1,0,2:T(4,128)S(1)}, f32[4,258,1]{1,0,2:T(4,128)S(1)}, u32[]{:S(2)}, u32[]{:S(2)}) collective-permute-start(f32[4,258,1]{1,0,2:T(4,128)S(1)} %copy.549), channel_id=1, source_target_pairs={{1,0},{2,1},{3,2},{4,3},{5,4},{6,5},{7,6},{8,7},{9,8},{10,9},{11,1... | collective-permute-start | bytes 12392 | tf_op jit(solution)/shard_map/ppermute | solution.py:26
  330.3 5.9 collective-permute-start.28
  341.2 11.9 %collective-permute-start.30 = (f32[4,258,1]{1,0,2:T(4,128)S(1)}, f32[4,258,1]{1,0,2:T(4,128)S(1)}, u32[]{:S(2)}, u32[]{:S(2)}) collective-permute-start(f32[4,258,1]{1,0,2:T(4,128)S(1)} %copy.557), channel_id=1, source_target_pairs={{0,1},{1,2},{2,3},{3,4},{4,5},{5,6},{6,7},{7,8},{8,9},{9,10},{10,1... | collective-permute-start | bytes 12392 | tf_op jit(solution)/shard_map/ppermute | solution.py:24
  348.3 8.6 %collective-permute-start.31 = (f32[4,258,1]{1,0,2:T(4,128)S(1)}, f32[4,258,1]{1,0,2:T(4,128)S(1)}, u32[]{:S(2)}, u32[]{:S(2)}) collective-permute-start(f32[4,258,1]{1,0,2:T(4,128)S(1)} %copy.559), channel_id=1, source_target_pairs={{1,0},{2,1},{3,2},{4,3},{5,4},{6,5},{7,6},{8,7},{9,8},{10,9},{11,1... | collective-permute-start | bytes 12392 | tf_op jit(solution)/shard_map/ppermute | solution.py:26
  367.1 5.6 collective-permute-start.32
  376.1 11.6 %collective-permute-start.34 = (f32[4,258,1]{1,0,2:T(4,128)S(1)}, f32[4,258,1]{1,0,2:T(4,128)S(1)}, u32[]{:S(2)}, u32[]{:S(2)}) collective-permute-start(f32[4,258,1]{1,0,2:T(4,128)S(1)} %copy.567), channel_id=1, source_target_pairs={{0,1},{1,2},{2,3},{3,4},{4,5},{5,6},{6,7},{7,8},{8,9},{9,10},{10,1... | collective-permute-start | bytes 12392 | tf_op jit(solution)/shard_map/ppermute | solution.py:24
  381.6 8.6 %collective-permute-start.35 = (f32[4,258,1]{1,0,2:T(4,128)S(1)}, f32[4,258,1]{1,0,2:T(4,128)S(1)}, u32[]{:S(2)}, u32[]{:S(2)}) collective-permute-start(f32[4,258,1]{1,0,2:T(4,128)S(1)} %copy.569), channel_id=1, source_target_pairs={{1,0},{2,1},{3,2},{4,3},{5,4},{6,5},{7,6},{8,7},{9,8},{10,9},{11,1... | collective-permute-start | bytes 12392 | tf_op jit(solution)/shard_map/ppermute | solution.py:26
  400.7 5.6 collective-permute-start.36
  409.7 12.4 %collective-permute-start.38 = (f32[4,258,1]{1,0,2:T(4,128)S(1)}, f32[4,258,1]{1,0,2:T(4,128)S(1)}, u32[]{:S(2)}, u32[]{:S(2)}) collective-permute-start(f32[4,258,1]{1,0,2:T(4,128)S(1)} %copy.577), channel_id=1, source_target_pairs={{0,1},{1,2},{2,3},{3,4},{4,5},{5,6},{6,7},{7,8},{8,9},{9,10},{10,1... | collective-permute-start | bytes 12392 | tf_op jit(solution)/shard_map/ppermute | solution.py:24
  416.0 8.6 %collective-permute-start.39 = (f32[4,258,1]{1,0,2:T(4,128)S(1)}, f32[4,258,1]{1,0,2:T(4,128)S(1)}, u32[]{:S(2)}, u32[]{:S(2)}) collective-permute-start(f32[4,258,1]{1,0,2:T(4,128)S(1)} %copy.579), channel_id=1, source_target_pairs={{1,0},{2,1},{3,2},{4,3},{5,4},{6,5},{7,6},{8,7},{9,8},{10,9},{11,1... | collective-permute-start | bytes 12392 | tf_op jit(solution)/shard_map/ppermute | solution.py:26
  435.4 5.6 collective-permute-start.40
  444.4 12.5 %collective-permute-start.42 = (f32[4,258,1]{1,0,2:T(4,128)S(1)}, f32[4,258,1]{1,0,2:T(4,128)S(1)}, u32[]{:S(2)}, u32[]{:S(2)}) collective-permute-start(f32[4,258,1]{1,0,2:T(4,128)S(1)} %copy.587), channel_id=1, source_target_pairs={{0,1},{1,2},{2,3},{3,4},{4,5},{5,6},{6,7},{7,8},{8,9},{9,10},{10,1... | collective-permute-start | bytes 12392 | tf_op jit(solution)/shard_map/ppermute | solution.py:24
  450.7 8.6 %collective-permute-start.43 = (f32[4,258,1]{1,0,2:T(4,128)S(1)}, f32[4,258,1]{1,0,2:T(4,128)S(1)}, u32[]{:S(2)}, u32[]{:S(2)}) collective-permute-start(f32[4,258,1]{1,0,2:T(4,128)S(1)} %copy.589), channel_id=1, source_target_pairs={{1,0},{2,1},{3,2},{4,3},{5,4},{6,5},{7,6},{8,7},{9,8},{10,9},{11,1... | collective-permute-start | bytes 12392 | tf_op jit(solution)/shard_map/ppermute | solution.py:26
  471.0 5.9 collective-permute-start.44
  481.2 12.4 %collective-permute-start.46 = (f32[4,258,1]{1,0,2:T(4,128)S(1)}, f32[4,258,1]{1,0,2:T(4,128)S(1)}, u32[]{:S(2)}, u32[]{:S(2)}) collective-permute-start(f32[4,258,1]{1,0,2:T(4,128)S(1)} %copy.597), channel_id=1, source_target_pairs={{0,1},{1,2},{2,3},{3,4},{4,5},{5,6},{6,7},{7,8},{8,9},{9,10},{10,1... | collective-permute-start | bytes 12392 | tf_op jit(solution)/shard_map/ppermute | solution.py:24
  487.6 8.6 %collective-permute-start.47 = (f32[4,258,1]{1,0,2:T(4,128)S(1)}, f32[4,258,1]{1,0,2:T(4,128)S(1)}, u32[]{:S(2)}, u32[]{:S(2)}) collective-permute-start(f32[4,258,1]{1,0,2:T(4,128)S(1)} %copy.599), channel_id=1, source_target_pairs={{1,0},{2,1},{3,2},{4,3},{5,4},{6,5},{7,6},{8,7},{9,8},{10,9},{11,1... | collective-permute-start | bytes 12392 | tf_op jit(solution)/shard_map/ppermute | solution.py:26
  521.6 84.8 %all-to-all-start.2 = ((f32[128,2,4096]{2,1,0:T(2,128)}), f32[128,2,4096]{2,1,0:T(2,128)}, u32[]{:S(2)}, u32[]{:S(2)}) async-start(f32[128,2,4096]{2,1,0:T(2,128)} %copy.613), calls=%async_computation.2 | async-start | bytes 8388608 | tf_op jit(solution)/shard_map/all_to_all | solution.py:88
  531.0 44.4 %collective-permute-start.48 = (f32[4,1,512]{2,0,1:T(4,128)S(1)}, f32[4,1,512]{2,0,1:T(4,128)S(1)}, u32[]{:S(2)}, u32[]{:S(2)}) collective-permute-start(f32[4,1,512]{2,0,1:T(4,128)S(1)} %copy.601), channel_id=1, source_target_pairs={{0,16},{16,32},{32,48},{48,64},{64,80},{80,96},{96,112},{1,17},{17... | collective-permute-start | bytes 24584 | tf_op jit(solution)/shard_map/ppermute | solution.py:24
  534.2 41.3 %collective-permute-start.49 = (f32[4,1,512]{2,0,1:T(4,128)S(1)}, f32[4,1,512]{2,0,1:T(4,128)S(1)}, u32[]{:S(2)}, u32[]{:S(2)}) collective-permute-start(f32[4,1,512]{2,0,1:T(4,128)S(1)} %copy.603), channel_id=1, source_target_pairs={{16,0},{32,16},{48,32},{64,48},{80,64},{96,80},{112,96},{17,1},{33... | collective-permute-start | bytes 24584 | tf_op jit(solution)/shard_map/ppermute | solution.py:26
  577.3 15.4 %collective-permute-start.50 = (f32[4,258,1]{1,0,2:T(4,128)S(1)}, f32[4,258,1]{1,0,2:T(4,128)S(1)}, u32[]{:S(2)}, u32[]{:S(2)}) collective-permute-start(f32[4,258,1]{1,0,2:T(4,128)S(1)} %copy.607), channel_id=1, source_target_pairs={{0,1},{1,2},{2,3},{3,4},{4,5},{5,6},{6,7},{7,8},{8,9},{9,10},{10,1... | collective-permute-start | bytes 12392 | tf_op jit(solution)/shard_map/ppermute | solution.py:24
  586.4 8.6 %collective-permute-start.51 = (f32[4,258,1]{1,0,2:T(4,128)S(1)}, f32[4,258,1]{1,0,2:T(4,128)S(1)}, u32[]{:S(2)}, u32[]{:S(2)}) collective-permute-start(f32[4,258,1]{1,0,2:T(4,128)S(1)} %copy.609), channel_id=1, source_target_pairs={{1,0},{2,1},{3,2},{4,3},{5,4},{6,5},{7,6},{8,7},{9,8},{10,9},{11,1... | collective-permute-start | bytes 12392 | tf_op jit(solution)/shard_map/ppermute | solution.py:26
  (38 other events, 235.1 us)
where the time goes:
time: 630 us; the launch traced here: 619 us
  starting transfers between devices  218 us (35%)
  other arithmetic  182 us (29%)
  waiting for transfers between devices  115 us (18%)
  local copies, waits for them, and re-layouts  87.3 us (14%)
  matrix products  13.9 us (2%)
    ppermute x26, starting transfers between devices, extended(): lax.ppermute(tail, axis, [(i, (i + 1) % count) for i in range(ends)])  134 us
    add x12, other arithmetic, advance(): return middle + RATE * inflow  115 us
    ppermute x26, waiting for transfers between devices, extended(): lax.ppermute(tail, axis, [(i, (i + 1) % count) for i in range(ends)])  67.3 us
    ppermute x26, starting transfers between devices, extended(): lax.ppermute(head, axis, [((i + 1) % count, i) for i in range(ends)])  54.5 us
    ppermute x26, waiting for transfers between devices, extended(): lax.ppermute(head, axis, [((i + 1) % count, i) for i in range(ends)])  48.2 us
    mul x12, other arithmetic, advance(): vertical = roots[1:] * roots[:-1] * (middle[1:] - middle[:-1])  46 us
    ppermute x26, local copies, waits for them, and re-layouts, extended(): lax.ppermute(head, axis, [((i + 1) % count, i) for i in range(ends)])  13.7 us
  transfers between devices with their start and end apart: 55, of which 24 were waited for; matrix products, arithmetic and copies ran while one was open for 16% of the time, Pallas kernels for 0%

commit v1 on v0

--- a/solution.py
+++ b/solution.py
@@ -125,15 +125,30 @@
         .reshape(height, breadth)
     )
     root_cond = conduct_root(classes, cond_table)
-    padded_roots = extended(root_cond, (("row", 1), ("col", 2)), 1)
-    heat_field = init_temp
+    sides = (("row", 1), ("col", 2))
+    reach = STEPS
+    padded_roots = extended(root_cond, sides, reach)
+    padded_source = extended(source[None], sides, reach)[0]
+    heat_field = extended(init_temp, sides, reach)
     for step_index in range(STEPS):
-        heat_field = advance(step_rim(heat_field), padded_roots, source)
-    adjoint = jnp.concatenate([(heat_field[0] - target)[None], jnp.zeros_like(heat_field[1:])], 0)
+        edge = step_index
+        inner = edge + 1
+        heat_field = advance(
+            heat_field,
+            padded_roots[:, edge : edge + heat_field.shape[1], edge : edge + heat_field.shape[2]],
+            padded_source[inner : inner + heat_field.shape[1] - 2, inner : inner + heat_field.shape[2] - 2],
+        )
+    start = extended((heat_field[0] - target)[None], sides, reach)
+    adjoint = jnp.concatenate([start, jnp.zeros((layers - 1,) + start.shape[1:], start.dtype)], 0)
     grad_sum = jnp.zeros_like(target)
     for step_index in range(STEPS):
-        grad_sum = grad_sum + adjoint[0]
-        adjoint = advance(step_rim(adjoint), padded_roots, None)
+        edge = reach - step_index
+        grad_sum = grad_sum + adjoint[0, edge : edge + height, edge : edge + breadth]
+        adjoint = advance(
+            adjoint,
+            padded_roots[:, step_index : step_index + adjoint.shape[1], step_index : step_index + adjoint.shape[2]],
+            None,
+        )
     grad_tiles = (
         grad_sum.reshape(tile_rows, TILE, tile_cols, TILE)
         .transpose(0, 2, 1, 3)

time: 630 us -> 501 us (0.80)
  the two profiles are of different devices: /device:TPU:15 before, /device:TPU:5 now
where the time goes in v1:
time: 501 us; the launch traced here: 491 us
  other arithmetic  164 us (33%)
  local copies, waits for them, and re-layouts  136 us (27%)
  waiting for transfers between devices  89.5 us (18%)
  starting transfers between devices  86 us (17%)
  matrix products  13.9 us (3%)
    add x12, other arithmetic, advance(): return middle + RATE * inflow  64.7 us
    sub x6, other arithmetic, advance(): inflow + jnp.concatenate([vertical, zero_layer], 0)  54 us
    all_to_all x1, waiting for transfers between devices, return_grads(): lax.all_to_all(backward.reshape(row_count * col_count, CAP, -1), ('row',...  40.5 us
    slice x5, local copies, waits for them, and re-layouts, advance(): middle = field[:, 1:-1, 1:-1]  40.1 us
    ppermute x8, starting transfers between devices, extended(): lax.ppermute(tail, axis, [(i, (i + 1) % count) for i in range(ends)])  34.2 us
    ppermute x8, waiting for transfers between devices, extended(): lax.ppermute(tail, axis, [(i, (i + 1) % count) for i in range(ends)])  29.6 us
    mul x12, other arithmetic, advance(): vertical = roots[1:] * roots[:-1] * (middle[1:] - middle[:-1])  27.7 us
    ppermute x8, waiting for transfers between devices, extended(): lax.ppermute(head, axis, [((i + 1) % count, i) for i in range(ends)])  19.4 us
  transfers between devices with their start and end apart: 19, of which 7 were waited for; matrix products, arithmetic and copies ran while one was open for 13% of the time, Pallas kernels for 0%

profile of v1, /device:TPU:5, one launch (start us, length us, event | category | flops | bytes accessed | tf_op | source)
XLA Modules:
  0.0 491.5 jit_solution(15978967250666682922)
XLA Ops:
  3.0 10.8 %all-to-all-start = ((s32[128,1,2]{2,1,0:T(1,128)}), s32[128,1,2]{2,1,0:T(1,128)S(1)}, u32[]{:S(2)}, u32[]{:S(2)}) async-start(s32[128,1,2]{2,1,0:T(1,128)} %bitcast.1), calls=%async_computation | async-start | bytes 131072 | tf_op jit(solution)/shard_map/all_to_all | solution.py:73
  17.9 5.3 %copy.348 = f32[128,2,4096]{2,1,0:T(2,128)} copy(f32[128,2,4096]{2,0,1:T(8,128)S(1)} %fusion.166) | data formatting | bytes 8388608 | tf_op jit(solution)/shard_map/dot_general | solution.py:116
  23.2 10.2 %all-to-all-start.1 = ((f32[128,2,4096]{2,1,0:T(2,128)}), f32[128,2,4096]{2,1,0:T(2,128)}, u32[]{:S(2)}, u32[]{:S(2)}) async-start(f32[128,2,4096]{2,1,0:T(2,128)} %copy.348), calls=%async_computation.1 | async-start | bytes 8388608 | tf_op jit(solution)/shard_map/all_to_all | solution.py:66
  33.7 3.7 add_sqrt_fusion
  42.8 4.6 collective-permute-start
  49.4 29.4 %collective-permute-done.4 = f32[4,6,512]{2,0,1:T(4,128)S(1)} collective-permute-done((f32[4,6,512]{2,0,1:T(4,128)S(1)}, f32[4,6,512]{2,0,1:T(4,128)S(1)}, u32[]{:S(2)}, u32[]{:S(2)}) %collective-permute-start.4) | collective-permute-done | bytes 49184 | tf_op jit(solution)/shard_map/ppermute | solution.py:24
  81.5 3.9 collective-permute-start.6
  92.3 3.6 collective-permute-start.2
  110.8 3.8 fusion.147
  114.5 6.1 %reshape.131 = f32[256,4096]{1,0:T(8,128)} reshape(f32[128,2,4096]{2,1,0:T(2,128)} %all-to-all-done.1) | data formatting | bytes 8388608 | tf_op jit(solution)/shard_map/reshape | solution.py:82
  120.6 5.6 %copy.349 = f32[4096,256]{1,0:T(8,128)} copy(f32[4096,256]{0,1:T(8,128)} %bitcast.72) | data formatting | bytes 8388608 | tf_op jit(solution)/shard_map/dot_general | solution.py:121
  126.3 6.2 %convolution_bitcast_fusion = f32[4,64,8,64]{3,2,1,0:T(8,128)} fusion(f32[64,64,256,1]{2,1,0,3:T(8,128)} %bitcast.71, s32[256]{0:T(256)S(1)} %eq.158, s32[4,8]{1,0:T(4,128)S(1)} %multiply_add_fusion), kind=kOutput, calls=%fused_computation.268 | convolution fusion | flops 402661376 | bytes 4719744 | tf_op jit(solution)/shard_map/dot_general | solution.py:121
  139.7 14.5 %fusion.19 = (f32[4,266,522]{2,1,0:T(8,128)S(1)}, f32[4,266,522]{2,1,0:T(8,128)}) fusion(f32[4,268,524]{2,1,0:T(8,128)} %copy-done.3, f32[3,266,522]{2,1,0:T(8,128)} %fusion.147, f32[4,268,524]{2,1,0:T(8,128)S(1)} %pad_maximum_fusion.1), kind=kLoop, calls=%fused_computation.28 | loop fusion | flops 9441936 | bytes 28325808 | tf_op jit(solution)/shard_map/sub | solution.py:50
  154.3 6.6 %collective-permute-start.10 = (f32[1,268,6]{2,1,0:T(8,128)S(1)}, f32[1,268,6]{2,1,0:T(8,128)S(1)}, u32[]{:S(2)}, u32[]{:S(2)}) collective-permute-start(f32[1,268,6]{2,1,0:T(8,128)S(1)} %get-tuple-element.72), channel_id=1, source_target_pairs={{0,1},{1,2},{2,3},{3,4},{4,5},{5,6},{6,7},{7,8},{8,9},{9,10},{10,1... | collective-permute-start | bytes 19304 | tf_op jit(solution)/shard_map/ppermute | solution.py:24
  166.9 4.7 collective-permute-done.11
  172.9 4.3 fusion.26
  177.2 3.2 fusion.176
  180.4 8.5 %fusion.177 = (f32[4,264,520]{2,0,1:T(4,128)S(1)}, f32[4,264,520]{2,0,1:T(4,128)}, f32[4,264,520]{2,0,1:T(4,128)}, f32[4,264,520]{2,0,1:T(4,128)}, f32[4,264,520]{2,0,1:T(4,128)}) fusion(f32[4,266,522]{2,0,1:T(4,128)S(1)} %fusion.26), kind=kLoop, calls=%fused_computation.330 | loop fusion | bytes 21964800 | tf_op jit(solution)/shard_map/slice | solution.py:41
  193.3 7.7 %fusion.108 = f32[4,264,520]{2,1,0:T(8,128)} fusion(f32[4,264,520]{2,0,1:T(4,128)} %get-tuple-element.28, f32[4,264,520]{2,0,1:T(4,128)} %get-tuple-element.29, f32[4,264,520]{2,0,1:T(4,128)} %get-tuple-element.30, f32[4,264,520]{2,0,1:T(4,128)} %get-tuple-element.31, f32[4,264,520]{2,0,1:T(4,128)S(1)} %get-tuple-element.27, ...), kind=kLoop, calls=%fused_computation.176 | loop fusion | flops 9335040 | bytes 25808640 | tf_op jit(solution)/shard_map/sub | solution.py:50
  201.0 5.1 %fusion.77 = f32[4,264,520]{2,0,1:T(4,128)S(1)} fusion(f32[1,264,520]{2,0,1:T(1,128)S(1)} %copy.461, f32[4,264,520]{2,1,0:T(8,128)} %fusion.108, f32[1,264,520]{2,0,1:T(1,128)S(1)} %slice.856, f32[4,266,522]{2,0,1:T(4,128)S(1)} %fusion.26), kind=kLoop, calls=%fused_computation.132 | loop fusion | flops 2745600 | bytes 7687680 | tf_op jit(solution)/shard_map/add | solution.py:57
  206.1 3.2 fusion.178
  209.3 8.7 %fusion.179 = (f32[4,262,518]{2,0,1:T(4,128)S(1)}, f32[4,262,518]{2,0,1:T(4,128)}, f32[4,262,518]{2,0,1:T(4,128)}, f32[4,262,518]{2,0,1:T(4,128)}, f32[4,262,518]{2,0,1:T(4,128)}) fusion(f32[4,264,520]{2,0,1:T(4,128)S(1)} %fusion.77), kind=kLoop, calls=%fused_computation.332 | loop fusion | bytes 21714560 | tf_op jit(solution)/shard_map/slice | solution.py:41
  223.4 7.2 %fusion.99 = f32[4,262,518]{2,1,0:T(8,128)S(1)} fusion(f32[4,262,518]{2,0,1:T(4,128)} %get-tuple-element.35, f32[4,262,518]{2,0,1:T(4,128)} %get-tuple-element.36, f32[4,262,518]{2,0,1:T(4,128)} %get-tuple-element.37, f32[4,262,518]{2,0,1:T(4,128)} %get-tuple-element.38, f32[4,262,518]{2,0,1:T(4,128)S(1)} %get-tuple-element.34, f32[3,262,518]{2,1,0:T(8,128)} %fusion.154, ...), kind=kLoop, calls=%fused_computation.163 | loop fusion | flops 9228688 | bytes 25514608 | tf_op jit(solution)/shard_map/sub | solution.py:50
  230.7 3.3 fusion.115
  237.1 8.3 %fusion.181 = (f32[4,260,516]{2,0,1:T(4,128)S(1)}, f32[4,260,516]{2,0,1:T(4,128)}, f32[4,260,516]{2,0,1:T(4,128)}, f32[4,260,516]{2,0,1:T(4,128)}, f32[4,260,516]{2,0,1:T(4,128)}) fusion(f32[4,262,518]{2,0,1:T(4,128)S(1)} %fusion.115), kind=kLoop, calls=%fused_computation.334 | loop fusion | bytes 21465600 | tf_op jit(solution)/shard_map/slice | solution.py:41
  250.8 7.4 %fusion.90 = f32[4,260,516]{2,1,0:T(8,128)S(1)} fusion(f32[4,260,516]{2,0,1:T(4,128)} %get-tuple-element.42, f32[4,260,516]{2,0,1:T(4,128)} %get-tuple-element.43, f32[4,260,516]{2,0,1:T(4,128)} %get-tuple-element.44, f32[4,260,516]{2,0,1:T(4,128)} %get-tuple-element.45, f32[4,260,516]{2,0,1:T(4,128)S(1)} %get-tuple-element.41, f32[3,260,516]{2,1,0:T(8,128)} %fusion.153, ...), kind=kLoop, calls=%fused_computation.150 | loop fusion | flops 9122880 | bytes 25222080 | tf_op jit(solution)/shard_map/sub | solution.py:50
  264.4 8.9 %fusion.183 = (f32[4,258,514]{2,0,1:T(4,128)}, f32[4,258,514]{2,0,1:T(4,128)}, f32[4,258,514]{2,0,1:T(4,128)}, f32[4,258,514]{2,0,1:T(4,128)}, f32[4,258,514]{2,0,1:T(4,128)}) fusion(f32[4,260,516]{2,0,1:T(4,128)S(1)} %fusion.117), kind=kLoop, calls=%fused_computation.336 | loop fusion | bytes 21217920 | tf_op jit(solution)/shard_map/slice | solution.py:41
  278.7 9.0 %fusion.81 = f32[4,258,514]{2,1,0:T(8,128)S(1)} fusion(f32[4,258,514]{2,0,1:T(4,128)} %get-tuple-element.49, f32[4,258,514]{2,0,1:T(4,128)} %get-tuple-element.50, f32[4,258,514]{2,0,1:T(4,128)} %get-tuple-element.51, f32[4,258,514]{2,0,1:T(4,128)} %get-tuple-element.52, f32[4,258,514]{2,0,1:T(4,128)} %get-tuple-element.48, f32[3,258,514]{2,1,0:T(8,128)} %fusion.152, ...), kind=kLoop, calls=%fused_computation.137 | loop fusion | flops 9017616 | bytes 24931056 | tf_op jit(solution)/shard_map/sub | solution.py:50
  293.2 5.6 %fusion.185 = (f32[4,256,512]{2,0,1:T(4,128)S(1)}, f32[4,256,512]{2,0,1:T(4,128)S(1)}, f32[4,256,512]{2,0,1:T(4,128)S(1)}, f32[4,256,512]{2,0,1:T(4,128)S(1)}, f32[4,256,512]{2,0,1:T(4,128)}) fusion(f32[4,258,514]{2,0,1:T(4,128)S(1)} %fusion.119), kind=kLoop, calls=%fused_computation.338 | loop fusion | bytes 20971520 | tf_op jit(solution)/shard_map/slice | solution.py:41
  302.2 8.1 %fusion.137 = f32[4,256,512]{2,1,0:T(8,128)} fusion(f32[4,256,512]{2,0,1:T(4,128)S(1)} %get-tuple-element.56, f32[4,256,512]{2,0,1:T(4,128)S(1)} %get-tuple-element.57, f32[4,256,512]{2,0,1:T(4,128)S(1)} %get-tuple-element.58, f32[4,256,512]{2,0,1:T(4,128)} %get-tuple-element.59, f32[4,256,512]{2,0,1:T(4,128)S(1)} %get-tuple-element.55, ...), kind=kLoop, calls=%fused_computation.224 | loop fusion | flops 9961472 | bytes 20545536 | tf_op jit(solution)/shard_map/sub | solution.py:50
  310.3 4.4 fusion.145
  317.3 4.0 collective-permute-start.12
  322.6 4.1 collective-permute-done.13
  327.5 5.7 %collective-permute-start.14 = (f32[1,268,6]{2,1,0:T(8,128)}, f32[1,268,6]{2,1,0:T(8,128)}, u32[]{:S(2)}, u32[]{:S(2)}) collective-permute-start(f32[1,268,6]{2,1,0:T(8,128)} %get-tuple-element.70), channel_id=1, source_target_pairs={{0,1},{1,2},{2,3},{3,4},{4,5},{5,6},{6,7},{7,8},{8,9},{9,10},{10,1... | collective-permute-start | bytes 19304 | tf_op jit(solution)/shard_map/ppermute | solution.py:24
  335.5 9.1 %collective-permute-done.15 = f32[1,268,6]{2,1,0:T(8,128)} collective-permute-done((f32[1,268,6]{2,1,0:T(8,128)}, f32[1,268,6]{2,1,0:T(8,128)}, u32[]{:S(2)}, u32[]{:S(2)}) %collective-permute-start.15) | collective-permute-done | bytes 6464 | tf_op jit(solution)/shard_map/ppermute | solution.py:26
  347.9 6.3 %fusion.5 = f32[4,266,522]{2,1,0:T(8,128)S(1)} fusion(f32[4,268,524]{2,1,0:T(8,128)S(1)} %select_maximum_fusion, f32[3,266,522]{2,1,0:T(8,128)S(1)} %fusion.146, f32[4,268,524]{2,1,0:T(8,128)S(1)} %pad_maximum_fusion.1), kind=kLoop, calls=%fused_computation.7 | loop fusion | flops 10552752 | bytes 26104176 | tf_op jit(solution)/shard_map/add | solution.py:57
  356.9 6.9 %fusion.70 = f32[4,264,520]{2,1,0:T(8,128)S(1)} fusion(f32[4,266,522]{2,1,0:T(8,128)S(1)} %fusion.5, f32[1,264,520]{2,1,0:T(8,128)S(1)} %slice.935, f32[3,264,520]{2,1,0:T(8,128)S(1)} %fusion.151, f32[4,268,524]{2,1,0:T(8,128)S(1)} %pad_maximum_fusion.1), kind=kLoop, calls=%fused_computation.105 | loop fusion | flops 11531520 | bytes 26357760 | tf_op jit(solution)/shard_map/add | solution.py:57
  366.4 7.2 %fusion.58 = f32[4,262,518]{2,1,0:T(8,128)S(1)} fusion(f32[4,264,520]{2,1,0:T(8,128)S(1)} %fusion.70, f32[1,262,518]{2,1,0:T(8,128)S(1)} %slice.943, f32[3,262,518]{2,1,0:T(8,128)S(1)} %fusion.150, f32[4,268,524]{2,1,0:T(8,128)S(1)} %pad_maximum_fusion.1), kind=kLoop, calls=%fused_computation.89 | loop fusion | flops 11400144 | bytes 26057472 | tf_op jit(solution)/shard_map/add | solution.py:57
  376.3 7.0 %fusion.46 = f32[4,260,516]{2,1,0:T(8,128)S(1)} fusion(f32[4,262,518]{2,1,0:T(8,128)S(1)} %fusion.58, f32[1,260,516]{2,1,0:T(8,128)S(1)} %slice.951, f32[3,260,516]{2,1,0:T(8,128)S(1)} %fusion.149, f32[4,268,524]{2,1,0:T(8,128)S(1)} %pad_maximum_fusion.1), kind=kLoop, calls=%fused_computation.73 | loop fusion | flops 11269440 | bytes 25758720 | tf_op jit(solution)/shard_map/add | solution.py:57
  383.4 3.7 fusion.148
  388.1 9.2 %fusion.34 = f32[4,258,514]{2,1,0:T(8,128)S(1)} fusion(f32[4,260,516]{2,1,0:T(8,128)S(1)} %fusion.46, f32[1,258,514]{2,1,0:T(8,128)} %slice.959, f32[3,258,514]{2,1,0:T(8,128)} %fusion.148, f32[4,268,524]{2,1,0:T(8,128)S(1)} %pad_maximum_fusion.1, f32[4,268,518]{2,1,0:T(8,128)} %copy-done.9, f32[4,268,518]{2,1,0:T(8,128)S(1)} %copy-done.7), kind=kLoop, calls=%fused_computation.57 | loop fusion | flops 11139408 | bytes 25461504 | tf_op jit(solution)/shard_map/add | solution.py:57
  403.5 5.3 %copy.418 = f32[128,2,4096]{2,1,0:T(2,128)} copy(f32[128,2,4096]{2,0,1:T(8,128)S(1)} %fusion.164) | data formatting | bytes 8388608 | tf_op jit(solution)/shard_map/dot_general | solution.py:157
  408.8 17.1 %all-to-all-start.2 = ((f32[128,2,4096]{2,1,0:T(2,128)}), f32[128,2,4096]{2,1,0:T(2,128)}, u32[]{:S(2)}, u32[]{:S(2)}) async-start(f32[128,2,4096]{2,1,0:T(2,128)} %copy.418), calls=%async_computation.2 | async-start | bytes 8388608 | tf_op jit(solution)/shard_map/all_to_all | solution.py:88
  426.0 3.7 copy.419
  433.7 4.9 fusion.126
  438.6 40.5 %all-to-all-done.2 = f32[128,2,4096]{2,1,0:T(2,128)} async-done(((f32[128,2,4096]{2,1,0:T(2,128)}), f32[128,2,4096]{2,1,0:T(2,128)}, u32[]{:S(2)}, u32[]{:S(2)}) %all-to-all-start.2) | async-done | bytes 4194336 | tf_op jit(solution)/shard_map/all_to_all | solution.py:88
  479.1 6.1 %reshape.134 = f32[256,4096]{1,0:T(8,128)} reshape(f32[128,2,4096]{2,1,0:T(2,128)} %all-to-all-done.2) | data formatting | bytes 8388608 | tf_op jit(solution)/shard_map/reshape | solution.py:95
  485.1 3.9 convolution_multiply_fusion
  (180 shorter events, 122.9 us)
Async XLA Ops:
  2.1 15.8 %copy-start.30 = (s32[64]{0:T(128)}, s32[64]{0:T(128)S(1)}, u32[]{:S(2)}) copy-start(s32[64]{0:T(128)S(1)} %get-tuple-element.78) | copy-start | bytes 772
  3.0 20.1 %all-to-all-start = ((s32[128,1,2]{2,1,0:T(1,128)}), s32[128,1,2]{2,1,0:T(1,128)S(1)}, u32[]{:S(2)}, u32[]{:S(2)}) async-start(s32[128,1,2]{2,1,0:T(1,128)} %bitcast.1), calls=%async_computation | async-start | bytes 131072 | tf_op jit(solution)/shard_map/all_to_all | solution.py:73
  23.1 10.2 %copy-start.26 = (f32[4,8]{1,0:T(4,128)S(1)}, f32[4,8]{1,0:T(4,128)}, u32[]{:S(2)}) copy-start(f32[4,8]{1,0:T(4,128)} %param.12) | copy-start | bytes 388
  23.2 91.4 %all-to-all-start.1 = ((f32[128,2,4096]{2,1,0:T(2,128)}), f32[128,2,4096]{2,1,0:T(2,128)}, u32[]{:S(2)}, u32[]{:S(2)}) async-start(f32[128,2,4096]{2,1,0:T(2,128)} %copy.348), calls=%async_computation.1 | async-start | bytes 8388608 | tf_op jit(solution)/shard_map/all_to_all | solution.py:66
  37.4 66.7 %copy-start = (f32[4,256,512]{2,1,0:T(8,128)}, f32[4,256,512]{2,1,0:T(8,128)S(1)}, u32[]{:S(2)}) copy-start(f32[4,256,512]{2,1,0:T(8,128)S(1)} %add_sqrt_fusion) | copy-start | bytes 6291460
  37.5 41.3 %collective-permute-start.4 = (f32[4,6,512]{2,0,1:T(4,128)S(1)}, f32[4,6,512]{2,0,1:T(4,128)S(1)}, u32[]{:S(2)}, u32[]{:S(2)}) collective-permute-start(f32[4,6,512]{2,0,1:T(4,128)S(1)} %copy.337), channel_id=1, source_target_pairs={{0,16},{16,32},{32,48},{48,64},{64,80},{80,96},{96,112},{1,17},{17... | collective-permute-start | bytes 147464 | tf_op jit(solution)/shard_map/ppermute | solution.py:24
  40.6 39.7 %collective-permute-start.5 = (f32[4,6,512]{2,0,1:T(4,128)S(1)}, f32[4,6,512]{2,0,1:T(4,128)S(1)}, u32[]{:S(2)}, u32[]{:S(2)}) collective-permute-start(f32[4,6,512]{2,0,1:T(4,128)S(1)} %copy.338), channel_id=1, source_target_pairs={{16,0},{32,16},{48,32},{64,48},{80,64},{96,80},{112,96},{17,1},{33... | collective-permute-start | bytes 147464 | tf_op jit(solution)/shard_map/ppermute | solution.py:26
  42.8 45.4 %collective-permute-start = (f32[4,6,512]{2,0,1:T(4,128)S(1)}, f32[4,6,512]{2,0,1:T(4,128)}, u32[]{:S(2)}, u32[]{:S(2)}) collective-permute-start(f32[4,6,512]{2,0,1:T(4,128)S(1)} %copy.422), channel_id=1, source_target_pairs={{0,16},{16,32},{32,48},{48,64},{64,80},{80,96},{96,112},{1,17},{17... | collective-permute-start | bytes 147464 | tf_op jit(solution)/shard_map/ppermute | solution.py:24
  48.1 41.0 %collective-permute-start.1 = (f32[4,6,512]{2,0,1:T(4,128)}, f32[4,6,512]{2,0,1:T(4,128)}, u32[]{:S(2)}, u32[]{:S(2)}) collective-permute-start(f32[4,6,512]{2,0,1:T(4,128)} %copy.423), channel_id=1, source_target_pairs={{16,0},{32,16},{48,32},{64,48},{80,64},{96,80},{112,96},{17,1},{33... | collective-permute-start | bytes 147464 | tf_op jit(solution)/shard_map/ppermute | solution.py:26
  78.8 84.3 %copy-start.17 = (f32[4,6,512]{2,1,0:T(8,128)}, f32[4,6,512]{2,1,0:T(8,128)S(1)}, u32[]{:S(2)}) copy-start(f32[4,6,512]{2,1,0:T(8,128)S(1)} %copy.339) | copy-start | bytes 147460
  80.4 82.7 %copy-start.19 = (f32[4,6,512]{2,1,0:T(8,128)}, f32[4,6,512]{2,1,0:T(8,128)S(1)}, u32[]{:S(2)}) copy-start(f32[4,6,512]{2,1,0:T(8,128)S(1)} %copy.340) | copy-start | bytes 147460
  81.5 18.6 %collective-permute-start.6 = (f32[4,268,6]{1,0,2:T(4,128)}, f32[4,268,6]{1,0,2:T(4,128)}, u32[]{:S(2)}, u32[]{:S(2)}) collective-permute-start(f32[4,268,6]{1,0,2:T(4,128)} %copy.341), channel_id=1, source_target_pairs={{0,1},{1,2},{2,3},{3,4},{4,5},{5,6},{6,7},{7,8},{8,9},{9,10},{10,1... | collective-permute-start | bytes 77192 | tf_op jit(solution)/shard_map/ppermute | solution.py:24
  86.3 14.8 %collective-permute-start.7 = (f32[4,268,6]{1,0,2:T(4,128)}, f32[4,268,6]{1,0,2:T(4,128)}, u32[]{:S(2)}, u32[]{:S(2)}) collective-permute-start(f32[4,268,6]{1,0,2:T(4,128)} %copy.342), channel_id=1, source_target_pairs={{1,0},{2,1},{3,2},{4,3},{5,4},{6,5},{7,6},{8,7},{9,8},{10,9},{11,1... | collective-permute-start | bytes 77192 | tf_op jit(solution)/shard_map/ppermute | solution.py:26
  89.9 13.1 %copy-start.24 = (f32[4,6,512]{2,1,0:T(8,128)}, f32[4,6,512]{2,1,0:T(8,128)S(1)}, u32[]{:S(2)}) copy-start(f32[4,6,512]{2,1,0:T(8,128)S(1)} %copy.332) | copy-start | bytes 147460
  92.3 10.7 %collective-permute-start.2 = (f32[4,268,6]{1,0,2:T(4,128)}, f32[4,268,6]{1,0,2:T(4,128)S(1)}, u32[]{:S(2)}, u32[]{:S(2)}) collective-permute-start(f32[4,268,6]{1,0,2:T(4,128)} %copy.333), channel_id=1, source_target_pairs={{0,1},{1,2},{2,3},{3,4},{4,5},{5,6},{6,7},{7,8},{8,9},{9,10},{10,1... | collective-permute-start | bytes 77192 | tf_op jit(solution)/shard_map/ppermute | solution.py:24
  96.2 7.8 %collective-permute-start.3 = (f32[4,268,6]{1,0,2:T(4,128)S(1)}, f32[4,268,6]{1,0,2:T(4,128)S(1)}, u32[]{:S(2)}, u32[]{:S(2)}) collective-permute-start(f32[4,268,6]{1,0,2:T(4,128)S(1)} %copy.334), channel_id=1, source_target_pairs={{1,0},{2,1},{3,2},{4,3},{5,4},{6,5},{7,6},{8,7},{9,8},{10,9},{11,1... | collective-permute-start | bytes 77192 | tf_op jit(solution)/shard_map/ppermute | solution.py:26
  100.1 26.1 %copy-start.28 = (s32[256]{0:T(256)}, s32[256]{0:T(256)S(1)}, u32[]{:S(2)}) copy-start(s32[256]{0:T(256)S(1)} %eq.158) | copy-start | bytes 3076
  105.1 3.0 copy-start.13
  105.1 3.0 copy-start.21
  105.1 3.0 copy-start.22
  105.1 3.0 copy-start.25
  109.2 1.5 copy-start.3
  135.5 18.7 %collective-permute-start.8 = (f32[1,6,512]{2,1,0:T(8,128)S(1)}, f32[1,6,512]{2,1,0:T(8,128)S(1)}, u32[]{:S(2)}, u32[]{:S(2)}) collective-permute-start(f32[1,6,512]{2,1,0:T(8,128)S(1)} %get-tuple-element.76), channel_id=1, source_target_pairs={{0,16},{16,32},{32,48},{48,64},{64,80},{80,96},{96,112},{1,17},{17... | collective-permute-start | bytes 36872 | tf_op jit(solution)/shard_map/ppermute | solution.py:24
  138.1 16.1 %copy-start.15 = (f32[1,256,512]{2,1,0:T(8,128)S(1)}, f32[1,256,512]{2,1,0:T(8,128)}, u32[]{:S(2)}) copy-start(f32[1,256,512]{2,1,0:T(8,128)} %broadcast_in_dim_reshape.4) | copy-start | bytes 1572868
  138.1 25.0 %copy-start.1 = (f32[4,256,512]{2,1,0:T(8,128)S(1)}, f32[4,256,512]{2,1,0:T(8,128)}, u32[]{:S(2)}) copy-start(f32[4,256,512]{2,1,0:T(8,128)} %copy-done) | copy-start | bytes 6291460
  138.1 25.0 %copy-start.14 = (f32[4,268,6]{2,1,0:T(8,128)S(1)}, f32[4,268,6]{2,1,0:T(8,128)}, u32[]{:S(2)}) copy-start(f32[4,268,6]{2,1,0:T(8,128)} %copy.344) | copy-start | bytes 77188
  138.1 16.1 %collective-permute-start.9 = (f32[1,6,512]{2,1,0:T(8,128)S(1)}, f32[1,6,512]{2,1,0:T(8,128)S(1)}, u32[]{:S(2)}, u32[]{:S(2)}) collective-permute-start(f32[1,6,512]{2,1,0:T(8,128)S(1)} %get-tuple-element.77), channel_id=1, source_target_pairs={{16,0},{32,16},{48,32},{64,48},{80,64},{96,80},{112,96},{17,1},{33... | collective-permute-start | bytes 36872 | tf_op jit(solution)/shard_map/ppermute | solution.py:26
  154.3 12.6 %collective-permute-start.10 = (f32[1,268,6]{2,1,0:T(8,128)S(1)}, f32[1,268,6]{2,1,0:T(8,128)S(1)}, u32[]{:S(2)}, u32[]{:S(2)}) collective-permute-start(f32[1,268,6]{2,1,0:T(8,128)S(1)} %get-tuple-element.72), channel_id=1, source_target_pairs={{0,1},{1,2},{2,3},{3,4},{4,5},{5,6},{6,7},{7,8},{8,9},{9,10},{10,1... | collective-permute-start | bytes 19304 | tf_op jit(solution)/shard_map/ppermute | solution.py:24
  160.9 10.6 %collective-permute-start.11 = (f32[1,268,6]{2,1,0:T(8,128)S(1)}, f32[1,268,6]{2,1,0:T(8,128)S(1)}, u32[]{:S(2)}, u32[]{:S(2)}) collective-permute-start(f32[1,268,6]{2,1,0:T(8,128)S(1)} %get-tuple-element.73), channel_id=1, source_target_pairs={{1,0},{2,1},{3,2},{4,3},{5,4},{6,5},{7,6},{8,7},{9,8},{10,9},{11,1... | collective-permute-start | bytes 19304 | tf_op jit(solution)/shard_map/ppermute | solution.py:26
  164.3 137.9 %copy-start.6 = (f32[4,268,518]{2,1,0:T(8,128)}, f32[4,268,518]{2,1,0:T(8,128)S(1)}, u32[]{:S(2)}) copy-start(f32[4,268,518]{2,1,0:T(8,128)S(1)} %get-tuple-element.60) | copy-start | bytes 6663556
  164.3 137.9 %copy-start.9 = (f32[4,268,518]{2,1,0:T(8,128)}, f32[4,268,518]{2,1,0:T(8,128)S(1)}, u32[]{:S(2)}) copy-start(f32[4,268,518]{2,1,0:T(8,128)S(1)} %get-tuple-element.61) | copy-start | bytes 6663556
  166.2 6.7 %copy-start.11 = (f32[4,266,522]{2,1,0:T(8,128)S(1)}, f32[4,266,522]{2,1,0:T(8,128)}, u32[]{:S(2)}) copy-start(f32[4,266,522]{2,1,0:T(8,128)} %get-tuple-element.24) | copy-start | bytes 6664900
  310.3 6.9 %copy-start.23 = (f32[256,512]{1,0:T(8,128)S(1)}, f32[256,512]{1,0:T(8,128)}, u32[]{:S(2)}) copy-start(f32[256,512]{1,0:T(8,128)} %param.13) | copy-start | bytes 1572868
  314.7 1.3 copy-start.12
  316.0 19.1 %copy-start.29 = (s32[256]{0:T(256)S(1)}, s32[256]{0:T(256)}, u32[]{:S(2)}) copy-start(s32[256]{0:T(256)} %copy-done.28) | copy-start | bytes 3076
  317.3 5.3 %collective-permute-start.12 = (f32[1,6,512]{2,1,0:T(8,128)S(1)}, f32[1,6,512]{2,1,0:T(8,128)S(1)}, u32[]{:S(2)}, u32[]{:S(2)}) collective-permute-start(f32[1,6,512]{2,1,0:T(8,128)S(1)} %get-tuple-element.74), channel_id=1, source_target_pairs={{0,16},{16,32},{32,48},{48,64},{64,80},{80,96},{96,112},{1,17},{17... | collective-permute-start | bytes 36872 | tf_op jit(solution)/shard_map/ppermute | solution.py:24
  321.3 5.4 %collective-permute-start.13 = (f32[1,6,512]{2,1,0:T(8,128)S(1)}, f32[1,6,512]{2,1,0:T(8,128)S(1)}, u32[]{:S(2)}, u32[]{:S(2)}) collective-permute-start(f32[1,6,512]{2,1,0:T(8,128)S(1)} %get-tuple-element.75), channel_id=1, source_target_pairs={{16,0},{32,16},{48,32},{64,48},{80,64},{96,80},{112,96},{17,1},{33... | collective-permute-start | bytes 36872 | tf_op jit(solution)/shard_map/ppermute | solution.py:26
  326.7 8.4 %copy-start.27 = (f32[1,6,512]{2,1,0:T(8,128)}, f32[1,6,512]{2,1,0:T(8,128)S(1)}, u32[]{:S(2)}) copy-start(f32[1,6,512]{2,1,0:T(8,128)S(1)} %collective-permute-done.13) | copy-start | bytes 36868
  327.5 8.0 %collective-permute-start.14 = (f32[1,268,6]{2,1,0:T(8,128)}, f32[1,268,6]{2,1,0:T(8,128)}, u32[]{:S(2)}, u32[]{:S(2)}) collective-permute-start(f32[1,268,6]{2,1,0:T(8,128)} %get-tuple-element.70), channel_id=1, source_target_pairs={{0,1},{1,2},{2,3},{3,4},{4,5},{5,6},{6,7},{7,8},{8,9},{9,10},{10,1... | collective-permute-start | bytes 19304 | tf_op jit(solution)/shard_map/ppermute | solution.py:24
  333.2 11.4 %collective-permute-start.15 = (f32[1,268,6]{2,1,0:T(8,128)}, f32[1,268,6]{2,1,0:T(8,128)}, u32[]{:S(2)}, u32[]{:S(2)}) collective-permute-start(f32[1,268,6]{2,1,0:T(8,128)} %get-tuple-element.71), channel_id=1, source_target_pairs={{1,0},{2,1},{3,2},{4,3},{5,4},{6,5},{7,6},{8,7},{9,8},{10,9},{11,1... | collective-permute-start | bytes 19304 | tf_op jit(solution)/shard_map/ppermute | solution.py:26
  383.3 4.8 copy-start.7
  397.3 1.5 copy-start.4
  408.8 70.2 %all-to-all-start.2 = ((f32[128,2,4096]{2,1,0:T(2,128)}), f32[128,2,4096]{2,1,0:T(2,128)}, u32[]{:S(2)}, u32[]{:S(2)}) async-start(f32[128,2,4096]{2,1,0:T(2,128)} %copy.418), calls=%async_computation.2 | async-start | bytes 8388608 | tf_op jit(solution)/shard_map/all_to_all | solution.py:88
  426.0 5.1 %copy-start.2 = (f32[4,256,512]{2,1,0:T(8,128)S(1)}, f32[4,256,512]{2,1,0:T(8,128)}, u32[]{:S(2)}) copy-start(f32[4,256,512]{2,1,0:T(8,128)} %copy-done) | copy-start | bytes 6291460
  426.0 5.1 %copy-start.5 = (f32[4,258,514]{2,1,0:T(8,128)S(1)}, f32[4,258,514]{2,1,0:T(8,128)}, u32[]{:S(2)}) copy-start(f32[4,258,514]{2,1,0:T(8,128)} %copy-done.4) | copy-start | bytes 6365380
  431.1 1.8 copy-start.8
  431.1 2.6 copy-start.10
  438.6 46.5 %copy-start.31 = (s32[64]{0:T(128)S(1)}, s32[64]{0:T(128)}, u32[]{:S(2)}) copy-start(s32[64]{0:T(128)} %copy-done.30) | copy-start | bytes 772
  (3 other events, 3.3 us)

commit v2 on v0

--- a/solution.py
+++ b/solution.py
@@ -1,6 +1,8 @@
 import jax
 import jax.numpy as jnp
 from jax import lax
+from jax.experimental import pallas as pl
+from jax.experimental.pallas import tpu as pltpu
 from jax.sharding import PartitionSpec as P
 
 TILE = 64
@@ -57,8 +59,175 @@
     return middle + RATE * inflow
 
 
-def step_rim(field):
-    return extended(field, (("row", 1), ("col", 2)), 1)
+HALO = 8
+SLACK = 8
+CHUNK = 16
+LANE = 128
+
+
+def framed(cells):
+    depth, height, breadth = cells.shape
+    cols = lax.axis_size("col")
+    rows = lax.axis_size("row")
+    left = lax.ppermute(cells[:, :, breadth - HALO :], "col", [(i, i + 1) for i in range(cols - 1)])
+    right = lax.ppermute(cells[:, :, :HALO], "col", [(i + 1, i) for i in range(cols - 1)])
+    gap = jnp.zeros((depth, height, LANE - 2 * HALO), cells.dtype)
+    band = jnp.concatenate([cells, right, gap, left], axis=2)
+    top = lax.ppermute(band[:, height - HALO :], "row", [(i, i + 1) for i in range(rows - 1)])
+    bottom = lax.ppermute(band[:, :HALO], "row", [(i + 1, i) for i in range(rows - 1)])
+    pad = jnp.zeros((depth, SLACK, band.shape[2]), cells.dtype)
+    return jnp.concatenate([pad, top, band, bottom, pad], axis=1)
+
+
+def chunk_loop(count, body):
+    lax.fori_loop(0, count, lambda c, carry: (body(c), carry)[1], 0)
+
+
+def conductances(r_ref, cu, cd, cl, cr, cv):
+    layers, frame_rows, frame_cols = r_ref.shape
+    count = (frame_rows - 2 * SLACK) // CHUNK
+
+    def body(c):
+        lead = pl.multiple_of(c * CHUNK, 8)
+        rows = pl.ds(pl.multiple_of(lead + SLACK, 8), CHUNK)
+        for l in range(layers):
+            win = r_ref[l, pl.ds(lead, CHUNK + 2 * SLACK), :]
+            r = win[SLACK : SLACK + CHUNK]
+            cu[l, rows, :] = r * pltpu.roll(win, 1, 0)[SLACK : SLACK + CHUNK]
+            cd[l, rows, :] = r * pltpu.roll(win, CHUNK + 2 * SLACK - 1, 0)[SLACK : SLACK + CHUNK]
+            cl[l, rows, :] = r * pltpu.roll(r, 1, 1)
+            cr[l, rows, :] = r * pltpu.roll(r, frame_cols - 1, 1)
+            if l + 1 < layers:
+                cv[l, rows, :] = r_ref[l + 1, rows, :] * r
+
+    chunk_loop(count, body)
+
+
+def explicit_step(src, dst, cu, cd, cl, cr, cv, s_ref):
+    layers, frame_rows, frame_cols = dst.shape
+    count = (frame_rows - 2 * SLACK) // CHUNK
+
+    def body(c):
+        lead = pl.multiple_of(c * CHUNK, 8)
+        rows = pl.ds(pl.multiple_of(lead + SLACK, 8), CHUNK)
+        for l in range(layers):
+            win = src[l, pl.ds(lead, CHUNK + 2 * SLACK), :]
+            f = win[SLACK : SLACK + CHUNK]
+            up = pltpu.roll(win, 1, 0)[SLACK : SLACK + CHUNK]
+            down = pltpu.roll(win, CHUNK + 2 * SLACK - 1, 0)[SLACK : SLACK + CHUNK]
+            left = pltpu.roll(f, 1, 1)
+            right = pltpu.roll(f, frame_cols - 1, 1)
+            inflow = cu[l, rows, :] * (up - f)
+            inflow = inflow + cd[l, rows, :] * (down - f)
+            inflow = inflow + cl[l, rows, :] * (left - f)
+            inflow = inflow + cr[l, rows, :] * (right - f)
+            if l + 1 < layers:
+                inflow = inflow + cv[l, rows, :] * (src[l + 1, rows, :] - f)
+            if l > 0:
+                inflow = inflow - cv[l - 1, rows, :] * (f - src[l - 1, rows, :])
+            if l == layers - 1:
+                inflow = inflow - AMBIENT_LOSS * f
+            if l == 0 and s_ref is not None:
+                inflow = inflow + s_ref[rows, :]
+            dst[l, rows, :] = f + RATE * inflow
+
+    chunk_loop(count, body)
+
+
+def clear_slack(buf):
+    layers, frame_rows, frame_cols = buf.shape
+    zero = jnp.zeros((layers, SLACK, frame_cols), buf.dtype)
+    buf[:, 0:SLACK, :] = zero
+    buf[:, frame_rows - SLACK : frame_rows, :] = zero
+
+
+def copy_center(src_view, dst_ref, height, breadth):
+    def body(c):
+        rows = pl.ds(pl.multiple_of(c * CHUNK, 8), CHUNK)
+        from_rows = pl.ds(pl.multiple_of(c * CHUNK + SLACK + HALO, 8), CHUNK)
+        dst_ref(rows, src_view(from_rows, breadth))
+
+    chunk_loop(height // CHUNK, body)
+
+
+def forward_kernel(f_ref, r_ref, s_ref, out_ref, cu, cd, cl, cr, cv, a, b):
+    layers, height, breadth = out_ref.shape
+    clear_slack(a)
+    clear_slack(b)
+    conductances(r_ref, cu, cd, cl, cr, cv)
+    src = f_ref
+    for index in range(STEPS):
+        dst = a if index % 2 == 0 else b
+        explicit_step(src, dst, cu, cd, cl, cr, cv, s_ref)
+        src = dst
+
+    def put(rows, value):
+        out_ref[:, rows, :] = value
+
+    copy_center(lambda rows, width: src[:, rows, 0:width], put, height, breadth)
+
+
+def adjoint_kernel(a0_ref, r_ref, grad_ref, gsum_ref, cu, cd, cl, cr, cv, a, b):
+    layers, height, breadth = grad_ref.shape
+    a[...] = jnp.zeros(a.shape, a.dtype)
+    clear_slack(b)
+    a[0] = a0_ref[...]
+    conductances(r_ref, cu, cd, cl, cr, cv)
+    src = a
+    for index in range(STEPS):
+        view = src
+
+        def put_sum(rows, value, first=(index == 0)):
+            if first:
+                gsum_ref[rows, :] = value
+            else:
+                gsum_ref[rows, :] = gsum_ref[rows, :] + value
+
+        copy_center(lambda rows, width, v=view: v[0, rows, 0:width], put_sum, height, breadth)
+        dst = b if index % 2 == 0 else a
+        explicit_step(src, dst, cu, cd, cl, cr, cv, None)
+        src = dst
+
+    def put(rows, value):
+        grad_ref[:, rows, :] = value
+
+    copy_center(lambda rows, width: src[:, rows, 0:width], put, height, breadth)
+
+
+def stencil_scratch(layers, frame_rows, frame_cols):
+    whole = pltpu.VMEM((layers, frame_rows, frame_cols), jnp.float32)
+    return [whole] * 4 + [pltpu.VMEM((layers - 1, frame_rows, frame_cols), jnp.float32), whole, whole]
+
+
+def vmem_specs(count):
+    return [pl.BlockSpec(memory_space=pltpu.VMEM) for _ in range(count)]
+
+
+def run_forward(f_frame, r_frame, s_frame, height, breadth):
+    layers, frame_rows, frame_cols = f_frame.shape
+    return pl.pallas_call(
+        forward_kernel,
+        out_shape=jax.ShapeDtypeStruct((layers, height, breadth), jnp.float32),
+        in_specs=vmem_specs(3),
+        out_specs=vmem_specs(1)[0],
+        scratch_shapes=stencil_scratch(layers, frame_rows, frame_cols),
+        compiler_params=pltpu.CompilerParams(vmem_limit_bytes=56 * 1024 * 1024),
+    )(f_frame, r_frame, s_frame)
+
+
+def run_adjoint(a0_frame, r_frame, height, breadth):
+    layers, frame_rows, frame_cols = r_frame.shape
+    return pl.pallas_call(
+        adjoint_kernel,
+        out_shape=(
+            jax.ShapeDtypeStruct((layers, height, breadth), jnp.float32),
+            jax.ShapeDtypeStruct((height, breadth), jnp.float32),
+        ),
+        in_specs=vmem_specs(2),
+        out_specs=tuple(vmem_specs(2)),
+        scratch_shapes=stencil_scratch(layers, frame_rows, frame_cols),
+        compiler_params=pltpu.CompilerParams(vmem_limit_bytes=56 * 1024 * 1024),
+    )(a0_frame, r_frame)
 
 
 def send_dies(outbound, tile_ids, row_count, col_count):
@@ -125,15 +294,12 @@
         .reshape(height, breadth)
     )
     root_cond = conduct_root(classes, cond_table)
-    padded_roots = extended(root_cond, (("row", 1), ("col", 2)), 1)
-    heat_field = init_temp
-    for step_index in range(STEPS):
-        heat_field = advance(step_rim(heat_field), padded_roots, source)
-    adjoint = jnp.concatenate([(heat_field[0] - target)[None], jnp.zeros_like(heat_field[1:])], 0)
-    grad_sum = jnp.zeros_like(target)
-    for step_index in range(STEPS):
-        grad_sum = grad_sum + adjoint[0]
-        adjoint = advance(step_rim(adjoint), padded_roots, None)
+    r_frame = framed(root_cond)
+    s_frame = framed(source[None])[0]
+    f_frame = framed(init_temp)
+    heat_field = run_forward(f_frame, r_frame, s_frame, height, breadth)
+    a0_frame = framed((heat_field[0] - target)[None])[0]
+    adjoint, grad_sum = run_adjoint(a0_frame, r_frame, height, breadth)
     grad_tiles = (
         grad_sum.reshape(tile_rows, TILE, tile_cols, TILE)
         .transpose(0, 2, 1, 3)

time: 630 us -> 322 us (0.51); the launches traced: 619 us -> 317 us
  other arithmetic: 182 us -> 10.8 us
  starting transfers between devices: 218 us -> 84.5 us
  waiting for transfers between devices: 115 us -> 44.2 us
  blocking collectives: 0 us -> 63.1 us
  Pallas kernels: 0 us -> 53.6 us
  local copies, waits for them, and re-layouts: 87.3 us -> 47 us
    ppermute x52 -> x16, starting transfers between devices: 188 us -> 63.6 us  [the longest x4 30.8 us: framed(): lax.ppermute(cells[:, :, breadth - HALO:], 'col', [(i, i + 1) for i in ra...]
    add x13 -> x0, other arithmetic: 117 us -> none  [the longest x12 115 us: advance(): return middle + RATE * inflow]
    ppermute x52 -> x16, waiting for transfers between devices: 115 us -> 44.2 us  [the longest x4 34.4 us: framed(): lax.ppermute(cells[:, :, :HALO], 'col', [(i + 1, i) for i in range(cols -...]
    all_to_all x0 -> x1, blocking collectives: none -> 63.1 us  [return_grads(): lax.all_to_all(backward.reshape(row_count * col_count, CAP, -1), ('row',...]
    pallas_call x0 -> x2, Pallas kernels: none -> 53.6 us  [the longest x1 26.8 us: run_adjoint(): pl.pallas_call(adjoint_kernel, out_shape=(jax.ShapeDtypeStruct((layers, h...]
    mul x12 -> x0, other arithmetic: 46 us -> none  [advance(): vertical = roots[1:] * roots[:-1] * (middle[1:] - middle[:-1])]
    ppermute x52 -> x0, local copies, waits for them, and re-layouts: 22.5 us -> none  [the longest x26 13.7 us: extended(): lax.ppermute(head, axis, [((i + 1) % count, i) for i in range(ends)])]
    slice x84 -> x8, local copies, waits for them, and re-layouts: 20.4 us -> 2.33 us  [the longest x4 2.29 us: framed(): cells[:, :, :HALO]]
  transfers between devices with their start and end apart: 55 -> 18, of which waited for: 24 -> 7; matrix products, arithmetic and copies ran while one was open for 16% -> 15% of each run, Pallas kernels for 0% -> 0%
where the time goes in v2:
time: 322 us; the launch traced here: 317 us
  starting transfers between devices  84.5 us (26%)
  blocking collectives  63.1 us (20%)
  Pallas kernels  53.6 us (17%)
  local copies, waits for them, and re-layouts  47 us (15%)
  waiting for transfers between devices  44.2 us (14%)
  matrix products  12.9 us (4%)
  other arithmetic  10.8 us (3%)
    all_to_all x1, blocking collectives, return_grads(): lax.all_to_all(backward.reshape(row_count * col_count, CAP, -1), ('row',...  63.1 us
    ppermute x4, waiting for transfers between devices, framed(): lax.ppermute(cells[:, :, :HALO], 'col', [(i + 1, i) for i in range(cols -...  34.4 us
    ppermute x4, starting transfers between devices, framed(): lax.ppermute(cells[:, :, breadth - HALO:], 'col', [(i, i + 1) for i in ra...  30.8 us
    pallas_call x1, Pallas kernels, run_adjoint(): pl.pallas_call(adjoint_kernel, out_shape=(jax.ShapeDtypeStruct((layers, h...  26.8 us
    pallas_call x1, Pallas kernels, run_forward(): pl.pallas_call(forward_kernel, out_shape=jax.ShapeDtypeStruct((layers, he...  26.8 us
    ppermute x4, starting transfers between devices, framed(): lax.ppermute(band[:, height - HALO:], 'row', [(i, i + 1) for i in range(r...  16.9 us
    all_to_all x1, starting transfers between devices, send_dies(): lax.all_to_all(tile_ids.reshape(row_count * col_count, CAP), ('row', 'col...  10.6 us
    all_to_all x1, starting transfers between devices, send_dies(): lax.all_to_all(outbound.reshape(row_count * col_count, CAP, -1), ('row',...  10.2 us
  transfers between devices with their start and end apart: 18, of which 7 were waited for; matrix products, arithmetic and copies ran while one was open for 15% of the time, Pallas kernels for 0%

profile of v2, /device:TPU:15, one launch (start us, length us, event | category | flops | bytes accessed | tf_op | source)
XLA Modules:
  0.0 317.1 jit_solution(5007300564717280462)
XLA Ops:
  3.0 10.6 %all-to-all-start = ((s32[128,1,2]{2,1,0:T(1,128)}), s32[128,1,2]{2,1,0:T(1,128)S(1)}, u32[]{:S(2)}, u32[]{:S(2)}) async-start(s32[128,1,2]{2,1,0:T(1,128)} %bitcast.1), calls=%async_computation | async-start | bytes 131072 | tf_op jit(solution)/shard_map/all_to_all | solution.py:242
  13.7 2.1 reshape.135
  15.8 1.9 fusion.4
  17.7 5.2 %copy.23 = f32[128,2,4096]{2,1,0:T(2,128)} copy(f32[128,2,4096]{2,0,1:T(8,128)S(1)} %fusion.4) | data formatting | bytes 8388608 | tf_op jit(solution)/shard_map/dot_general | solution.py:285
  23.0 10.2 %all-to-all-start.1 = ((f32[128,2,4096]{2,1,0:T(2,128)}), f32[128,2,4096]{2,1,0:T(2,128)}, u32[]{:S(2)}, u32[]{:S(2)}) async-start(f32[128,2,4096]{2,1,0:T(2,128)} %copy.23), calls=%async_computation.1 | async-start | bytes 8388608 | tf_op jit(solution)/shard_map/all_to_all | solution.py:235
  33.5 3.8 %add_sqrt_fusion = f32[4,256,512]{2,1,0:T(8,128)S(1)} fusion(s32[4,256,512]{2,1,0:T(8,128)} %param.11, f32[4]{0:T(128)S(1)} %get-tuple-element.13, f32[4]{0:T(128)S(1)} %get-tuple-element.14, f32[4]{0:T(128)S(1)} %get-tuple-element.8, f32[4]{0:T(128)S(1)} %get-tuple-element.9, f32[4]{0:T(128)S(1)} %get-tuple-element.10, f32[4]{0:T(128)S(1)} %get-tuple-element.11, ...), kind=kLoop, calls=%fused_computation.3 | loop fusion | flops 12058624 | bytes 4194432 | tf_op jit(solution)/shard_map/sqrt | solution.py:39
  37.3 1.0 fusion.16
  38.3 2.3 collective-permute-start.4
  40.6 6.9 %collective-permute-start.5 = (f32[4,256,8]{2,1,0:T(8,128)S(1)}, f32[4,256,8]{2,1,0:T(8,128)}, u32[]{:S(2)}, u32[]{:S(2)}) collective-permute-start(f32[4,256,8]{2,1,0:T(8,128)S(1)} %get-tuple-element.20), channel_id=1, source_target_pairs={{0,1},{1,2},{2,3},{3,4},{4,5},{5,6},{6,7},{7,8},{8,9},{9,10},{10,1... | collective-permute-start | bytes 98312 | tf_op jit(solution)/shard_map/ppermute | solution.py:72
  47.5 1.1 fusion.17
  48.6 1.9 collective-permute-start
  50.5 7.3 %collective-permute-start.1 = (f32[4,256,8]{2,1,0:T(8,128)}, f32[4,256,8]{2,1,0:T(8,128)}, u32[]{:S(2)}, u32[]{:S(2)}) collective-permute-start(f32[4,256,8]{2,1,0:T(8,128)} %get-tuple-element.22), channel_id=1, source_target_pairs={{0,1},{1,2},{2,3},{3,4},{4,5},{5,6},{6,7},{7,8},{8,9},{9,10},{10,1... | collective-permute-start | bytes 98312 | tf_op jit(solution)/shard_map/ppermute | solution.py:72
  60.5 28.0 %collective-permute-done.4 = f32[4,256,8]{2,1,0:T(8,128)} collective-permute-done((f32[4,256,8]{2,1,0:T(8,128)}, f32[4,256,8]{2,1,0:T(8,128)}, u32[]{:S(2)}, u32[]{:S(2)}) %collective-permute-start.4) | collective-permute-done | bytes 32800 | tf_op jit(solution)/shard_map/ppermute | solution.py:73
  88.6 5.6 %collective-permute-done = f32[4,256,8]{2,1,0:T(8,128)} collective-permute-done((f32[4,256,8]{2,1,0:T(8,128)}, f32[4,256,8]{2,1,0:T(8,128)}, u32[]{:S(2)}, u32[]{:S(2)}) %collective-permute-start) | collective-permute-done | bytes 32800 | tf_op jit(solution)/shard_map/ppermute | solution.py:73
  94.2 3.0 pad_maximum_fusion.1
  97.2 5.0 %collective-permute-start.6 = (f32[4,8,640]{2,1,0:T(8,128)S(1)}, f32[4,8,640]{2,1,0:T(8,128)S(1)}, u32[]{:S(2)}, u32[]{:S(2)}) collective-permute-start(f32[4,8,640]{2,1,0:T(8,128)S(1)} %get-tuple-element.16), channel_id=1, source_target_pairs={{0,16},{16,32},{32,48},{48,64},{64,80},{80,96},{96,112},{1,17},{17... | collective-permute-start | bytes 245768 | tf_op jit(solution)/shard_map/ppermute | solution.py:76
  102.2 1.9 collective-permute-start.7
  104.2 3.4 %collective-permute-start.2 = (f32[4,8,640]{2,1,0:T(8,128)S(1)}, f32[4,8,640]{2,1,0:T(8,128)S(1)}, u32[]{:S(2)}, u32[]{:S(2)}) collective-permute-start(f32[4,8,640]{2,1,0:T(8,128)S(1)} %get-tuple-element.18), channel_id=1, source_target_pairs={{0,16},{16,32},{32,48},{48,64},{64,80},{80,96},{96,112},{1,17},{17... | collective-permute-start | bytes 245768 | tf_op jit(solution)/shard_map/ppermute | solution.py:76
  107.6 2.1 collective-permute-start.3
  110.3 1.7 constant_dynamic-update-slice_fusion.7
  114.0 1.7 constant_dynamic-update-slice_fusion.2
  115.7 6.1 %reshape.130 = f32[256,4096]{1,0:T(8,128)} reshape(f32[128,2,4096]{2,1,0:T(2,128)} %all-to-all-done.1) | data formatting | bytes 8388608 | tf_op jit(solution)/shard_map/reshape | solution.py:251
  121.8 5.6 %copy.24 = f32[4096,256]{1,0:T(8,128)} copy(f32[4096,256]{0,1:T(8,128)} %bitcast.34) | data formatting | bytes 8388608 | tf_op jit(solution)/shard_map/dot_general | solution.py:290
  127.4 5.2 %convolution_bitcast_fusion = f32[4,64,8,64]{3,2,1,0:T(8,128)S(1)} fusion(f32[64,64,256,1]{2,1,0,3:T(8,128)} %bitcast.33, s32[256]{0:T(256)S(1)} %eq.158, s32[4,8]{1,0:T(4,128)S(1)} %multiply_add_fusion), kind=kOutput, calls=%fused_computation.4 | convolution fusion | flops 402661376 | bytes 4719744 | tf_op jit(solution)/shard_map/dot_general | solution.py:290
  133.0 1.9 collective-permute-start.8
  134.9 7.3 %collective-permute-start.9 = (f32[1,256,8]{2,1,0:T(8,128)S(1)}, f32[1,256,8]{2,1,0:T(8,128)S(1)}, u32[]{:S(2)}, u32[]{:S(2)}) collective-permute-start(f32[1,256,8]{2,1,0:T(8,128)S(1)} %get-tuple-element.30), channel_id=1, source_target_pairs={{0,1},{1,2},{2,3},{3,4},{4,5},{5,6},{6,7},{7,8},{8,9},{9,10},{10,1... | collective-permute-start | bytes 24584 | tf_op jit(solution)/shard_map/ppermute | solution.py:72
  142.9 1.2 collective-permute-done.9
  144.2 3.4 %collective-permute-start.10 = (f32[1,8,640]{2,1,0:T(8,128)S(1)}, f32[1,8,640]{2,1,0:T(8,128)S(1)}, u32[]{:S(2)}, u32[]{:S(2)}) collective-permute-start(f32[1,8,640]{2,1,0:T(8,128)S(1)} %get-tuple-element.26), channel_id=1, source_target_pairs={{0,16},{16,32},{32,48},{48,64},{64,80},{80,96},{96,112},{1,17},{17... | collective-permute-start | bytes 61448 | tf_op jit(solution)/shard_map/ppermute | solution.py:76
  148.3 1.9 collective-permute-start.11
  150.3 2.5 collective-permute-done.11
  152.8 0.9 copy-done.2
  153.6 26.8 %shard_map.94 = f32[4,256,512]{2,1,0:T(8,128)} custom-call(f32[4,288,640]{2,1,0:T(8,128)} %constant_dynamic-update-slice_fusion.f_ref, f32[4,288,640]{2,1,0:T(8,128)} %constant_dynamic-update-slice_fusion.5.r_ref, f32[288,640]{1,0:T(8,128)} %bitcast.37), custom_call_target="tpu_custom_call" | custom-call | tf_op jit(solution)/shard_map/pallas_call | solution.py:208
  180.4 1.1 fusion.1
  181.6 1.9 collective-permute-start.12
  183.6 9.4 %collective-permute-start.13 = (f32[1,256,8]{2,1,0:T(8,128)S(1)}, f32[1,256,8]{2,1,0:T(8,128)S(1)}, u32[]{:S(2)}, u32[]{:S(2)}) collective-permute-start(f32[1,256,8]{2,1,0:T(8,128)S(1)} %get-tuple-element.28), channel_id=1, source_target_pairs={{0,1},{1,2},{2,3},{3,4},{4,5},{5,6},{6,7},{7,8},{8,9},{9,10},{10,1... | collective-permute-start | bytes 24584 | tf_op jit(solution)/shard_map/ppermute | solution.py:72
  193.7 1.2 collective-permute-done.13
  195.0 5.2 %collective-permute-start.14 = (f32[1,8,640]{2,1,0:T(8,128)S(1)}, f32[1,8,640]{2,1,0:T(8,128)S(1)}, u32[]{:S(2)}, u32[]{:S(2)}) collective-permute-start(f32[1,8,640]{2,1,0:T(8,128)S(1)} %get-tuple-element.24), channel_id=1, source_target_pairs={{0,16},{16,32},{32,48},{48,64},{64,80},{80,96},{96,112},{1,17},{17... | collective-permute-start | bytes 61448 | tf_op jit(solution)/shard_map/ppermute | solution.py:76
  200.4 1.9 collective-permute-start.15
  202.4 4.9 %collective-permute-done.15 = f32[1,8,640]{2,1,0:T(8,128)S(1)} collective-permute-done((f32[1,8,640]{2,1,0:T(8,128)S(1)}, f32[1,8,640]{2,1,0:T(8,128)S(1)}, u32[]{:S(2)}, u32[]{:S(2)}) %collective-permute-start.15) | collective-permute-done | bytes 20512 | tf_op jit(solution)/shard_map/ppermute | solution.py:77
  207.3 0.9 copy-done.1
  208.2 26.8 %shard_map.95 = (f32[4,256,512]{2,1,0:T(8,128)}, f32[256,512]{1,0:T(8,128)}) custom-call(f32[288,640]{1,0:T(8,128)} %bitcast.36, f32[4,288,640]{2,1,0:T(8,128)} %constant_dynamic-update-slice_fusion.5.r_ref), custom_call_target="tpu_custom_call" | custom-call | tf_op jit(solution)/shard_map/pallas_call | solution.py:220
  235.0 1.2 reshape.131
  236.8 1.8 fusion.2
  238.6 3.2 %copy.27 = f32[128,2,4096]{2,1,0:T(2,128)S(1)} copy(f32[128,2,4096]{2,0,1:T(8,128)S(1)} %fusion.2) | data formatting | bytes 8388608 | tf_op jit(solution)/shard_map/dot_general | solution.py:308
  241.8 63.1 %all_to_all.16 = f32[128,2,4096]{2,1,0:T(2,128)} all-to-all(f32[128,2,4096]{2,1,0:T(2,128)S(1)} %copy.27), channel_id=1, replica_groups=mesh['row'=8,'col'=16] {'row','col'}, dimensions={0} | all-to-all | bytes 8388608 | tf_op jit(solution)/shard_map/all_to_all | solution.py:257
  305.0 6.1 %reshape.133 = f32[256,4096]{1,0:T(8,128)} reshape(f32[128,2,4096]{2,1,0:T(2,128)} %all_to_all.16) | data formatting | bytes 8388608 | tf_op jit(solution)/shard_map/reshape | solution.py:264
  311.0 3.9 %convolution_multiply_fusion = f32[64,4096]{1,0:T(8,128)S(1)} fusion(f32[256,4096]{1,0:T(8,128)} %reshape.133, s32[64]{0:T(128)S(1)} %get-tuple-element.33), kind=kOutput, calls=%fused_computation | convolution fusion | flops 805584896 | bytes 5243136 | tf_op jit(solution)/shard_map/dot_general | solution.py:310
  315.0 2.2 reshape.134
  (64 shorter events, 11.7 us)
Async XLA Ops:
  3.0 19.9 %all-to-all-start = ((s32[128,1,2]{2,1,0:T(1,128)}), s32[128,1,2]{2,1,0:T(1,128)S(1)}, u32[]{:S(2)}, u32[]{:S(2)}) async-start(s32[128,1,2]{2,1,0:T(1,128)} %bitcast.1), calls=%async_computation | async-start | bytes 131072 | tf_op jit(solution)/shard_map/all_to_all | solution.py:242
  22.9 10.2 %copy-start.4 = (f32[4,8]{1,0:T(4,128)S(1)}, f32[4,8]{1,0:T(4,128)}, u32[]{:S(2)}) copy-start(f32[4,8]{1,0:T(4,128)} %param.12) | copy-start | bytes 388
  23.0 92.8 %all-to-all-start.1 = ((f32[128,2,4096]{2,1,0:T(2,128)}), f32[128,2,4096]{2,1,0:T(2,128)}, u32[]{:S(2)}, u32[]{:S(2)}) async-start(f32[128,2,4096]{2,1,0:T(2,128)} %copy.23), calls=%async_computation.1 | async-start | bytes 8388608 | tf_op jit(solution)/shard_map/all_to_all | solution.py:235
  33.5 14.0 %copy-start = (f32[4,256,512]{2,1,0:T(8,128)S(1)}, f32[4,256,512]{2,1,0:T(8,128)}, u32[]{:S(2)}) copy-start(f32[4,256,512]{2,1,0:T(8,128)} %param.7) | copy-start | bytes 6291460
  38.3 50.2 %collective-permute-start.4 = (f32[4,256,8]{2,1,0:T(8,128)}, f32[4,256,8]{2,1,0:T(8,128)}, u32[]{:S(2)}, u32[]{:S(2)}) collective-permute-start(f32[4,256,8]{2,1,0:T(8,128)} %get-tuple-element.19), channel_id=1, source_target_pairs={{1,0},{2,1},{3,2},{4,3},{5,4},{6,5},{7,6},{8,7},{9,8},{10,9},{11,1... | collective-permute-start | bytes 98312 | tf_op jit(solution)/shard_map/ppermute | solution.py:73
  40.6 47.9 %collective-permute-start.5 = (f32[4,256,8]{2,1,0:T(8,128)S(1)}, f32[4,256,8]{2,1,0:T(8,128)}, u32[]{:S(2)}, u32[]{:S(2)}) collective-permute-start(f32[4,256,8]{2,1,0:T(8,128)S(1)} %get-tuple-element.20), channel_id=1, source_target_pairs={{0,1},{1,2},{2,3},{3,4},{4,5},{5,6},{6,7},{7,8},{8,9},{9,10},{10,1... | collective-permute-start | bytes 98312 | tf_op jit(solution)/shard_map/ppermute | solution.py:72
  48.6 45.5 %collective-permute-start = (f32[4,256,8]{2,1,0:T(8,128)}, f32[4,256,8]{2,1,0:T(8,128)}, u32[]{:S(2)}, u32[]{:S(2)}) collective-permute-start(f32[4,256,8]{2,1,0:T(8,128)} %get-tuple-element.21), channel_id=1, source_target_pairs={{1,0},{2,1},{3,2},{4,3},{5,4},{6,5},{7,6},{8,7},{9,8},{10,9},{11,1... | collective-permute-start | bytes 98312 | tf_op jit(solution)/shard_map/ppermute | solution.py:73
  50.5 43.6 %collective-permute-start.1 = (f32[4,256,8]{2,1,0:T(8,128)}, f32[4,256,8]{2,1,0:T(8,128)}, u32[]{:S(2)}, u32[]{:S(2)}) collective-permute-start(f32[4,256,8]{2,1,0:T(8,128)} %get-tuple-element.22), channel_id=1, source_target_pairs={{0,1},{1,2},{2,3},{3,4},{4,5},{5,6},{6,7},{7,8},{8,9},{9,10},{10,1... | collective-permute-start | bytes 98312 | tf_op jit(solution)/shard_map/ppermute | solution.py:72
  97.2 12.5 %collective-permute-start.6 = (f32[4,8,640]{2,1,0:T(8,128)S(1)}, f32[4,8,640]{2,1,0:T(8,128)S(1)}, u32[]{:S(2)}, u32[]{:S(2)}) collective-permute-start(f32[4,8,640]{2,1,0:T(8,128)S(1)} %get-tuple-element.16), channel_id=1, source_target_pairs={{0,16},{16,32},{32,48},{48,64},{64,80},{80,96},{96,112},{1,17},{17... | collective-permute-start | bytes 245768 | tf_op jit(solution)/shard_map/ppermute | solution.py:76
  102.2 9.8 %collective-permute-start.7 = (f32[4,8,640]{2,1,0:T(8,128)S(1)}, f32[4,8,640]{2,1,0:T(8,128)S(1)}, u32[]{:S(2)}, u32[]{:S(2)}) collective-permute-start(f32[4,8,640]{2,1,0:T(8,128)S(1)} %get-tuple-element.15), channel_id=1, source_target_pairs={{16,0},{32,16},{48,32},{64,48},{80,64},{96,80},{112,96},{17,1},{33... | collective-permute-start | bytes 245768 | tf_op jit(solution)/shard_map/ppermute | solution.py:77
  104.2 9.2 %collective-permute-start.2 = (f32[4,8,640]{2,1,0:T(8,128)S(1)}, f32[4,8,640]{2,1,0:T(8,128)S(1)}, u32[]{:S(2)}, u32[]{:S(2)}) collective-permute-start(f32[4,8,640]{2,1,0:T(8,128)S(1)} %get-tuple-element.18), channel_id=1, source_target_pairs={{0,16},{16,32},{32,48},{48,64},{64,80},{80,96},{96,112},{1,17},{17... | collective-permute-start | bytes 245768 | tf_op jit(solution)/shard_map/ppermute | solution.py:76
  107.6 34.6 %collective-permute-start.3 = (f32[4,8,640]{2,1,0:T(8,128)S(1)}, f32[4,8,640]{2,1,0:T(8,128)S(1)}, u32[]{:S(2)}, u32[]{:S(2)}) collective-permute-start(f32[4,8,640]{2,1,0:T(8,128)S(1)} %get-tuple-element.17), channel_id=1, source_target_pairs={{16,0},{32,16},{48,32},{64,48},{80,64},{96,80},{112,96},{17,1},{33... | collective-permute-start | bytes 245768 | tf_op jit(solution)/shard_map/ppermute | solution.py:77
  133.0 9.9 %collective-permute-start.8 = (f32[1,256,8]{2,1,0:T(8,128)S(1)}, f32[1,256,8]{2,1,0:T(8,128)S(1)}, u32[]{:S(2)}, u32[]{:S(2)}) collective-permute-start(f32[1,256,8]{2,1,0:T(8,128)S(1)} %get-tuple-element.29), channel_id=1, source_target_pairs={{1,0},{2,1},{3,2},{4,3},{5,4},{6,5},{7,6},{8,7},{9,8},{10,9},{11,1... | collective-permute-start | bytes 24584 | tf_op jit(solution)/shard_map/ppermute | solution.py:73
  134.9 9.2 %collective-permute-start.9 = (f32[1,256,8]{2,1,0:T(8,128)S(1)}, f32[1,256,8]{2,1,0:T(8,128)S(1)}, u32[]{:S(2)}, u32[]{:S(2)}) collective-permute-start(f32[1,256,8]{2,1,0:T(8,128)S(1)} %get-tuple-element.30), channel_id=1, source_target_pairs={{0,1},{1,2},{2,3},{3,4},{4,5},{5,6},{6,7},{7,8},{8,9},{9,10},{10,1... | collective-permute-start | bytes 24584 | tf_op jit(solution)/shard_map/ppermute | solution.py:72
  144.2 5.9 %collective-permute-start.10 = (f32[1,8,640]{2,1,0:T(8,128)S(1)}, f32[1,8,640]{2,1,0:T(8,128)S(1)}, u32[]{:S(2)}, u32[]{:S(2)}) collective-permute-start(f32[1,8,640]{2,1,0:T(8,128)S(1)} %get-tuple-element.26), channel_id=1, source_target_pairs={{0,16},{16,32},{32,48},{48,64},{64,80},{80,96},{96,112},{1,17},{17... | collective-permute-start | bytes 61448 | tf_op jit(solution)/shard_map/ppermute | solution.py:76
  148.3 4.5 %collective-permute-start.11 = (f32[1,8,640]{2,1,0:T(8,128)S(1)}, f32[1,8,640]{2,1,0:T(8,128)S(1)}, u32[]{:S(2)}, u32[]{:S(2)}) collective-permute-start(f32[1,8,640]{2,1,0:T(8,128)S(1)} %get-tuple-element.25), channel_id=1, source_target_pairs={{16,0},{32,16},{48,32},{64,48},{80,64},{96,80},{112,96},{17,1},{33... | collective-permute-start | bytes 61448 | tf_op jit(solution)/shard_map/ppermute | solution.py:77
  152.8 0.9 copy-start.2
  153.6 26.8 %copy-start.3 = (f32[256,512]{1,0:T(8,128)S(1)}, f32[256,512]{1,0:T(8,128)}, u32[]{:S(2)}) copy-start(f32[256,512]{1,0:T(8,128)} %param.13) | copy-start | bytes 1572868
  181.6 12.0 %collective-permute-start.12 = (f32[1,256,8]{2,1,0:T(8,128)S(1)}, f32[1,256,8]{2,1,0:T(8,128)S(1)}, u32[]{:S(2)}, u32[]{:S(2)}) collective-permute-start(f32[1,256,8]{2,1,0:T(8,128)S(1)} %get-tuple-element.27), channel_id=1, source_target_pairs={{1,0},{2,1},{3,2},{4,3},{5,4},{6,5},{7,6},{8,7},{9,8},{10,9},{11,1... | collective-permute-start | bytes 24584 | tf_op jit(solution)/shard_map/ppermute | solution.py:73
  183.6 11.3 %collective-permute-start.13 = (f32[1,256,8]{2,1,0:T(8,128)S(1)}, f32[1,256,8]{2,1,0:T(8,128)S(1)}, u32[]{:S(2)}, u32[]{:S(2)}) collective-permute-start(f32[1,256,8]{2,1,0:T(8,128)S(1)} %get-tuple-element.28), channel_id=1, source_target_pairs={{0,1},{1,2},{2,3},{3,4},{4,5},{5,6},{6,7},{7,8},{8,9},{9,10},{10,1... | collective-permute-start | bytes 24584 | tf_op jit(solution)/shard_map/ppermute | solution.py:72
  195.0 7.3 %collective-permute-start.14 = (f32[1,8,640]{2,1,0:T(8,128)S(1)}, f32[1,8,640]{2,1,0:T(8,128)S(1)}, u32[]{:S(2)}, u32[]{:S(2)}) collective-permute-start(f32[1,8,640]{2,1,0:T(8,128)S(1)} %get-tuple-element.24), channel_id=1, source_target_pairs={{0,16},{16,32},{32,48},{48,64},{64,80},{80,96},{96,112},{1,17},{17... | collective-permute-start | bytes 61448 | tf_op jit(solution)/shard_map/ppermute | solution.py:76
  200.4 6.9 %collective-permute-start.15 = (f32[1,8,640]{2,1,0:T(8,128)S(1)}, f32[1,8,640]{2,1,0:T(8,128)S(1)}, u32[]{:S(2)}, u32[]{:S(2)}) collective-permute-start(f32[1,8,640]{2,1,0:T(8,128)S(1)} %get-tuple-element.23), channel_id=1, source_target_pairs={{16,0},{32,16},{48,32},{64,48},{80,64},{96,80},{112,96},{17,1},{33... | collective-permute-start | bytes 61448 | tf_op jit(solution)/shard_map/ppermute | solution.py:77
  207.3 0.9 copy-start.1

commit v3 on v2

--- a/solution.py
+++ b/solution.py
@@ -69,8 +69,12 @@
     depth, height, breadth = cells.shape
     cols = lax.axis_size("col")
     rows = lax.axis_size("row")
-    left = lax.ppermute(cells[:, :, breadth - HALO :], "col", [(i, i + 1) for i in range(cols - 1)])
-    right = lax.ppermute(cells[:, :, :HALO], "col", [(i + 1, i) for i in range(cols - 1)])
+    left = lax.ppermute(
+        jnp.swapaxes(cells[:, :, breadth - HALO :], 1, 2), "col", [(i, i + 1) for i in range(cols - 1)]
+    )
+    right = lax.ppermute(jnp.swapaxes(cells[:, :, :HALO], 1, 2), "col", [(i + 1, i) for i in range(cols - 1)])
+    left = jnp.swapaxes(left, 1, 2)
+    right = jnp.swapaxes(right, 1, 2)
     gap = jnp.zeros((depth, height, LANE - 2 * HALO), cells.dtype)
     band = jnp.concatenate([cells, right, gap, left], axis=2)
     top = lax.ppermute(band[:, height - HALO :], "row", [(i, i + 1) for i in range(rows - 1)])
@@ -230,27 +234,15 @@
     )(a0_frame, r_frame)
 
 
-def send_dies(outbound, tile_ids, row_count, col_count):
-    received, recv_tiles = (
-        lax.all_to_all(
-            outbound.reshape(row_count * col_count, CAP, -1),
-            ("row", "col"),
-            split_axis=0,
-            concat_axis=0,
-            tiled=True,
-        ),
-        lax.all_to_all(
-            tile_ids.reshape(row_count * col_count, CAP),
-            ("row", "col"),
-            split_axis=0,
-            concat_axis=0,
-            tiled=True,
-        ),
-    )
-    return (
-        received.reshape(row_count * col_count * CAP, -1),
-        recv_tiles.reshape(row_count * col_count * CAP),
-    )
+def send_dies(outbound, row_count, col_count):
+    received = lax.all_to_all(
+        outbound.reshape(row_count * col_count, CAP, -1),
+        ("row", "col"),
+        split_axis=0,
+        concat_axis=0,
+        tiled=True,
+    )
+    return received.reshape(row_count * col_count * CAP, -1)
 
 
 def return_grads(backward, row_count, col_count):
@@ -282,9 +274,11 @@
     all_slots = jnp.arange(devices_all * CAP, dtype=jnp.int32)
     matched = all_slots[:, None] == slot_index[None, :]
     send_hot = matched.astype(jnp.float32)
-    outbound = jnp.dot(send_hot, power_flat, precision=highest)
-    tile_ids = jnp.sum(jnp.where(matched, die_tile[None, :] + 1, 0), axis=1) - 1
-    received, recv_tiles = send_dies(outbound, tile_ids, row_count, col_count)
+    tile_column = jnp.zeros((die_count, LANE), jnp.float32).at[:, 0].set((die_tile + 1).astype(jnp.float32))
+    outbound = jnp.dot(send_hot, jnp.concatenate([power_flat, tile_column], 1), precision=highest)
+    received = send_dies(outbound, row_count, col_count)
+    recv_tiles = received[:, TILE * TILE].astype(jnp.int32) - 1
+    received = received[:, : TILE * TILE]
     tile_range = jnp.arange(tile_rows * tile_cols, dtype=jnp.int32)
     recv_hot = (tile_range[:, None] == recv_tiles[None, :]).astype(jnp.float32)
     source_tiles = jnp.dot(recv_hot, received, precision=highest)

time: 322 us -> 306 us (0.950)
  local copies, waits for them, and re-layouts: 47 us -> 37.1 us
  starting transfers between devices: 84.5 us -> 75.1 us
  waiting for transfers between devices: 44.2 us -> 50.1 us
    dot_general x2 -> x0, local copies, waits for them, and re-layouts: 10.8 us -> none  [the longest x1 5.6 us: on_device(): source_tiles = jnp.dot(recv_hot, received, precision=highest)]
    all_to_all x1 -> x0, starting transfers between devices: 10.6 us -> none  [send_dies(): lax.all_to_all(tile_ids.reshape(row_count * col_count, CAP), ('row', 'col...]
    reshape x1 -> x4, local copies, waits for them, and re-layouts: 6.07 us -> 13.3 us  [the longest x1 6.25 us: send_dies(): return received.reshape(row_count * col_count * CAP, -1)]
    ppermute x8, waiting for transfers between devices: 36.8 us -> 42.9 us  [the longest x4 40.5 us: framed(): lax.ppermute(jnp.swapaxes(cells[:, :, :HALO], 1, 2), 'col', [(i + 1, i) f...]
    unnamed x24 -> x33, local copies, waits for them, and re-layouts: 9.07 us -> 6.42 us
  transfers between devices with their start and end apart: 18 -> 17, of which waited for: 7 -> 8; matrix products, arithmetic and copies ran while one was open for 15% -> 7% of each run, Pallas kernels for 0% -> 0%
where the time goes in v3:
time: 306 us; the launch traced here: 302 us
  starting transfers between devices  75.1 us (25%)
  blocking collectives  63.1 us (21%)
  Pallas kernels  53.6 us (18%)
  waiting for transfers between devices  50.1 us (16%)
  local copies, waits for them, and re-layouts  37.1 us (12%)
  matrix products  13.4 us (4%)
  other arithmetic  8.31 us (3%)
    all_to_all x1, blocking collectives, return_grads(): lax.all_to_all(backward.reshape(row_count * col_count, CAP, -1), ('row',...  63.1 us
    ppermute x4, waiting for transfers between devices, framed(): lax.ppermute(jnp.swapaxes(cells[:, :, :HALO], 1, 2), 'col', [(i + 1, i) f...  40.5 us
    ppermute x4, starting transfers between devices, framed(): lax.ppermute(jnp.swapaxes(cells[:, :, breadth - HALO:], 1, 2), 'col', [(i...  30.8 us
    pallas_call x1, Pallas kernels, run_adjoint(): pl.pallas_call(adjoint_kernel, out_shape=(jax.ShapeDtypeStruct((layers, h...  26.8 us
    pallas_call x1, Pallas kernels, run_forward(): pl.pallas_call(forward_kernel, out_shape=jax.ShapeDtypeStruct((layers, he...  26.8 us
    ppermute x4, starting transfers between devices, framed(): lax.ppermute(band[:, height - HALO:], 'row', [(i, i + 1) for i in range(r...  17.2 us
    all_to_all x1, starting transfers between devices, send_dies(): lax.all_to_all(outbound.reshape(row_count * col_count, CAP, -1), ('row',...  11 us
    ppermute x4, starting transfers between devices, framed(): lax.ppermute(band[:, :HALO], 'row', [(i + 1, i) for i in range(rows - 1)])  8.07 us
  transfers between devices with their start and end apart: 17, of which 8 were waited for; matrix products, arithmetic and copies ran while one was open for 7% of the time, Pallas kernels for 0%

profile of v3, /device:TPU:15, one launch (start us, length us, event | category | flops | bytes accessed | tf_op | source)
XLA Modules:
  0.0 301.8 jit_solution(1450462794933879698)
XLA Ops:
  1.3 0.8 convert_reduce_fusion
  2.1 0.7 multiply_add_fusion
  2.8 2.1 reshape.110
  5.7 3.8 %fusion.2 = f32[256,4224]{1,0:T(8,128)} fusion(f32[64,1]{1,0:T(8,128)S(1)} %copy.34, f32[64,4096]{1,0:T(8,128)S(1)} %reshape.110, s32[64]{0:T(128)S(1)} %multiply_add_fusion), kind=kOutput, calls=%fused_computation.7 | convolution fusion | flops 831299584 | bytes 5374464 | tf_op jit(solution)/shard_map/dot_general | solution.py:278
  9.5 6.0 %reshape.112 = f32[128,2,4224]{2,1,0:T(2,128)} reshape(f32[256,4224]{1,0:T(8,128)} %fusion.2) | data formatting | bytes 8650752 | tf_op jit(solution)/shard_map/reshape | solution.py:239
  15.5 11.0 %all-to-all-start = ((f32[128,2,4224]{2,1,0:T(2,128)}), f32[128,2,4224]{2,1,0:T(2,128)}, u32[]{:S(2)}, u32[]{:S(2)}) async-start(f32[128,2,4224]{2,1,0:T(2,128)} %reshape.112), calls=%async_computation | async-start | bytes 8650752 | tf_op jit(solution)/shard_map/all_to_all | solution.py:238
  26.9 2.1 add_sqrt_fusion
  29.2 2.3 collective-permute-start.4
  31.5 6.9 %collective-permute-start.5 = (f32[4,8,256]{1,2,0:T(8,128)S(1)}, f32[4,8,256]{1,2,0:T(8,128)S(1)}, u32[]{:S(2)}, u32[]{:S(2)}) collective-permute-start(f32[4,8,256]{1,2,0:T(8,128)S(1)} %get-tuple-element.32), channel_id=1, source_target_pairs={{0,1},{1,2},{2,3},{3,4},{4,5},{5,6},{6,7},{7,8},{8,9},{9,10},{10,1... | collective-permute-start | bytes 98312 | tf_op jit(solution)/shard_map/ppermute | solution.py:72
  38.6 1.9 collective-permute-start
  40.5 7.3 %collective-permute-start.1 = (f32[4,8,256]{1,2,0:T(8,128)S(1)}, f32[4,8,256]{1,2,0:T(8,128)S(1)}, u32[]{:S(2)}, u32[]{:S(2)}) collective-permute-start(f32[4,8,256]{1,2,0:T(8,128)S(1)} %get-tuple-element.34), channel_id=1, source_target_pairs={{0,1},{1,2},{2,3},{3,4},{4,5},{5,6},{6,7},{7,8},{8,9},{9,10},{10,1... | collective-permute-start | bytes 98312 | tf_op jit(solution)/shard_map/ppermute | solution.py:72
  49.1 34.1 %collective-permute-done.4 = f32[4,8,256]{1,2,0:T(8,128)S(1)} collective-permute-done((f32[4,8,256]{1,2,0:T(8,128)S(1)}, f32[4,8,256]{1,2,0:T(8,128)S(1)}, u32[]{:S(2)}, u32[]{:S(2)}) %collective-permute-start.4) | collective-permute-done | bytes 32800 | tf_op jit(solution)/shard_map/ppermute | solution.py:75
  83.2 5.6 %collective-permute-done = f32[4,8,256]{1,2,0:T(8,128)S(1)} collective-permute-done((f32[4,8,256]{1,2,0:T(8,128)S(1)}, f32[4,8,256]{1,2,0:T(8,128)S(1)}, u32[]{:S(2)}, u32[]{:S(2)}) %collective-permute-start) | collective-permute-done | bytes 32800 | tf_op jit(solution)/shard_map/ppermute | solution.py:75
  88.9 0.8 pad_maximum_fusion.1
  89.7 4.7 %collective-permute-start.6 = (f32[4,8,640]{2,1,0:T(8,128)S(1)}, f32[4,8,640]{2,1,0:T(8,128)S(1)}, u32[]{:S(2)}, u32[]{:S(2)}) collective-permute-start(f32[4,8,640]{2,1,0:T(8,128)S(1)} %get-tuple-element.28), channel_id=1, source_target_pairs={{0,16},{16,32},{32,48},{48,64},{64,80},{80,96},{96,112},{1,17},{17... | collective-permute-start | bytes 245768 | tf_op jit(solution)/shard_map/ppermute | solution.py:80
  94.4 1.9 collective-permute-start.7
  96.4 3.4 %collective-permute-start.2 = (f32[4,8,640]{2,1,0:T(8,128)S(1)}, f32[4,8,640]{2,1,0:T(8,128)S(1)}, u32[]{:S(2)}, u32[]{:S(2)}) collective-permute-start(f32[4,8,640]{2,1,0:T(8,128)S(1)} %get-tuple-element.30), channel_id=1, source_target_pairs={{0,16},{16,32},{32,48},{48,64},{64,80},{80,96},{96,112},{1,17},{17... | collective-permute-start | bytes 245768 | tf_op jit(solution)/shard_map/ppermute | solution.py:80
  99.7 2.1 collective-permute-start.3
  102.1 0.7 constant_dynamic-update-slice_fusion.3
  102.8 1.8 constant_dynamic-update-slice_fusion.2
  104.6 6.2 %reshape.113 = f32[256,4224]{1,0:T(8,128)} reshape(f32[128,2,4224]{2,1,0:T(2,128)} %all-to-all-done) | data formatting | bytes 8650752 | tf_op jit(solution)/shard_map/reshape | solution.py:245
  110.8 1.0 fusion.10
  111.9 3.8 %fusion = f32[32,4096]{1,0:T(8,128)S(1)} fusion(f32[256,4224]{1,0:T(8,128)} %reshape.113, s32[256]{0:T(256)S(1)} %fusion.10), kind=kOutput, calls=%fused_computation.1 | convolution fusion | flops 402661376 | bytes 4719616 | tf_op jit(solution)/shard_map/dot_general | solution.py:284
  117.1 1.9 collective-permute-start.8
  119.0 7.3 %collective-permute-start.9 = (f32[1,8,256]{1,2,0:T(8,128)S(1)}, f32[1,8,256]{1,2,0:T(8,128)S(1)}, u32[]{:S(2)}, u32[]{:S(2)}) collective-permute-start(f32[1,8,256]{1,2,0:T(8,128)S(1)} %get-tuple-element.42), channel_id=1, source_target_pairs={{0,1},{1,2},{2,3},{3,4},{4,5},{5,6},{6,7},{7,8},{8,9},{9,10},{10,1... | collective-permute-start | bytes 24584 | tf_op jit(solution)/shard_map/ppermute | solution.py:72
  127.0 1.2 collective-permute-done.9
  128.3 3.4 %collective-permute-start.10 = (f32[1,8,640]{2,1,0:T(8,128)S(1)}, f32[1,8,640]{2,1,0:T(8,128)S(1)}, u32[]{:S(2)}, u32[]{:S(2)}) collective-permute-start(f32[1,8,640]{2,1,0:T(8,128)S(1)} %get-tuple-element.38), channel_id=1, source_target_pairs={{0,16},{16,32},{32,48},{48,64},{64,80},{80,96},{96,112},{1,17},{17... | collective-permute-start | bytes 61448 | tf_op jit(solution)/shard_map/ppermute | solution.py:80
  132.4 1.9 collective-permute-start.11
  134.4 2.5 collective-permute-done.11
  136.9 0.9 copy-done.5
  137.7 26.8 %shard_map.94 = f32[4,256,512]{2,1,0:T(8,128)} custom-call(f32[4,288,640]{2,1,0:T(8,128)} %constant_dynamic-update-slice_fusion.f_ref, f32[4,288,640]{2,1,0:T(8,128)} %copy-done, f32[288,640]{1,0:T(8,128)} %bitcast.51), custom_call_target="tpu_custom_call" | custom-call | tf_op jit(solution)/shard_map/pallas_call | solution.py:212
  164.5 1.1 fusion.8
  165.7 1.9 collective-permute-start.12
  167.7 9.4 %collective-permute-start.13 = (f32[1,8,256]{1,2,0:T(8,128)S(1)}, f32[1,8,256]{1,2,0:T(8,128)S(1)}, u32[]{:S(2)}, u32[]{:S(2)}) collective-permute-start(f32[1,8,256]{1,2,0:T(8,128)S(1)} %get-tuple-element.40), channel_id=1, source_target_pairs={{0,1},{1,2},{2,3},{3,4},{4,5},{5,6},{6,7},{7,8},{8,9},{9,10},{10,1... | collective-permute-start | bytes 24584 | tf_op jit(solution)/shard_map/ppermute | solution.py:72
  177.1 0.7 collective-permute-done.12
  177.8 1.2 collective-permute-done.13
  179.1 5.7 %collective-permute-start.14 = (f32[1,8,640]{2,1,0:T(8,128)S(1)}, f32[1,8,640]{2,1,0:T(8,128)S(1)}, u32[]{:S(2)}, u32[]{:S(2)}) collective-permute-start(f32[1,8,640]{2,1,0:T(8,128)S(1)} %get-tuple-element.36), channel_id=1, source_target_pairs={{0,16},{16,32},{32,48},{48,64},{64,80},{80,96},{96,112},{1,17},{17... | collective-permute-start | bytes 61448 | tf_op jit(solution)/shard_map/ppermute | solution.py:80
  185.0 2.1 collective-permute-start.15
  187.3 4.6 %collective-permute-done.15 = f32[1,8,640]{2,1,0:T(8,128)S(1)} collective-permute-done((f32[1,8,640]{2,1,0:T(8,128)S(1)}, f32[1,8,640]{2,1,0:T(8,128)S(1)}, u32[]{:S(2)}, u32[]{:S(2)}) %collective-permute-start.15) | collective-permute-done | bytes 20512 | tf_op jit(solution)/shard_map/ppermute | solution.py:81
  191.9 0.9 copy-done.3
  192.8 26.8 %shard_map.95 = (f32[4,256,512]{2,1,0:T(8,128)}, f32[256,512]{1,0:T(8,128)}) custom-call(f32[288,640]{1,0:T(8,128)} %bitcast.50, f32[4,288,640]{2,1,0:T(8,128)} %copy-done), custom_call_target="tpu_custom_call" | custom-call | tf_op jit(solution)/shard_map/pallas_call | solution.py:224
  219.6 1.2 reshape.115
  221.4 1.8 fusion.11
  223.2 3.2 %copy.33 = f32[128,2,4096]{2,1,0:T(2,128)S(1)} copy(f32[128,2,4096]{2,0,1:T(8,128)S(1)} %fusion.11) | data formatting | bytes 8388608 | tf_op jit(solution)/shard_map/dot_general | solution.py:302
  226.4 63.1 %all_to_all.10 = f32[128,2,4096]{2,1,0:T(2,128)} all-to-all(f32[128,2,4096]{2,1,0:T(2,128)S(1)} %copy.33), channel_id=1, replica_groups=mesh['row'=8,'col'=16] {'row','col'}, dimensions={0} | all-to-all | bytes 8388608 | tf_op jit(solution)/shard_map/all_to_all | solution.py:249
  289.6 6.1 %reshape.117 = f32[256,4096]{1,0:T(8,128)} reshape(f32[128,2,4096]{2,1,0:T(2,128)} %all_to_all.10) | data formatting | bytes 8388608 | tf_op jit(solution)/shard_map/reshape | solution.py:256
  295.7 3.9 %convolution_multiply_fusion = f32[64,4096]{1,0:T(8,128)S(1)} fusion(f32[256,4096]{1,0:T(8,128)} %reshape.117, s32[64]{0:T(128)S(1)} %multiply_add_fusion), kind=kOutput, calls=%fused_computation | convolution fusion | flops 805584896 | bytes 5243136 | tf_op jit(solution)/shard_map/dot_general | solution.py:304
  299.6 2.2 reshape.118
  (67 shorter events, 7.7 us)
Async XLA Ops:
  0.6 4.3 %copy-start.8 = (s32[64]{0:T(128)S(1)}, s32[64]{0:T(128)}, u32[]{:S(2)}) copy-start(s32[64]{0:T(128)} %param.12) | copy-start | bytes 772
  15.5 11.1 %copy-start.7 = (f32[4,8]{1,0:T(4,128)S(1)}, f32[4,8]{1,0:T(4,128)}, u32[]{:S(2)}) copy-start(f32[4,8]{1,0:T(4,128)} %param.14) | copy-start | bytes 388
  15.5 11.4 %copy-start.2 = (s32[4,256,512]{2,1,0:T(8,128)S(1)}, s32[4,256,512]{2,1,0:T(8,128)}, u32[]{:S(2)}) copy-start(s32[4,256,512]{2,1,0:T(8,128)} %param.13) | copy-start | bytes 6291460
  15.5 89.1 %all-to-all-start = ((f32[128,2,4224]{2,1,0:T(2,128)}), f32[128,2,4224]{2,1,0:T(2,128)}, u32[]{:S(2)}, u32[]{:S(2)}) async-start(f32[128,2,4224]{2,1,0:T(2,128)} %reshape.112), calls=%async_computation | async-start | bytes 8650752 | tf_op jit(solution)/shard_map/all_to_all | solution.py:238
  26.9 11.5 %copy-start.1 = (f32[4,256,512]{2,1,0:T(8,128)S(1)}, f32[4,256,512]{2,1,0:T(8,128)}, u32[]{:S(2)}) copy-start(f32[4,256,512]{2,1,0:T(8,128)} %param.9) | copy-start | bytes 6291460
  29.2 54.1 %collective-permute-start.4 = (f32[4,8,256]{1,2,0:T(8,128)S(1)}, f32[4,8,256]{1,2,0:T(8,128)S(1)}, u32[]{:S(2)}, u32[]{:S(2)}) collective-permute-start(f32[4,8,256]{1,2,0:T(8,128)S(1)} %get-tuple-element.31), channel_id=1, source_target_pairs={{1,0},{2,1},{3,2},{4,3},{5,4},{6,5},{7,6},{8,7},{9,8},{10,9},{11,1... | collective-permute-start | bytes 98312 | tf_op jit(solution)/shard_map/ppermute | solution.py:75
  31.5 51.8 %collective-permute-start.5 = (f32[4,8,256]{1,2,0:T(8,128)S(1)}, f32[4,8,256]{1,2,0:T(8,128)S(1)}, u32[]{:S(2)}, u32[]{:S(2)}) collective-permute-start(f32[4,8,256]{1,2,0:T(8,128)S(1)} %get-tuple-element.32), channel_id=1, source_target_pairs={{0,1},{1,2},{2,3},{3,4},{4,5},{5,6},{6,7},{7,8},{8,9},{9,10},{10,1... | collective-permute-start | bytes 98312 | tf_op jit(solution)/shard_map/ppermute | solution.py:72
  38.6 50.3 %collective-permute-start = (f32[4,8,256]{1,2,0:T(8,128)S(1)}, f32[4,8,256]{1,2,0:T(8,128)S(1)}, u32[]{:S(2)}, u32[]{:S(2)}) collective-permute-start(f32[4,8,256]{1,2,0:T(8,128)S(1)} %get-tuple-element.33), channel_id=1, source_target_pairs={{1,0},{2,1},{3,2},{4,3},{5,4},{6,5},{7,6},{8,7},{9,8},{10,9},{11,1... | collective-permute-start | bytes 98312 | tf_op jit(solution)/shard_map/ppermute | solution.py:75
  40.5 48.4 %collective-permute-start.1 = (f32[4,8,256]{1,2,0:T(8,128)S(1)}, f32[4,8,256]{1,2,0:T(8,128)S(1)}, u32[]{:S(2)}, u32[]{:S(2)}) collective-permute-start(f32[4,8,256]{1,2,0:T(8,128)S(1)} %get-tuple-element.34), channel_id=1, source_target_pairs={{0,1},{1,2},{2,3},{3,4},{4,5},{5,6},{6,7},{7,8},{8,9},{9,10},{10,1... | collective-permute-start | bytes 98312 | tf_op jit(solution)/shard_map/ppermute | solution.py:72
  89.7 12.2 %collective-permute-start.6 = (f32[4,8,640]{2,1,0:T(8,128)S(1)}, f32[4,8,640]{2,1,0:T(8,128)S(1)}, u32[]{:S(2)}, u32[]{:S(2)}) collective-permute-start(f32[4,8,640]{2,1,0:T(8,128)S(1)} %get-tuple-element.28), channel_id=1, source_target_pairs={{0,16},{16,32},{32,48},{48,64},{64,80},{80,96},{96,112},{1,17},{17... | collective-permute-start | bytes 245768 | tf_op jit(solution)/shard_map/ppermute | solution.py:80
  94.4 7.6 %collective-permute-start.7 = (f32[4,8,640]{2,1,0:T(8,128)S(1)}, f32[4,8,640]{2,1,0:T(8,128)S(1)}, u32[]{:S(2)}, u32[]{:S(2)}) collective-permute-start(f32[4,8,640]{2,1,0:T(8,128)S(1)} %get-tuple-element.27), channel_id=1, source_target_pairs={{16,0},{32,16},{48,32},{64,48},{80,64},{96,80},{112,96},{17,1},{33... | collective-permute-start | bytes 245768 | tf_op jit(solution)/shard_map/ppermute | solution.py:81
  96.4 5.7 %collective-permute-start.2 = (f32[4,8,640]{2,1,0:T(8,128)S(1)}, f32[4,8,640]{2,1,0:T(8,128)S(1)}, u32[]{:S(2)}, u32[]{:S(2)}) collective-permute-start(f32[4,8,640]{2,1,0:T(8,128)S(1)} %get-tuple-element.30), channel_id=1, source_target_pairs={{0,16},{16,32},{32,48},{48,64},{64,80},{80,96},{96,112},{1,17},{17... | collective-permute-start | bytes 245768 | tf_op jit(solution)/shard_map/ppermute | solution.py:80
  99.7 26.5 %collective-permute-start.3 = (f32[4,8,640]{2,1,0:T(8,128)S(1)}, f32[4,8,640]{2,1,0:T(8,128)S(1)}, u32[]{:S(2)}, u32[]{:S(2)}) collective-permute-start(f32[4,8,640]{2,1,0:T(8,128)S(1)} %get-tuple-element.29), channel_id=1, source_target_pairs={{16,0},{32,16},{48,32},{64,48},{80,64},{96,80},{112,96},{17,1},{33... | collective-permute-start | bytes 245768 | tf_op jit(solution)/shard_map/ppermute | solution.py:81
  102.1 2.5 copy-start
  116.1 18.2 %copy-start.4 = (f32[1,288,640]{2,1,0:T(8,128)S(1)}, f32[1,288,640]{2,1,0:T(8,128)}, u32[]{:S(2)}) copy-start(f32[1,288,640]{2,1,0:T(8,128)} %constant_dynamic-update-slice_fusion.14) | copy-start | bytes 2211844
  117.1 9.9 %collective-permute-start.8 = (f32[1,8,256]{1,2,0:T(8,128)S(1)}, f32[1,8,256]{1,2,0:T(8,128)S(1)}, u32[]{:S(2)}, u32[]{:S(2)}) collective-permute-start(f32[1,8,256]{1,2,0:T(8,128)S(1)} %get-tuple-element.41), channel_id=1, source_target_pairs={{1,0},{2,1},{3,2},{4,3},{5,4},{6,5},{7,6},{8,7},{9,8},{10,9},{11,1... | collective-permute-start | bytes 24584 | tf_op jit(solution)/shard_map/ppermute | solution.py:75
  119.0 9.2 %collective-permute-start.9 = (f32[1,8,256]{1,2,0:T(8,128)S(1)}, f32[1,8,256]{1,2,0:T(8,128)S(1)}, u32[]{:S(2)}, u32[]{:S(2)}) collective-permute-start(f32[1,8,256]{1,2,0:T(8,128)S(1)} %get-tuple-element.42), channel_id=1, source_target_pairs={{0,1},{1,2},{2,3},{3,4},{4,5},{5,6},{6,7},{7,8},{8,9},{9,10},{10,1... | collective-permute-start | bytes 24584 | tf_op jit(solution)/shard_map/ppermute | solution.py:72
  128.3 6.0 %collective-permute-start.10 = (f32[1,8,640]{2,1,0:T(8,128)S(1)}, f32[1,8,640]{2,1,0:T(8,128)S(1)}, u32[]{:S(2)}, u32[]{:S(2)}) collective-permute-start(f32[1,8,640]{2,1,0:T(8,128)S(1)} %get-tuple-element.38), channel_id=1, source_target_pairs={{0,16},{16,32},{32,48},{48,64},{64,80},{80,96},{96,112},{1,17},{17... | collective-permute-start | bytes 61448 | tf_op jit(solution)/shard_map/ppermute | solution.py:80
  132.4 4.5 %collective-permute-start.11 = (f32[1,8,640]{2,1,0:T(8,128)S(1)}, f32[1,8,640]{2,1,0:T(8,128)S(1)}, u32[]{:S(2)}, u32[]{:S(2)}) collective-permute-start(f32[1,8,640]{2,1,0:T(8,128)S(1)} %get-tuple-element.37), channel_id=1, source_target_pairs={{16,0},{32,16},{48,32},{64,48},{80,64},{96,80},{112,96},{17,1},{33... | collective-permute-start | bytes 61448 | tf_op jit(solution)/shard_map/ppermute | solution.py:81
  136.9 0.9 copy-start.5
  137.7 26.8 %copy-start.6 = (f32[256,512]{1,0:T(8,128)S(1)}, f32[256,512]{1,0:T(8,128)}, u32[]{:S(2)}) copy-start(f32[256,512]{1,0:T(8,128)} %param.15) | copy-start | bytes 1572868
  165.7 12.0 %collective-permute-start.12 = (f32[1,8,256]{1,2,0:T(8,128)S(1)}, f32[1,8,256]{1,2,0:T(8,128)S(1)}, u32[]{:S(2)}, u32[]{:S(2)}) collective-permute-start(f32[1,8,256]{1,2,0:T(8,128)S(1)} %get-tuple-element.39), channel_id=1, source_target_pairs={{1,0},{2,1},{3,2},{4,3},{5,4},{6,5},{7,6},{8,7},{9,8},{10,9},{11,1... | collective-permute-start | bytes 24584 | tf_op jit(solution)/shard_map/ppermute | solution.py:75
  167.7 11.3 %collective-permute-start.13 = (f32[1,8,256]{1,2,0:T(8,128)S(1)}, f32[1,8,256]{1,2,0:T(8,128)S(1)}, u32[]{:S(2)}, u32[]{:S(2)}) collective-permute-start(f32[1,8,256]{1,2,0:T(8,128)S(1)} %get-tuple-element.40), channel_id=1, source_target_pairs={{0,1},{1,2},{2,3},{3,4},{4,5},{5,6},{6,7},{7,8},{8,9},{9,10},{10,1... | collective-permute-start | bytes 24584 | tf_op jit(solution)/shard_map/ppermute | solution.py:72
  179.1 8.0 %collective-permute-start.14 = (f32[1,8,640]{2,1,0:T(8,128)S(1)}, f32[1,8,640]{2,1,0:T(8,128)S(1)}, u32[]{:S(2)}, u32[]{:S(2)}) collective-permute-start(f32[1,8,640]{2,1,0:T(8,128)S(1)} %get-tuple-element.36), channel_id=1, source_target_pairs={{0,16},{16,32},{32,48},{48,64},{64,80},{80,96},{96,112},{1,17},{17... | collective-permute-start | bytes 61448 | tf_op jit(solution)/shard_map/ppermute | solution.py:80
  185.0 6.9 %collective-permute-start.15 = (f32[1,8,640]{2,1,0:T(8,128)S(1)}, f32[1,8,640]{2,1,0:T(8,128)S(1)}, u32[]{:S(2)}, u32[]{:S(2)}) collective-permute-start(f32[1,8,640]{2,1,0:T(8,128)S(1)} %get-tuple-element.35), channel_id=1, source_target_pairs={{16,0},{32,16},{48,32},{64,48},{80,64},{96,80},{112,96},{17,1},{33... | collective-permute-start | bytes 61448 | tf_op jit(solution)/shard_map/ppermute | solution.py:81
  191.9 0.9 copy-start.3

commit v4 on v3

--- a/solution.py
+++ b/solution.py
@@ -234,28 +234,6 @@
     )(a0_frame, r_frame)
 
 
-def send_dies(outbound, row_count, col_count):
-    received = lax.all_to_all(
-        outbound.reshape(row_count * col_count, CAP, -1),
-        ("row", "col"),
-        split_axis=0,
-        concat_axis=0,
-        tiled=True,
-    )
-    return received.reshape(row_count * col_count * CAP, -1)
-
-
-def return_grads(backward, row_count, col_count):
-    returned = lax.all_to_all(
-        backward.reshape(row_count * col_count, CAP, -1),
-        ("row", "col"),
-        split_axis=0,
-        concat_axis=0,
-        tiled=True,
-    )
-    return returned.reshape(row_count * col_count * CAP, -1)
-
-
 def on_device(init_temp, power, die_owner, die_tile, classes, cond_table, target):
     row_count = lax.axis_size("row")
     col_count = lax.axis_size("col")
@@ -273,15 +251,17 @@
     slot_index = owners * CAP + ranking
     all_slots = jnp.arange(devices_all * CAP, dtype=jnp.int32)
     matched = all_slots[:, None] == slot_index[None, :]
-    send_hot = matched.astype(jnp.float32)
+    slot_die = jnp.sum(jnp.where(matched, ordinal[None, :] + 1, 0), axis=1) - 1
+    slot_die = jnp.where(slot_die < 0, die_count, slot_die).reshape(devices_all, CAP)
     tile_column = jnp.zeros((die_count, LANE), jnp.float32).at[:, 0].set((die_tile + 1).astype(jnp.float32))
-    outbound = jnp.dot(send_hot, jnp.concatenate([power_flat, tile_column], 1), precision=highest)
-    received = send_dies(outbound, row_count, col_count)
-    recv_tiles = received[:, TILE * TILE].astype(jnp.int32) - 1
-    received = received[:, : TILE * TILE]
+    payload = jnp.concatenate([power_flat, tile_column], 1)
+    payload = jnp.concatenate([payload, jnp.zeros((1, payload.shape[1]), payload.dtype)], 0)
+    outbound = jnp.take(payload, slot_die, axis=0)
+    received = lax.all_to_all(outbound, ("row", "col"), split_axis=0, concat_axis=0, tiled=True)
+    recv_tiles = received[:, :, TILE * TILE].astype(jnp.int32) - 1
     tile_range = jnp.arange(tile_rows * tile_cols, dtype=jnp.int32)
-    recv_hot = (tile_range[:, None] == recv_tiles[None, :]).astype(jnp.float32)
-    source_tiles = jnp.dot(recv_hot, received, precision=highest)
+    recv_hot = (tile_range[:, None, None] == recv_tiles[None]).astype(jnp.float32)
+    source_tiles = jnp.einsum("tdc,dcn->tn", recv_hot, received[:, :, : TILE * TILE], precision=highest)
     source = (
         source_tiles.reshape(tile_rows, tile_cols, TILE, TILE)
         .transpose(0, 2, 1, 3)
@@ -299,11 +279,11 @@
         .transpose(0, 2, 1, 3)
         .reshape(tile_rows * tile_cols, TILE * TILE)
     )
-    backward = jnp.dot(recv_hot.T, grad_tiles, precision=highest)
-    returned = return_grads(backward, row_count, col_count)
-    die_grad = (RATE * jnp.dot(send_hot.T, returned, precision=highest)).reshape(
-        die_count, TILE, TILE
-    )
+    grad_tiles = jnp.concatenate([grad_tiles, jnp.zeros((1, grad_tiles.shape[1]), grad_tiles.dtype)], 0)
+    tile_count = tile_rows * tile_cols
+    backward = jnp.take(grad_tiles, jnp.where(recv_tiles < 0, tile_count, recv_tiles), axis=0)
+    returned = lax.all_to_all(backward, ("row", "col"), split_axis=0, concat_axis=0, tiled=True)
+    die_grad = (RATE * returned[owners, ranking]).reshape(die_count, TILE, TILE)
     return (heat_field, adjoint, die_grad)
 
 

time: 306 us -> 317 us (1.036)
  blocking collectives: 63.1 us -> 0 us
  waiting for transfers between devices: 50.1 us -> 99.8 us
  other arithmetic: 8.31 us -> 22.9 us
  starting transfers between devices: 75.1 us -> 87.9 us
  matrix products: 13.4 us -> 3.92 us
  local copies, waits for them, and re-layouts: 37.1 us -> 43.4 us
    all_to_all x1 -> x0, blocking collectives: 63.1 us -> none  [return_grads(): lax.all_to_all(backward.reshape(row_count * col_count, CAP, -1), ('row',...]
    all_to_all x1 -> x2, waiting for transfers between devices: 0.01 us -> 50.6 us  [the longest x1 50.6 us: on_device(): lax.all_to_all(backward, ('row', 'col'), split_axis=0, concat_axis=0, til...]
    gather x0 -> x5, local copies, waits for them, and re-layouts: none -> 22.3 us  [the longest x2 10.1 us: on_device(): outbound = jnp.take(payload, slot_die, axis=0)]
    reshape x4 -> x0, local copies, waits for them, and re-layouts: 20.5 us -> none  [the longest x1 6.25 us: send_dies(): return received.reshape(row_count * col_count * CAP, -1)]
    select_n x0 -> x4, other arithmetic: none -> 15.3 us  [the longest x2 8.19 us: on_device(): jnp.take(grad_tiles, jnp.where(recv_tiles < 0, tile_count, recv_tiles), a...]
    all_to_all x1 -> x2, starting transfers between devices: 11 us -> 23.8 us  [the longest x1 12.7 us: on_device(): lax.all_to_all(backward, ('row', 'col'), split_axis=0, concat_axis=0, til...]
    dot_general x4 -> x1, matrix products: 13.4 us -> 3.92 us  [on_device(): jnp.einsum('tdc,dcn->tn', recv_hot, received[:, :, :TILE * TILE], precisi...]
    slice x0 -> x2, local copies, waits for them, and re-layouts: none -> 3.43 us  [the longest x1 2.52 us: on_device(): received[:, :, :TILE * TILE]]
  transfers between devices with their start and end apart: 17 -> 18, of which waited for: 8 -> 8; matrix products, arithmetic and copies ran while one was open for 7% -> 6% of each run, Pallas kernels for 0% -> 0%
where the time goes in v4:
time: 317 us; the launch traced here: 313 us
  waiting for transfers between devices  99.8 us (31%)
  starting transfers between devices  87.9 us (28%)
  Pallas kernels  53.6 us (17%)
  local copies, waits for them, and re-layouts  43.4 us (14%)
  other arithmetic  22.9 us (7%)
  matrix products  3.92 us (1%)
    all_to_all x1, waiting for transfers between devices, on_device(): lax.all_to_all(backward, ('row', 'col'), split_axis=0, concat_axis=0, til...  50.6 us
    ppermute x4, waiting for transfers between devices, framed(): lax.ppermute(jnp.swapaxes(cells[:, :, :HALO], 1, 2), 'col', [(i + 1, i) f...  39.7 us
    ppermute x4, starting transfers between devices, framed(): lax.ppermute(jnp.swapaxes(cells[:, :, breadth - HALO:], 1, 2), 'col', [(i...  30.8 us
    pallas_call x1, Pallas kernels, run_adjoint(): pl.pallas_call(adjoint_kernel, out_shape=(jax.ShapeDtypeStruct((layers, h...  26.8 us
    pallas_call x1, Pallas kernels, run_forward(): pl.pallas_call(forward_kernel, out_shape=jax.ShapeDtypeStruct((layers, he...  26.8 us
    ppermute x4, starting transfers between devices, framed(): lax.ppermute(band[:, height - HALO:], 'row', [(i, i + 1) for i in range(r...  17.2 us
    all_to_all x1, starting transfers between devices, on_device(): lax.all_to_all(backward, ('row', 'col'), split_axis=0, concat_axis=0, til...  12.7 us
    all_to_all x1, starting transfers between devices, on_device(): lax.all_to_all(outbound, ('row', 'col'), split_axis=0, concat_axis=0, til...  11 us
  transfers between devices with their start and end apart: 18, of which 8 were waited for; matrix products, arithmetic and copies ran while one was open for 6% of the time, Pallas kernels for 0%

profile of v4, /device:TPU:15, one launch (start us, length us, event | category | flops | bytes accessed | tf_op | source)
XLA Modules:
  0.0 312.7 jit_solution(6529796799719625027)
XLA Ops:
  1.3 0.8 convert_reduce_fusion
  3.3 2.1 reshape.135
  6.4 4.1 %gather_fusion = f32[256,4224]{1,0:T(8,128)} fusion(f32[65,4224]{1,0:T(8,128)S(1)} %concatenate.43, s32[1024]{0:T(1024)S(1)} %pad_clamp_fusion.1), kind=kCustom, calls=%fused_computation | custom fusion | bytes 8651776 | tf_op jit(solution)/shard_map/jit(_take)/gather | solution.py:259
  10.5 6.0 %reshape.141 = f32[128,2,4224]{2,1,0:T(2,128)} reshape(f32[256,4224]{1,0:T(8,128)} %gather_fusion) | data formatting | bytes 8650752 | tf_op jit(solution)/shard_map/jit(_take)/gather | solution.py:259
  16.5 7.1 %broadcast_select_fusion = f32[128,2,4224]{2,1,0:T(2,128)} fusion(f32[128,2,4224]{2,1,0:T(2,128)} %reshape.141, pred[128,2]{1,0:T(8,128)(4,1)S(1)} %compare_and_fusion), kind=kLoop, calls=%fused_computation.4 | loop fusion | flops 1081344 | bytes 8651008 | tf_op jit(solution)/shard_map/jit(_take)/select_n | solution.py:259
  23.6 11.0 %all-to-all-start = ((f32[128,2,4224]{2,1,0:T(2,128)}), f32[128,2,4224]{2,1,0:T(2,128)}, u32[]{:S(2)}, u32[]{:S(2)}) async-start(f32[128,2,4224]{2,1,0:T(2,128)} %broadcast_select_fusion), calls=%async_computation | async-start | bytes 8650752 | tf_op jit(solution)/shard_map/all_to_all | solution.py:260
  35.0 2.1 add_sqrt_fusion
  37.3 2.3 collective-permute-start.4
  39.6 6.9 %collective-permute-start.5 = (f32[4,8,256]{1,2,0:T(8,128)S(1)}, f32[4,8,256]{1,2,0:T(8,128)S(1)}, u32[]{:S(2)}, u32[]{:S(2)}) collective-permute-start(f32[4,8,256]{1,2,0:T(8,128)S(1)} %get-tuple-element.32), channel_id=1, source_target_pairs={{0,1},{1,2},{2,3},{3,4},{4,5},{5,6},{6,7},{7,8},{8,9},{9,10},{10,1... | collective-permute-start | bytes 98312 | tf_op jit(solution)/shard_map/ppermute | solution.py:72
  46.7 1.9 collective-permute-start
  48.7 7.3 %collective-permute-start.1 = (f32[4,8,256]{1,2,0:T(8,128)S(1)}, f32[4,8,256]{1,2,0:T(8,128)S(1)}, u32[]{:S(2)}, u32[]{:S(2)}) collective-permute-start(f32[4,8,256]{1,2,0:T(8,128)S(1)} %get-tuple-element.34), channel_id=1, source_target_pairs={{0,1},{1,2},{2,3},{3,4},{4,5},{5,6},{6,7},{7,8},{8,9},{9,10},{10,1... | collective-permute-start | bytes 98312 | tf_op jit(solution)/shard_map/ppermute | solution.py:72
  57.9 33.5 %collective-permute-done.4 = f32[4,8,256]{1,2,0:T(8,128)S(1)} collective-permute-done((f32[4,8,256]{1,2,0:T(8,128)S(1)}, f32[4,8,256]{1,2,0:T(8,128)S(1)}, u32[]{:S(2)}, u32[]{:S(2)}) %collective-permute-start.4) | collective-permute-done | bytes 32800 | tf_op jit(solution)/shard_map/ppermute | solution.py:75
  91.4 5.6 %collective-permute-done = f32[4,8,256]{1,2,0:T(8,128)S(1)} collective-permute-done((f32[4,8,256]{1,2,0:T(8,128)S(1)}, f32[4,8,256]{1,2,0:T(8,128)S(1)}, u32[]{:S(2)}, u32[]{:S(2)}) %collective-permute-start) | collective-permute-done | bytes 32800 | tf_op jit(solution)/shard_map/ppermute | solution.py:75
  97.0 0.8 pad_maximum_fusion.1
  97.8 4.7 %collective-permute-start.6 = (f32[4,8,640]{2,1,0:T(8,128)S(1)}, f32[4,8,640]{2,1,0:T(8,128)S(1)}, u32[]{:S(2)}, u32[]{:S(2)}) collective-permute-start(f32[4,8,640]{2,1,0:T(8,128)S(1)} %get-tuple-element.28), channel_id=1, source_target_pairs={{0,16},{16,32},{32,48},{48,64},{64,80},{80,96},{96,112},{1,17},{17... | collective-permute-start | bytes 245768 | tf_op jit(solution)/shard_map/ppermute | solution.py:80
  102.6 1.9 collective-permute-start.7
  104.5 3.4 %collective-permute-start.2 = (f32[4,8,640]{2,1,0:T(8,128)S(1)}, f32[4,8,640]{2,1,0:T(8,128)S(1)}, u32[]{:S(2)}, u32[]{:S(2)}) collective-permute-start(f32[4,8,640]{2,1,0:T(8,128)S(1)} %get-tuple-element.30), channel_id=1, source_target_pairs={{0,16},{16,32},{32,48},{48,64},{64,80},{80,96},{96,112},{1,17},{17... | collective-permute-start | bytes 245768 | tf_op jit(solution)/shard_map/ppermute | solution.py:80
  107.9 2.1 collective-permute-start.3
  111.0 1.7 constant_dynamic-update-slice_fusion.2
  112.7 0.9 slice.134
  113.6 0.9 copy.41
  114.6 2.5 slice.135
  117.1 3.9 %convolution_bitcast_fusion = f32[32,4096]{1,0:T(8,128)S(1)} fusion(f32[128,2,4096]{2,1,0:T(2,128)S(1)} %slice.135, s32[128,2]{0,1:T(2,128)S(1)} %bitcast.77), kind=kOutput, calls=%fused_computation.3 | convolution fusion | flops 402661376 | bytes 4719616 | tf_op jit(solution)/shard_map/tdc,dcn->tn/dot_general | solution.py:264
  122.5 1.9 collective-permute-start.8
  124.4 7.3 %collective-permute-start.9 = (f32[1,8,256]{1,2,0:T(8,128)S(1)}, f32[1,8,256]{1,2,0:T(8,128)S(1)}, u32[]{:S(2)}, u32[]{:S(2)}) collective-permute-start(f32[1,8,256]{1,2,0:T(8,128)S(1)} %get-tuple-element.42), channel_id=1, source_target_pairs={{0,1},{1,2},{2,3},{3,4},{4,5},{5,6},{6,7},{7,8},{8,9},{9,10},{10,1... | collective-permute-start | bytes 24584 | tf_op jit(solution)/shard_map/ppermute | solution.py:72
  132.4 1.2 collective-permute-done.9
  133.7 3.4 %collective-permute-start.10 = (f32[1,8,640]{2,1,0:T(8,128)S(1)}, f32[1,8,640]{2,1,0:T(8,128)S(1)}, u32[]{:S(2)}, u32[]{:S(2)}) collective-permute-start(f32[1,8,640]{2,1,0:T(8,128)S(1)} %get-tuple-element.38), channel_id=1, source_target_pairs={{0,16},{16,32},{32,48},{48,64},{64,80},{80,96},{96,112},{1,17},{17... | collective-permute-start | bytes 61448 | tf_op jit(solution)/shard_map/ppermute | solution.py:80
  137.7 1.9 collective-permute-start.11
  139.8 2.5 collective-permute-done.11
  142.2 0.9 copy-done.6
  143.1 26.8 %shard_map.94 = f32[4,256,512]{2,1,0:T(8,128)} custom-call(f32[4,288,640]{2,1,0:T(8,128)} %constant_dynamic-update-slice_fusion.f_ref, f32[4,288,640]{2,1,0:T(8,128)} %copy-done, f32[288,640]{1,0:T(8,128)} %bitcast.64), custom_call_target="tpu_custom_call" | custom-call | tf_op jit(solution)/shard_map/pallas_call | solution.py:212
  169.9 1.2 fusion.2
  171.2 1.9 collective-permute-start.12
  173.1 9.4 %collective-permute-start.13 = (f32[1,8,256]{1,2,0:T(8,128)S(1)}, f32[1,8,256]{1,2,0:T(8,128)S(1)}, u32[]{:S(2)}, u32[]{:S(2)}) collective-permute-start(f32[1,8,256]{1,2,0:T(8,128)S(1)} %get-tuple-element.40), channel_id=1, source_target_pairs={{0,1},{1,2},{2,3},{3,4},{4,5},{5,6},{6,7},{7,8},{8,9},{9,10},{10,1... | collective-permute-start | bytes 24584 | tf_op jit(solution)/shard_map/ppermute | solution.py:72
  183.2 1.2 collective-permute-done.13
  184.6 5.7 %collective-permute-start.14 = (f32[1,8,640]{2,1,0:T(8,128)S(1)}, f32[1,8,640]{2,1,0:T(8,128)S(1)}, u32[]{:S(2)}, u32[]{:S(2)}) collective-permute-start(f32[1,8,640]{2,1,0:T(8,128)S(1)} %get-tuple-element.36), channel_id=1, source_target_pairs={{0,16},{16,32},{32,48},{48,64},{64,80},{80,96},{96,112},{1,17},{17... | collective-permute-start | bytes 61448 | tf_op jit(solution)/shard_map/ppermute | solution.py:80
  190.3 2.1 collective-permute-start.15
  192.6 4.6 %collective-permute-done.15 = f32[1,8,640]{2,1,0:T(8,128)S(1)} collective-permute-done((f32[1,8,640]{2,1,0:T(8,128)S(1)}, f32[1,8,640]{2,1,0:T(8,128)S(1)}, u32[]{:S(2)}, u32[]{:S(2)}) %collective-permute-start.15) | collective-permute-done | bytes 20512 | tf_op jit(solution)/shard_map/ppermute | solution.py:81
  197.2 0.9 copy-done.4
  198.1 26.8 %shard_map.95 = (f32[4,256,512]{2,1,0:T(8,128)}, f32[256,512]{1,0:T(8,128)}) custom-call(f32[288,640]{1,0:T(8,128)} %bitcast.63, f32[4,288,640]{2,1,0:T(8,128)} %copy-done), custom_call_target="tpu_custom_call" | custom-call | tf_op jit(solution)/shard_map/pallas_call | solution.py:224
  224.9 1.2 reshape.138
  226.7 3.9 %gather_fusion.1 = f32[256,4096]{1,0:T(8,128)} fusion(f32[33,4096]{1,0:T(8,128)S(1)} %concatenate.48, s32[1024]{0:T(1024)S(1)} %pad_clamp_fusion), kind=kCustom, calls=%fused_computation.1 | custom fusion | bytes 8389632 | tf_op jit(solution)/shard_map/jit(_take)/gather | solution.py:284
  230.6 5.9 %reshape.149 = f32[128,2,4096]{2,1,0:T(2,128)} reshape(f32[256,4096]{1,0:T(8,128)} %gather_fusion.1) | data formatting | bytes 8388608 | tf_op jit(solution)/shard_map/jit(_take)/gather | solution.py:284
  236.4 8.2 %broadcast_select_fusion.1 = f32[128,2,4096]{2,1,0:T(2,128)} fusion(f32[128,2,4096]{2,1,0:T(2,128)} %reshape.149, pred[128,2]{1,0:T(8,128)(4,1)S(1)} %and_bitcast_fusion), kind=kLoop, calls=%fused_computation.6 | loop fusion | flops 1048576 | bytes 8388864 | tf_op jit(solution)/shard_map/jit(_take)/select_n | solution.py:284
  244.6 12.7 %all-to-all-start.1 = ((f32[128,2,4096]{2,1,0:T(2,128)}), f32[128,2,4096]{2,1,0:T(2,128)}, u32[]{:S(2)}, u32[]{:S(2)}) async-start(f32[128,2,4096]{2,1,0:T(2,128)} %broadcast_select_fusion.1), calls=%async_computation.1 | async-start | bytes 8388608 | tf_op jit(solution)/shard_map/all_to_all | solution.py:285
  257.3 50.6 %all-to-all-done.1 = f32[128,2,4096]{2,1,0:T(2,128)} async-done(((f32[128,2,4096]{2,1,0:T(2,128)}), f32[128,2,4096]{2,1,0:T(2,128)}, u32[]{:S(2)}, u32[]{:S(2)}) %all-to-all-start.1) | async-done | bytes 4194336 | tf_op jit(solution)/shard_map/all_to_all | solution.py:285
  307.9 2.5 gather_fusion.2
  310.6 2.2 mul.20
  (90 shorter events, 11.1 us)
Async XLA Ops:
  0.6 4.8 %copy-start.10 = (s32[64]{0:T(128)S(1)}, s32[64]{0:T(128)}, u32[]{:S(2)}) copy-start(s32[64]{0:T(128)} %param.12) | copy-start | bytes 772
  23.6 11.1 %copy-start.8 = (f32[4,8]{1,0:T(4,128)S(1)}, f32[4,8]{1,0:T(4,128)}, u32[]{:S(2)}) copy-start(f32[4,8]{1,0:T(4,128)} %param.14) | copy-start | bytes 388
  23.6 11.4 %copy-start.2 = (s32[4,256,512]{2,1,0:T(8,128)S(1)}, s32[4,256,512]{2,1,0:T(8,128)}, u32[]{:S(2)}) copy-start(s32[4,256,512]{2,1,0:T(8,128)} %param.13) | copy-start | bytes 6291460
  23.6 89.1 %all-to-all-start = ((f32[128,2,4224]{2,1,0:T(2,128)}), f32[128,2,4224]{2,1,0:T(2,128)}, u32[]{:S(2)}, u32[]{:S(2)}) async-start(f32[128,2,4224]{2,1,0:T(2,128)} %broadcast_select_fusion), calls=%async_computation | async-start | bytes 8650752 | tf_op jit(solution)/shard_map/all_to_all | solution.py:260
  35.0 11.5 %copy-start.1 = (f32[4,256,512]{2,1,0:T(8,128)S(1)}, f32[4,256,512]{2,1,0:T(8,128)}, u32[]{:S(2)}) copy-start(f32[4,256,512]{2,1,0:T(8,128)} %param.9) | copy-start | bytes 6291460
  37.3 54.1 %collective-permute-start.4 = (f32[4,8,256]{1,2,0:T(8,128)S(1)}, f32[4,8,256]{1,2,0:T(8,128)S(1)}, u32[]{:S(2)}, u32[]{:S(2)}) collective-permute-start(f32[4,8,256]{1,2,0:T(8,128)S(1)} %get-tuple-element.31), channel_id=1, source_target_pairs={{1,0},{2,1},{3,2},{4,3},{5,4},{6,5},{7,6},{8,7},{9,8},{10,9},{11,1... | collective-permute-start | bytes 98312 | tf_op jit(solution)/shard_map/ppermute | solution.py:75
  39.6 51.8 %collective-permute-start.5 = (f32[4,8,256]{1,2,0:T(8,128)S(1)}, f32[4,8,256]{1,2,0:T(8,128)S(1)}, u32[]{:S(2)}, u32[]{:S(2)}) collective-permute-start(f32[4,8,256]{1,2,0:T(8,128)S(1)} %get-tuple-element.32), channel_id=1, source_target_pairs={{0,1},{1,2},{2,3},{3,4},{4,5},{5,6},{6,7},{7,8},{8,9},{9,10},{10,1... | collective-permute-start | bytes 98312 | tf_op jit(solution)/shard_map/ppermute | solution.py:72
  46.7 50.3 %collective-permute-start = (f32[4,8,256]{1,2,0:T(8,128)S(1)}, f32[4,8,256]{1,2,0:T(8,128)S(1)}, u32[]{:S(2)}, u32[]{:S(2)}) collective-permute-start(f32[4,8,256]{1,2,0:T(8,128)S(1)} %get-tuple-element.33), channel_id=1, source_target_pairs={{1,0},{2,1},{3,2},{4,3},{5,4},{6,5},{7,6},{8,7},{9,8},{10,9},{11,1... | collective-permute-start | bytes 98312 | tf_op jit(solution)/shard_map/ppermute | solution.py:75
  48.7 48.4 %collective-permute-start.1 = (f32[4,8,256]{1,2,0:T(8,128)S(1)}, f32[4,8,256]{1,2,0:T(8,128)S(1)}, u32[]{:S(2)}, u32[]{:S(2)}) collective-permute-start(f32[4,8,256]{1,2,0:T(8,128)S(1)} %get-tuple-element.34), channel_id=1, source_target_pairs={{0,1},{1,2},{2,3},{3,4},{4,5},{5,6},{6,7},{7,8},{8,9},{9,10},{10,1... | collective-permute-start | bytes 98312 | tf_op jit(solution)/shard_map/ppermute | solution.py:72
  97.8 12.2 %collective-permute-start.6 = (f32[4,8,640]{2,1,0:T(8,128)S(1)}, f32[4,8,640]{2,1,0:T(8,128)S(1)}, u32[]{:S(2)}, u32[]{:S(2)}) collective-permute-start(f32[4,8,640]{2,1,0:T(8,128)S(1)} %get-tuple-element.28), channel_id=1, source_target_pairs={{0,16},{16,32},{32,48},{48,64},{64,80},{80,96},{96,112},{1,17},{17... | collective-permute-start | bytes 245768 | tf_op jit(solution)/shard_map/ppermute | solution.py:80
  102.6 7.6 %collective-permute-start.7 = (f32[4,8,640]{2,1,0:T(8,128)S(1)}, f32[4,8,640]{2,1,0:T(8,128)S(1)}, u32[]{:S(2)}, u32[]{:S(2)}) collective-permute-start(f32[4,8,640]{2,1,0:T(8,128)S(1)} %get-tuple-element.27), channel_id=1, source_target_pairs={{16,0},{32,16},{48,32},{64,48},{80,64},{96,80},{112,96},{17,1},{33... | collective-permute-start | bytes 245768 | tf_op jit(solution)/shard_map/ppermute | solution.py:81
  104.5 5.7 %collective-permute-start.2 = (f32[4,8,640]{2,1,0:T(8,128)S(1)}, f32[4,8,640]{2,1,0:T(8,128)S(1)}, u32[]{:S(2)}, u32[]{:S(2)}) collective-permute-start(f32[4,8,640]{2,1,0:T(8,128)S(1)} %get-tuple-element.30), channel_id=1, source_target_pairs={{0,16},{16,32},{32,48},{48,64},{64,80},{80,96},{96,112},{1,17},{17... | collective-permute-start | bytes 245768 | tf_op jit(solution)/shard_map/ppermute | solution.py:80
  107.9 23.8 %collective-permute-start.3 = (f32[4,8,640]{2,1,0:T(8,128)S(1)}, f32[4,8,640]{2,1,0:T(8,128)S(1)}, u32[]{:S(2)}, u32[]{:S(2)}) collective-permute-start(f32[4,8,640]{2,1,0:T(8,128)S(1)} %get-tuple-element.29), channel_id=1, source_target_pairs={{16,0},{32,16},{48,32},{64,48},{80,64},{96,80},{112,96},{17,1},{33... | collective-permute-start | bytes 245768 | tf_op jit(solution)/shard_map/ppermute | solution.py:81
  110.3 2.5 copy-start
  121.5 18.2 %copy-start.5 = (f32[1,288,640]{2,1,0:T(8,128)S(1)}, f32[1,288,640]{2,1,0:T(8,128)}, u32[]{:S(2)}) copy-start(f32[1,288,640]{2,1,0:T(8,128)} %constant_dynamic-update-slice_fusion.14) | copy-start | bytes 2211844
  122.5 9.9 %collective-permute-start.8 = (f32[1,8,256]{1,2,0:T(8,128)S(1)}, f32[1,8,256]{1,2,0:T(8,128)S(1)}, u32[]{:S(2)}, u32[]{:S(2)}) collective-permute-start(f32[1,8,256]{1,2,0:T(8,128)S(1)} %get-tuple-element.41), channel_id=1, source_target_pairs={{1,0},{2,1},{3,2},{4,3},{5,4},{6,5},{7,6},{8,7},{9,8},{10,9},{11,1... | collective-permute-start | bytes 24584 | tf_op jit(solution)/shard_map/ppermute | solution.py:75
  124.4 9.2 %collective-permute-start.9 = (f32[1,8,256]{1,2,0:T(8,128)S(1)}, f32[1,8,256]{1,2,0:T(8,128)S(1)}, u32[]{:S(2)}, u32[]{:S(2)}) collective-permute-start(f32[1,8,256]{1,2,0:T(8,128)S(1)} %get-tuple-element.42), channel_id=1, source_target_pairs={{0,1},{1,2},{2,3},{3,4},{4,5},{5,6},{6,7},{7,8},{8,9},{9,10},{10,1... | collective-permute-start | bytes 24584 | tf_op jit(solution)/shard_map/ppermute | solution.py:72
  133.7 5.9 %collective-permute-start.10 = (f32[1,8,640]{2,1,0:T(8,128)S(1)}, f32[1,8,640]{2,1,0:T(8,128)S(1)}, u32[]{:S(2)}, u32[]{:S(2)}) collective-permute-start(f32[1,8,640]{2,1,0:T(8,128)S(1)} %get-tuple-element.38), channel_id=1, source_target_pairs={{0,16},{16,32},{32,48},{48,64},{64,80},{80,96},{96,112},{1,17},{17... | collective-permute-start | bytes 61448 | tf_op jit(solution)/shard_map/ppermute | solution.py:80
  137.7 4.5 %collective-permute-start.11 = (f32[1,8,640]{2,1,0:T(8,128)S(1)}, f32[1,8,640]{2,1,0:T(8,128)S(1)}, u32[]{:S(2)}, u32[]{:S(2)}) collective-permute-start(f32[1,8,640]{2,1,0:T(8,128)S(1)} %get-tuple-element.37), channel_id=1, source_target_pairs={{16,0},{32,16},{48,32},{64,48},{80,64},{96,80},{112,96},{17,1},{33... | collective-permute-start | bytes 61448 | tf_op jit(solution)/shard_map/ppermute | solution.py:81
  142.2 0.9 copy-start.6
  143.1 26.8 %copy-start.7 = (f32[256,512]{1,0:T(8,128)S(1)}, f32[256,512]{1,0:T(8,128)}, u32[]{:S(2)}) copy-start(f32[256,512]{1,0:T(8,128)} %param.15) | copy-start | bytes 1572868
  169.9 22.6 %copy-start.3 = (f32[1,288,640]{2,1,0:T(8,128)S(1)}, f32[1,288,640]{2,1,0:T(8,128)}, u32[]{:S(2)}) copy-start(f32[1,288,640]{2,1,0:T(8,128)} %constant_dynamic-update-slice_fusion.19) | copy-start | bytes 2211844
  171.2 12.0 %collective-permute-start.12 = (f32[1,8,256]{1,2,0:T(8,128)S(1)}, f32[1,8,256]{1,2,0:T(8,128)S(1)}, u32[]{:S(2)}, u32[]{:S(2)}) collective-permute-start(f32[1,8,256]{1,2,0:T(8,128)S(1)} %get-tuple-element.39), channel_id=1, source_target_pairs={{1,0},{2,1},{3,2},{4,3},{5,4},{6,5},{7,6},{8,7},{9,8},{10,9},{11,1... | collective-permute-start | bytes 24584 | tf_op jit(solution)/shard_map/ppermute | solution.py:75
  173.1 11.3 %collective-permute-start.13 = (f32[1,8,256]{1,2,0:T(8,128)S(1)}, f32[1,8,256]{1,2,0:T(8,128)S(1)}, u32[]{:S(2)}, u32[]{:S(2)}) collective-permute-start(f32[1,8,256]{1,2,0:T(8,128)S(1)} %get-tuple-element.40), channel_id=1, source_target_pairs={{0,1},{1,2},{2,3},{3,4},{4,5},{5,6},{6,7},{7,8},{8,9},{9,10},{10,1... | collective-permute-start | bytes 24584 | tf_op jit(solution)/shard_map/ppermute | solution.py:72
  184.6 7.9 %collective-permute-start.14 = (f32[1,8,640]{2,1,0:T(8,128)S(1)}, f32[1,8,640]{2,1,0:T(8,128)S(1)}, u32[]{:S(2)}, u32[]{:S(2)}) collective-permute-start(f32[1,8,640]{2,1,0:T(8,128)S(1)} %get-tuple-element.36), channel_id=1, source_target_pairs={{0,16},{16,32},{32,48},{48,64},{64,80},{80,96},{96,112},{1,17},{17... | collective-permute-start | bytes 61448 | tf_op jit(solution)/shard_map/ppermute | solution.py:80
  190.3 6.9 %collective-permute-start.15 = (f32[1,8,640]{2,1,0:T(8,128)S(1)}, f32[1,8,640]{2,1,0:T(8,128)S(1)}, u32[]{:S(2)}, u32[]{:S(2)}) collective-permute-start(f32[1,8,640]{2,1,0:T(8,128)S(1)} %get-tuple-element.35), channel_id=1, source_target_pairs={{16,0},{32,16},{48,32},{64,48},{80,64},{96,80},{112,96},{17,1},{33... | collective-permute-start | bytes 61448 | tf_op jit(solution)/shard_map/ppermute | solution.py:81
  197.2 0.9 copy-start.4
  244.6 12.7 %copy-start.9 = (s32[64,1]{0,1:T(1,128)S(1)}, s32[64,1]{0,1:T(1,128)}, u32[]{:S(2)}) copy-start(s32[64,1]{0,1:T(1,128)} %param.11) | copy-start | bytes 772
  244.6 63.4 %all-to-all-start.1 = ((f32[128,2,4096]{2,1,0:T(2,128)}), f32[128,2,4096]{2,1,0:T(2,128)}, u32[]{:S(2)}, u32[]{:S(2)}) async-start(f32[128,2,4096]{2,1,0:T(2,128)} %broadcast_select_fusion.1), calls=%async_computation.1 | async-start | bytes 8388608 | tf_op jit(solution)/shard_map/all_to_all | solution.py:285

commit v5 on v3

--- a/solution.py
+++ b/solution.py
@@ -59,7 +59,7 @@
     return middle + RATE * inflow
 
 
-HALO = 8
+HALO = 16
 SLACK = 8
 CHUNK = 16
 LANE = 128
@@ -154,8 +154,9 @@
     chunk_loop(height // CHUNK, body)
 
 
-def forward_kernel(f_ref, r_ref, s_ref, out_ref, cu, cd, cl, cr, cv, a, b):
+def solve_kernel(f_ref, r_ref, s_ref, t_ref, out_ref, grad_ref, gsum_ref, cu, cd, cl, cr, cv, a, b):
     layers, height, breadth = out_ref.shape
+    frame_rows = a.shape[1]
     clear_slack(a)
     clear_slack(b)
     conductances(r_ref, cu, cd, cl, cr, cv)
@@ -168,16 +169,17 @@
     def put(rows, value):
         out_ref[:, rows, :] = value
 
-    copy_center(lambda rows, width: src[:, rows, 0:width], put, height, breadth)
-
-
-def adjoint_kernel(a0_ref, r_ref, grad_ref, gsum_ref, cu, cd, cl, cr, cv, a, b):
-    layers, height, breadth = grad_ref.shape
-    a[...] = jnp.zeros(a.shape, a.dtype)
-    clear_slack(b)
-    a[0] = a0_ref[...]
-    conductances(r_ref, cu, cd, cl, cr, cv)
-    src = a
+    copy_center(lambda rows, width, v=src: v[:, rows, 0:width], put, height, breadth)
+    final = src
+    start = b if final is a else a
+    start[1:] = jnp.zeros((layers - 1,) + start.shape[1:], start.dtype)
+
+    def seed(c):
+        rows = pl.ds(pl.multiple_of(c * CHUNK, 8), CHUNK)
+        start[0, rows, :] = final[0, rows, :] - t_ref[rows, :]
+
+    chunk_loop(frame_rows // CHUNK, seed)
+    src = start
     for index in range(STEPS):
         view = src
 
@@ -188,14 +190,14 @@
                 gsum_ref[rows, :] = gsum_ref[rows, :] + value
 
         copy_center(lambda rows, width, v=view: v[0, rows, 0:width], put_sum, height, breadth)
-        dst = b if index % 2 == 0 else a
+        dst = final if src is start else start
         explicit_step(src, dst, cu, cd, cl, cr, cv, None)
         src = dst
 
-    def put(rows, value):
+    def put_grad(rows, value):
         grad_ref[:, rows, :] = value
 
-    copy_center(lambda rows, width: src[:, rows, 0:width], put, height, breadth)
+    copy_center(lambda rows, width, v=src: v[:, rows, 0:width], put_grad, height, breadth)
 
 
 def stencil_scratch(layers, frame_rows, frame_cols):
@@ -207,31 +209,17 @@
     return [pl.BlockSpec(memory_space=pltpu.VMEM) for _ in range(count)]
 
 
-def run_forward(f_frame, r_frame, s_frame, height, breadth):
+def run_solve(f_frame, r_frame, s_frame, t_frame, height, breadth):
     layers, frame_rows, frame_cols = f_frame.shape
+    field = jax.ShapeDtypeStruct((layers, height, breadth), jnp.float32)
     return pl.pallas_call(
-        forward_kernel,
-        out_shape=jax.ShapeDtypeStruct((layers, height, breadth), jnp.float32),
-        in_specs=vmem_specs(3),
-        out_specs=vmem_specs(1)[0],
+        solve_kernel,
+        out_shape=(field, field, jax.ShapeDtypeStruct((height, breadth), jnp.float32)),
+        in_specs=vmem_specs(4),
+        out_specs=tuple(vmem_specs(3)),
         scratch_shapes=stencil_scratch(layers, frame_rows, frame_cols),
-        compiler_params=pltpu.CompilerParams(vmem_limit_bytes=56 * 1024 * 1024),
-    )(f_frame, r_frame, s_frame)
-
-
-def run_adjoint(a0_frame, r_frame, height, breadth):
-    layers, frame_rows, frame_cols = r_frame.shape
-    return pl.pallas_call(
-        adjoint_kernel,
-        out_shape=(
-            jax.ShapeDtypeStruct((layers, height, breadth), jnp.float32),
-            jax.ShapeDtypeStruct((height, breadth), jnp.float32),
-        ),
-        in_specs=vmem_specs(2),
-        out_specs=tuple(vmem_specs(2)),
-        scratch_shapes=stencil_scratch(layers, frame_rows, frame_cols),
-        compiler_params=pltpu.CompilerParams(vmem_limit_bytes=56 * 1024 * 1024),
-    )(a0_frame, r_frame)
+        compiler_params=pltpu.CompilerParams(vmem_limit_bytes=60 * 1024 * 1024),
+    )(f_frame, r_frame, s_frame, t_frame)
 
 
 def send_dies(outbound, row_count, col_count):
@@ -291,9 +279,8 @@
     r_frame = framed(root_cond)
     s_frame = framed(source[None])[0]
     f_frame = framed(init_temp)
-    heat_field = run_forward(f_frame, r_frame, s_frame, height, breadth)
-    a0_frame = framed((heat_field[0] - target)[None])[0]
-    adjoint, grad_sum = run_adjoint(a0_frame, r_frame, height, breadth)
+    t_frame = framed(target[None])[0]
+    heat_field, adjoint, grad_sum = run_solve(f_frame, r_frame, s_frame, t_frame, height, breadth)
     grad_tiles = (
         grad_sum.reshape(tile_rows, TILE, tile_cols, TILE)
         .transpose(0, 2, 1, 3)

time: 306 us -> 292 us (0.954)
  waiting for transfers between devices: 50.1 us -> 40.1 us
  starting transfers between devices: 75.1 us -> 67.5 us
  blocking collectives: 63.1 us -> 67.4 us
    ppermute x4, starting transfers between devices: 30.8 us -> 23.3 us  [framed(): lax.ppermute(jnp.swapaxes(cells[:, :, breadth - HALO:], 1, 2), 'col', [(i...]
    ppermute x4, waiting for transfers between devices: 40.5 us -> 35.6 us  [framed(): lax.ppermute(jnp.swapaxes(cells[:, :, :HALO], 1, 2), 'col', [(i + 1, i) f...]
    ppermute x4, waiting for transfers between devices: 7.1 us -> 2.62 us  [framed(): lax.ppermute(band[:, :HALO], 'row', [(i + 1, i) for i in range(rows - 1)])]
    all_to_all x1, blocking collectives: 63.1 us -> 67.4 us  [return_grads(): lax.all_to_all(backward.reshape(row_count * col_count, CAP, -1), ('row',...]
    ppermute x4, starting transfers between devices: 17.2 us -> 13.3 us  [framed(): lax.ppermute(band[:, height - HALO:], 'row', [(i, i + 1) for i in range(r...]
    ppermute x4, starting transfers between devices: 8.07 us -> 11.7 us  [framed(): lax.ppermute(band[:, :HALO], 'row', [(i + 1, i) for i in range(rows - 1)])]
    pallas_call x2 -> x1, Pallas kernels: 53.6 us -> 52.2 us  [run_solve(): pl.pallas_call(solve_kernel, out_shape=(field, field, jax.ShapeDtypeStruc...]
    unnamed x33 -> x35, local copies, waits for them, and re-layouts: 6.42 us -> 6.09 us
  transfers between devices with their start and end apart: 17 -> 17, of which waited for: 8 -> 6; matrix products, arithmetic and copies ran while one was open for 7% -> 8% of each run, Pallas kernels for 0% -> 0%
where the time goes in v5:
time: 292 us; the launch traced here: 287 us
  starting transfers between devices  67.5 us (23%)
  blocking collectives  67.4 us (23%)
  Pallas kernels  52.2 us (18%)
  waiting for transfers between devices  40.1 us (14%)
  local copies, waits for them, and re-layouts  37.4 us (13%)
  matrix products  13.4 us (5%)
  other arithmetic  7.91 us (3%)
    all_to_all x1, blocking collectives, return_grads(): lax.all_to_all(backward.reshape(row_count * col_count, CAP, -1), ('row',...  67.4 us
    pallas_call x1, Pallas kernels, run_solve(): pl.pallas_call(solve_kernel, out_shape=(field, field, jax.ShapeDtypeStruc...  52.2 us
    ppermute x4, waiting for transfers between devices, framed(): lax.ppermute(jnp.swapaxes(cells[:, :, :HALO], 1, 2), 'col', [(i + 1, i) f...  35.6 us
    ppermute x4, starting transfers between devices, framed(): lax.ppermute(jnp.swapaxes(cells[:, :, breadth - HALO:], 1, 2), 'col', [(i...  23.3 us
    ppermute x4, starting transfers between devices, framed(): lax.ppermute(band[:, height - HALO:], 'row', [(i, i + 1) for i in range(r...  13.3 us
    ppermute x4, starting transfers between devices, framed(): lax.ppermute(band[:, :HALO], 'row', [(i + 1, i) for i in range(rows - 1)])  11.7 us
    all_to_all x1, starting transfers between devices, send_dies(): lax.all_to_all(outbound.reshape(row_count * col_count, CAP, -1), ('row',...  11 us
    ppermute x4, starting transfers between devices, framed(): lax.ppermute(jnp.swapaxes(cells[:, :, :HALO], 1, 2), 'col', [(i + 1, i) f...  8.18 us
  transfers between devices with their start and end apart: 17, of which 6 were waited for; matrix products, arithmetic and copies ran while one was open for 8% of the time, Pallas kernels for 0%

profile of v5, /device:TPU:15, one launch (start us, length us, event | category | flops | bytes accessed | tf_op | source)
XLA Modules:
  0.0 287.1 jit_solution(539028785908563469)
XLA Ops:
  1.3 0.8 convert_reduce_fusion
  2.1 0.7 multiply_add_fusion
  2.8 2.1 reshape.110
  4.9 0.7 fusion.15
  5.7 3.8 %fusion.2 = f32[256,4224]{1,0:T(8,128)} fusion(f32[64,1]{1,0:T(8,128)S(1)} %copy.34, f32[64,4096]{1,0:T(8,128)S(1)} %reshape.110, s32[64]{0:T(128)S(1)} %multiply_add_fusion), kind=kOutput, calls=%fused_computation.7 | convolution fusion | flops 831299584 | bytes 5374464 | tf_op jit(solution)/shard_map/dot_general | solution.py:266
  9.5 6.0 %reshape.112 = f32[128,2,4224]{2,1,0:T(2,128)} reshape(f32[256,4224]{1,0:T(8,128)} %fusion.2) | data formatting | bytes 8650752 | tf_op jit(solution)/shard_map/reshape | solution.py:227
  15.5 11.0 %all-to-all-start = ((f32[128,2,4224]{2,1,0:T(2,128)}), f32[128,2,4224]{2,1,0:T(2,128)}, u32[]{:S(2)}, u32[]{:S(2)}) async-start(f32[128,2,4224]{2,1,0:T(2,128)} %reshape.112), calls=%async_computation | async-start | bytes 8650752 | tf_op jit(solution)/shard_map/all_to_all | solution.py:226
  26.9 2.1 add_sqrt_fusion
  29.2 2.3 collective-permute-start.4
  31.5 6.9 %collective-permute-start.5 = (f32[4,16,256]{1,2,0:T(8,128)S(1)}, f32[4,16,256]{1,2,0:T(8,128)S(1)}, u32[]{:S(2)}, u32[]{:S(2)}) collective-permute-start(f32[4,16,256]{1,2,0:T(8,128)S(1)} %get-tuple-element.34), channel_id=1, source_target_pairs={{0,1},{1,2},{2,3},{3,4},{4,5},{5,6},{6,7},{7,8},{8,9},{9,10},{10,1... | collective-permute-start | bytes 196616 | tf_op jit(solution)/shard_map/ppermute | solution.py:72
  38.6 1.9 collective-permute-start
  40.5 7.3 %collective-permute-start.1 = (f32[4,16,256]{1,2,0:T(8,128)S(1)}, f32[4,16,256]{1,2,0:T(8,128)S(1)}, u32[]{:S(2)}, u32[]{:S(2)}) collective-permute-start(f32[4,16,256]{1,2,0:T(8,128)S(1)} %get-tuple-element.36), channel_id=1, source_target_pairs={{0,1},{1,2},{2,3},{3,4},{4,5},{5,6},{6,7},{7,8},{8,9},{9,10},{10,1... | collective-permute-start | bytes 196616 | tf_op jit(solution)/shard_map/ppermute | solution.py:72
  47.8 0.8 slice_bitcast_fusion.5
  48.5 1.9 collective-permute-start.12
  51.2 0.7 constant_dynamic-update-slice_fusion.4
  51.8 31.4 %collective-permute-done.4 = f32[4,16,256]{1,2,0:T(8,128)S(1)} collective-permute-done((f32[4,16,256]{1,2,0:T(8,128)S(1)}, f32[4,16,256]{1,2,0:T(8,128)S(1)}, u32[]{:S(2)}, u32[]{:S(2)}) %collective-permute-start.4) | collective-permute-done | bytes 65568 | tf_op jit(solution)/shard_map/ppermute | solution.py:75
  83.2 1.9 collective-permute-start.13
  85.2 3.7 %collective-permute-done = f32[4,16,256]{1,2,0:T(8,128)S(1)} collective-permute-done((f32[4,16,256]{1,2,0:T(8,128)S(1)}, f32[4,16,256]{1,2,0:T(8,128)S(1)}, u32[]{:S(2)}, u32[]{:S(2)}) %collective-permute-start) | collective-permute-done | bytes 65568 | tf_op jit(solution)/shard_map/ppermute | solution.py:75
  88.9 0.8 pad_maximum_fusion.1
  89.7 4.7 %collective-permute-start.6 = (f32[4,16,640]{2,1,0:T(8,128)S(1)}, f32[4,16,640]{2,1,0:T(8,128)S(1)}, u32[]{:S(2)}, u32[]{:S(2)}) collective-permute-start(f32[4,16,640]{2,1,0:T(8,128)S(1)} %get-tuple-element.30), channel_id=1, source_target_pairs={{0,16},{16,32},{32,48},{48,64},{64,80},{80,96},{96,112},{1,17},{17... | collective-permute-start | bytes 491528 | tf_op jit(solution)/shard_map/ppermute | solution.py:80
  94.4 3.2 %collective-permute-start.7 = (f32[4,16,640]{2,1,0:T(8,128)S(1)}, f32[4,16,640]{2,1,0:T(8,128)S(1)}, u32[]{:S(2)}, u32[]{:S(2)}) collective-permute-start(f32[4,16,640]{2,1,0:T(8,128)S(1)} %get-tuple-element.29), channel_id=1, source_target_pairs={{16,0},{32,16},{48,32},{64,48},{80,64},{96,80},{112,96},{17,1},{33... | collective-permute-start | bytes 491528 | tf_op jit(solution)/shard_map/ppermute | solution.py:81
  97.7 2.0 collective-permute-start.2
  99.8 3.4 %collective-permute-start.3 = (f32[4,16,640]{2,1,0:T(8,128)S(1)}, f32[4,16,640]{2,1,0:T(8,128)S(1)}, u32[]{:S(2)}, u32[]{:S(2)}) collective-permute-start(f32[4,16,640]{2,1,0:T(8,128)S(1)} %get-tuple-element.31), channel_id=1, source_target_pairs={{16,0},{32,16},{48,32},{64,48},{80,64},{96,80},{112,96},{17,1},{33... | collective-permute-start | bytes 491528 | tf_op jit(solution)/shard_map/ppermute | solution.py:81
  104.1 1.1 constant_dynamic-update-slice_fusion.3
  105.2 1.7 constant_dynamic-update-slice_fusion.2
  106.9 0.7 constant_dynamic-update-slice_fusion.1
  107.6 0.7 constant_dynamic-update-slice_fusion.f_ref
  108.2 6.2 %reshape.113 = f32[256,4224]{1,0:T(8,128)} reshape(f32[128,2,4224]{2,1,0:T(2,128)} %all-to-all-done) | data formatting | bytes 8650752 | tf_op jit(solution)/shard_map/reshape | solution.py:233
  114.5 1.0 fusion.8
  115.5 3.8 %fusion = f32[32,4096]{1,0:T(8,128)S(1)} fusion(f32[256,4224]{1,0:T(8,128)} %reshape.113, s32[256]{0:T(256)S(1)} %fusion.8), kind=kOutput, calls=%fused_computation.1 | convolution fusion | flops 402661376 | bytes 4719616 | tf_op jit(solution)/shard_map/dot_general | solution.py:272
  120.7 2.1 collective-permute-start.8
  122.8 7.3 %collective-permute-start.9 = (f32[1,16,256]{1,2,0:T(8,128)S(1)}, f32[1,16,256]{1,2,0:T(8,128)S(1)}, u32[]{:S(2)}, u32[]{:S(2)}) collective-permute-start(f32[1,16,256]{1,2,0:T(8,128)S(1)} %get-tuple-element.44), channel_id=1, source_target_pairs={{0,1},{1,2},{2,3},{3,4},{4,5},{5,6},{6,7},{7,8},{8,9},{9,10},{10,1... | collective-permute-start | bytes 49160 | tf_op jit(solution)/shard_map/ppermute | solution.py:72
  130.8 1.2 collective-permute-done.9
  132.0 1.1 pad_maximum_fusion.3
  133.1 2.2 collective-permute-start.14
  135.4 3.1 %collective-permute-start.15 = (f32[1,16,640]{2,1,0:T(8,128)S(1)}, f32[1,16,640]{2,1,0:T(8,128)S(1)}, u32[]{:S(2)}, u32[]{:S(2)}) collective-permute-start(f32[1,16,640]{2,1,0:T(8,128)S(1)} %get-tuple-element.37), channel_id=1, source_target_pairs={{16,0},{32,16},{48,32},{64,48},{80,64},{96,80},{112,96},{17,1},{33... | collective-permute-start | bytes 122888 | tf_op jit(solution)/shard_map/ppermute | solution.py:81
  138.5 4.3 %collective-permute-start.10 = (f32[1,16,640]{2,1,0:T(8,128)S(1)}, f32[1,16,640]{2,1,0:T(8,128)S(1)}, u32[]{:S(2)}, u32[]{:S(2)}) collective-permute-start(f32[1,16,640]{2,1,0:T(8,128)S(1)} %get-tuple-element.40), channel_id=1, source_target_pairs={{0,16},{16,32},{32,48},{48,64},{64,80},{80,96},{96,112},{1,17},{17... | collective-permute-start | bytes 122888 | tf_op jit(solution)/shard_map/ppermute | solution.py:80
  142.8 1.9 collective-permute-start.11
  144.9 2.6 collective-permute-done.11
  147.6 0.9 copy-done.4
  148.4 52.2 %shard_map.94 = (f32[4,256,512]{2,1,0:T(8,128)}, f32[4,256,512]{2,1,0:T(8,128)}, f32[256,512]{1,0:T(8,128)}) custom-call(f32[4,304,640]{2,1,0:T(8,128)} %constant_dynamic-update-slice_fusion.f_ref, f32[4,304,640]{2,1,0:T(8,128)} %copy-done.1, f32[304,640]{1,0:T(8,128)} %bitcast.45, f32[304,640]{1,0:T(8,128)} %bitcast.46), custom_call_target="tpu_custom_call" | custom-call | tf_op jit(solution)/shard_map/pallas_call | solution.py:215
  200.6 1.2 reshape.115
  202.4 1.8 fusion.9
  204.2 3.2 %copy.33 = f32[128,2,4096]{2,1,0:T(2,128)S(1)} copy(f32[128,2,4096]{2,0,1:T(8,128)S(1)} %fusion.9) | data formatting | bytes 8388608 | tf_op jit(solution)/shard_map/dot_general | solution.py:289
  207.5 67.4 %all_to_all.10 = f32[128,2,4096]{2,1,0:T(2,128)} all-to-all(f32[128,2,4096]{2,1,0:T(2,128)S(1)} %copy.33), channel_id=1, replica_groups=mesh['row'=8,'col'=16] {'row','col'}, dimensions={0} | all-to-all | bytes 8388608 | tf_op jit(solution)/shard_map/all_to_all | solution.py:237
  274.9 6.1 %reshape.117 = f32[256,4096]{1,0:T(8,128)} reshape(f32[128,2,4096]{2,1,0:T(2,128)} %all_to_all.10) | data formatting | bytes 8388608 | tf_op jit(solution)/shard_map/reshape | solution.py:244
  281.0 3.9 %convolution_multiply_fusion = f32[64,4096]{1,0:T(8,128)S(1)} fusion(f32[256,4096]{1,0:T(8,128)} %reshape.117, s32[64]{0:T(128)S(1)} %multiply_add_fusion), kind=kOutput, calls=%fused_computation | convolution fusion | flops 805584896 | bytes 5243136 | tf_op jit(solution)/shard_map/dot_general | solution.py:291
  284.9 2.2 reshape.118
  (64 shorter events, 5.8 us)
Async XLA Ops:
  0.6 4.3 %copy-start.8 = (s32[64]{0:T(128)S(1)}, s32[64]{0:T(128)}, u32[]{:S(2)}) copy-start(s32[64]{0:T(128)} %param.12) | copy-start | bytes 772
  15.5 11.1 %copy-start.7 = (f32[4,8]{1,0:T(4,128)S(1)}, f32[4,8]{1,0:T(4,128)}, u32[]{:S(2)}) copy-start(f32[4,8]{1,0:T(4,128)} %param.14) | copy-start | bytes 388
  15.5 11.4 %copy-start.2 = (s32[4,256,512]{2,1,0:T(8,128)S(1)}, s32[4,256,512]{2,1,0:T(8,128)}, u32[]{:S(2)}) copy-start(s32[4,256,512]{2,1,0:T(8,128)} %param.13) | copy-start | bytes 6291460
  15.5 92.8 %all-to-all-start = ((f32[128,2,4224]{2,1,0:T(2,128)}), f32[128,2,4224]{2,1,0:T(2,128)}, u32[]{:S(2)}, u32[]{:S(2)}) async-start(f32[128,2,4224]{2,1,0:T(2,128)} %reshape.112), calls=%async_computation | async-start | bytes 8650752 | tf_op jit(solution)/shard_map/all_to_all | solution.py:226
  26.8 11.5 %copy-start = (f32[4,256,512]{2,1,0:T(8,128)S(1)}, f32[4,256,512]{2,1,0:T(8,128)}, u32[]{:S(2)}) copy-start(f32[4,256,512]{2,1,0:T(8,128)} %param.9) | copy-start | bytes 6291460
  29.0 18.8 %copy-start.3 = (f32[256,512]{1,0:T(8,128)S(1)}, f32[256,512]{1,0:T(8,128)}, u32[]{:S(2)}) copy-start(f32[256,512]{1,0:T(8,128)} %param.15) | copy-start | bytes 1572868
  29.2 54.1 %collective-permute-start.4 = (f32[4,16,256]{1,2,0:T(8,128)S(1)}, f32[4,16,256]{1,2,0:T(8,128)S(1)}, u32[]{:S(2)}, u32[]{:S(2)}) collective-permute-start(f32[4,16,256]{1,2,0:T(8,128)S(1)} %get-tuple-element.33), channel_id=1, source_target_pairs={{1,0},{2,1},{3,2},{4,3},{5,4},{6,5},{7,6},{8,7},{9,8},{10,9},{11,1... | collective-permute-start | bytes 196616 | tf_op jit(solution)/shard_map/ppermute | solution.py:75
  31.5 53.7 %collective-permute-start.5 = (f32[4,16,256]{1,2,0:T(8,128)S(1)}, f32[4,16,256]{1,2,0:T(8,128)S(1)}, u32[]{:S(2)}, u32[]{:S(2)}) collective-permute-start(f32[4,16,256]{1,2,0:T(8,128)S(1)} %get-tuple-element.34), channel_id=1, source_target_pairs={{0,1},{1,2},{2,3},{3,4},{4,5},{5,6},{6,7},{7,8},{8,9},{9,10},{10,1... | collective-permute-start | bytes 196616 | tf_op jit(solution)/shard_map/ppermute | solution.py:72
  38.6 50.3 %collective-permute-start = (f32[4,16,256]{1,2,0:T(8,128)S(1)}, f32[4,16,256]{1,2,0:T(8,128)S(1)}, u32[]{:S(2)}, u32[]{:S(2)}) collective-permute-start(f32[4,16,256]{1,2,0:T(8,128)S(1)} %get-tuple-element.35), channel_id=1, source_target_pairs={{1,0},{2,1},{3,2},{4,3},{5,4},{6,5},{7,6},{8,7},{9,8},{10,9},{11,1... | collective-permute-start | bytes 196616 | tf_op jit(solution)/shard_map/ppermute | solution.py:75
  40.5 48.4 %collective-permute-start.1 = (f32[4,16,256]{1,2,0:T(8,128)S(1)}, f32[4,16,256]{1,2,0:T(8,128)S(1)}, u32[]{:S(2)}, u32[]{:S(2)}) collective-permute-start(f32[4,16,256]{1,2,0:T(8,128)S(1)} %get-tuple-element.36), channel_id=1, source_target_pairs={{0,1},{1,2},{2,3},{3,4},{4,5},{5,6},{6,7},{7,8},{8,9},{9,10},{10,1... | collective-permute-start | bytes 196616 | tf_op jit(solution)/shard_map/ppermute | solution.py:72
  48.5 81.7 %collective-permute-start.12 = (f32[1,16,256]{1,2,0:T(8,128)}, f32[1,16,256]{1,2,0:T(8,128)}, u32[]{:S(2)}, u32[]{:S(2)}) collective-permute-start(f32[1,16,256]{1,2,0:T(8,128)} %get-tuple-element.41), channel_id=1, source_target_pairs={{1,0},{2,1},{3,2},{4,3},{5,4},{6,5},{7,6},{8,7},{9,8},{10,9},{11,1... | collective-permute-start | bytes 49160 | tf_op jit(solution)/shard_map/ppermute | solution.py:75
  83.2 47.0 %collective-permute-start.13 = (f32[1,16,256]{1,2,0:T(8,128)}, f32[1,16,256]{1,2,0:T(8,128)}, u32[]{:S(2)}, u32[]{:S(2)}) collective-permute-start(f32[1,16,256]{1,2,0:T(8,128)} %get-tuple-element.42), channel_id=1, source_target_pairs={{0,1},{1,2},{2,3},{3,4},{4,5},{5,6},{6,7},{7,8},{8,9},{9,10},{10,1... | collective-permute-start | bytes 49160 | tf_op jit(solution)/shard_map/ppermute | solution.py:72
  89.7 10.1 %collective-permute-start.6 = (f32[4,16,640]{2,1,0:T(8,128)S(1)}, f32[4,16,640]{2,1,0:T(8,128)S(1)}, u32[]{:S(2)}, u32[]{:S(2)}) collective-permute-start(f32[4,16,640]{2,1,0:T(8,128)S(1)} %get-tuple-element.30), channel_id=1, source_target_pairs={{0,16},{16,32},{32,48},{48,64},{64,80},{80,96},{96,112},{1,17},{17... | collective-permute-start | bytes 491528 | tf_op jit(solution)/shard_map/ppermute | solution.py:80
  94.4 9.0 %collective-permute-start.7 = (f32[4,16,640]{2,1,0:T(8,128)S(1)}, f32[4,16,640]{2,1,0:T(8,128)S(1)}, u32[]{:S(2)}, u32[]{:S(2)}) collective-permute-start(f32[4,16,640]{2,1,0:T(8,128)S(1)} %get-tuple-element.29), channel_id=1, source_target_pairs={{16,0},{32,16},{48,32},{64,48},{80,64},{96,80},{112,96},{17,1},{33... | collective-permute-start | bytes 491528 | tf_op jit(solution)/shard_map/ppermute | solution.py:81
  97.7 6.4 %collective-permute-start.2 = (f32[4,16,640]{2,1,0:T(8,128)S(1)}, f32[4,16,640]{2,1,0:T(8,128)S(1)}, u32[]{:S(2)}, u32[]{:S(2)}) collective-permute-start(f32[4,16,640]{2,1,0:T(8,128)S(1)} %get-tuple-element.32), channel_id=1, source_target_pairs={{0,16},{16,32},{32,48},{48,64},{64,80},{80,96},{96,112},{1,17},{17... | collective-permute-start | bytes 491528 | tf_op jit(solution)/shard_map/ppermute | solution.py:80
  99.8 7.1 %collective-permute-start.3 = (f32[4,16,640]{2,1,0:T(8,128)S(1)}, f32[4,16,640]{2,1,0:T(8,128)S(1)}, u32[]{:S(2)}, u32[]{:S(2)}) collective-permute-start(f32[4,16,640]{2,1,0:T(8,128)S(1)} %get-tuple-element.31), channel_id=1, source_target_pairs={{16,0},{32,16},{48,32},{64,48},{80,64},{96,80},{112,96},{17,1},{33... | collective-permute-start | bytes 491528 | tf_op jit(solution)/shard_map/ppermute | solution.py:81
  103.5 3.4 %copy-start.1 = (f32[4,304,640]{2,1,0:T(8,128)}, f32[4,304,640]{2,1,0:T(8,128)S(1)}, u32[]{:S(2)}) copy-start(f32[4,304,640]{2,1,0:T(8,128)S(1)} %constant_dynamic-update-slice_fusion.5.r_ref) | copy-start | bytes 9338884
  120.6 24.1 %copy-start.5 = (f32[1,304,640]{2,1,0:T(8,128)S(1)}, f32[1,304,640]{2,1,0:T(8,128)}, u32[]{:S(2)}) copy-start(f32[1,304,640]{2,1,0:T(8,128)} %constant_dynamic-update-slice_fusion.19) | copy-start | bytes 2334724
  120.7 10.0 %collective-permute-start.8 = (f32[1,16,256]{1,2,0:T(8,128)S(1)}, f32[1,16,256]{1,2,0:T(8,128)S(1)}, u32[]{:S(2)}, u32[]{:S(2)}) collective-permute-start(f32[1,16,256]{1,2,0:T(8,128)S(1)} %get-tuple-element.43), channel_id=1, source_target_pairs={{1,0},{2,1},{3,2},{4,3},{5,4},{6,5},{7,6},{8,7},{9,8},{10,9},{11,1... | collective-permute-start | bytes 49160 | tf_op jit(solution)/shard_map/ppermute | solution.py:75
  122.8 9.2 %collective-permute-start.9 = (f32[1,16,256]{1,2,0:T(8,128)S(1)}, f32[1,16,256]{1,2,0:T(8,128)S(1)}, u32[]{:S(2)}, u32[]{:S(2)}) collective-permute-start(f32[1,16,256]{1,2,0:T(8,128)S(1)} %get-tuple-element.44), channel_id=1, source_target_pairs={{0,1},{1,2},{2,3},{3,4},{4,5},{5,6},{6,7},{7,8},{8,9},{9,10},{10,1... | collective-permute-start | bytes 49160 | tf_op jit(solution)/shard_map/ppermute | solution.py:72
  133.1 11.6 %collective-permute-start.14 = (f32[1,16,640]{2,1,0:T(8,128)S(1)}, f32[1,16,640]{2,1,0:T(8,128)S(1)}, u32[]{:S(2)}, u32[]{:S(2)}) collective-permute-start(f32[1,16,640]{2,1,0:T(8,128)S(1)} %get-tuple-element.38), channel_id=1, source_target_pairs={{0,16},{16,32},{32,48},{48,64},{64,80},{80,96},{96,112},{1,17},{17... | collective-permute-start | bytes 122888 | tf_op jit(solution)/shard_map/ppermute | solution.py:80
  135.4 9.5 %collective-permute-start.15 = (f32[1,16,640]{2,1,0:T(8,128)S(1)}, f32[1,16,640]{2,1,0:T(8,128)S(1)}, u32[]{:S(2)}, u32[]{:S(2)}) collective-permute-start(f32[1,16,640]{2,1,0:T(8,128)S(1)} %get-tuple-element.37), channel_id=1, source_target_pairs={{16,0},{32,16},{48,32},{64,48},{80,64},{96,80},{112,96},{17,1},{33... | collective-permute-start | bytes 122888 | tf_op jit(solution)/shard_map/ppermute | solution.py:81
  138.5 6.4 %collective-permute-start.10 = (f32[1,16,640]{2,1,0:T(8,128)S(1)}, f32[1,16,640]{2,1,0:T(8,128)S(1)}, u32[]{:S(2)}, u32[]{:S(2)}) collective-permute-start(f32[1,16,640]{2,1,0:T(8,128)S(1)} %get-tuple-element.40), channel_id=1, source_target_pairs={{0,16},{16,32},{32,48},{48,64},{64,80},{80,96},{96,112},{1,17},{17... | collective-permute-start | bytes 122888 | tf_op jit(solution)/shard_map/ppermute | solution.py:80
  142.8 4.7 %collective-permute-start.11 = (f32[1,16,640]{2,1,0:T(8,128)S(1)}, f32[1,16,640]{2,1,0:T(8,128)S(1)}, u32[]{:S(2)}, u32[]{:S(2)}) collective-permute-start(f32[1,16,640]{2,1,0:T(8,128)S(1)} %get-tuple-element.39), channel_id=1, source_target_pairs={{16,0},{32,16},{48,32},{64,48},{80,64},{96,80},{112,96},{17,1},{33... | collective-permute-start | bytes 122888 | tf_op jit(solution)/shard_map/ppermute | solution.py:81
  144.9 2.6 copy-start.6
  147.6 0.9 copy-start.4

commit v6 on v5

--- a/solution.py
+++ b/solution.py
@@ -87,27 +87,41 @@
     lax.fori_loop(0, count, lambda c, carry: (body(c), carry)[1], 0)
 
 
-def conductances(r_ref, cu, cd, cl, cr, cv):
+def conductances(r_ref, cu, cd, cl, cr, dg, cv):
     layers, frame_rows, frame_cols = r_ref.shape
     count = (frame_rows - 2 * SLACK) // CHUNK
 
     def body(c):
         lead = pl.multiple_of(c * CHUNK, 8)
         rows = pl.ds(pl.multiple_of(lead + SLACK, 8), CHUNK)
+        below = None
         for l in range(layers):
             win = r_ref[l, pl.ds(lead, CHUNK + 2 * SLACK), :]
             r = win[SLACK : SLACK + CHUNK]
-            cu[l, rows, :] = r * pltpu.roll(win, 1, 0)[SLACK : SLACK + CHUNK]
-            cd[l, rows, :] = r * pltpu.roll(win, CHUNK + 2 * SLACK - 1, 0)[SLACK : SLACK + CHUNK]
-            cl[l, rows, :] = r * pltpu.roll(r, 1, 1)
-            cr[l, rows, :] = r * pltpu.roll(r, frame_cols - 1, 1)
+            up = r * pltpu.roll(win, 1, 0)[SLACK : SLACK + CHUNK]
+            down = r * pltpu.roll(win, CHUNK + 2 * SLACK - 1, 0)[SLACK : SLACK + CHUNK]
+            left = r * pltpu.roll(r, 1, 1)
+            right = r * pltpu.roll(r, frame_cols - 1, 1)
+            total = up + down + left + right
+            cu[l, rows, :] = RATE * up
+            cd[l, rows, :] = RATE * down
+            cl[l, rows, :] = RATE * left
+            cr[l, rows, :] = RATE * right
             if l + 1 < layers:
-                cv[l, rows, :] = r_ref[l + 1, rows, :] * r
+                vertical = r_ref[l + 1, rows, :] * r
+                cv[l, rows, :] = RATE * vertical
+                total = total + vertical
+            if below is not None:
+                total = total + below
+            if l == layers - 1:
+                total = total + AMBIENT_LOSS
+            dg[l, rows, :] = 1.0 - RATE * total
+            below = vertical if l + 1 < layers else None
 
     chunk_loop(count, body)
 
 
-def explicit_step(src, dst, cu, cd, cl, cr, cv, s_ref):
+def explicit_step(src, dst, cu, cd, cl, cr, dg, cv, s_ref):
     layers, frame_rows, frame_cols = dst.shape
     count = (frame_rows - 2 * SLACK) // CHUNK
 
@@ -121,19 +135,17 @@
             down = pltpu.roll(win, CHUNK + 2 * SLACK - 1, 0)[SLACK : SLACK + CHUNK]
             left = pltpu.roll(f, 1, 1)
             right = pltpu.roll(f, frame_cols - 1, 1)
-            inflow = cu[l, rows, :] * (up - f)
-            inflow = inflow + cd[l, rows, :] * (down - f)
-            inflow = inflow + cl[l, rows, :] * (left - f)
-            inflow = inflow + cr[l, rows, :] * (right - f)
+            value = dg[l, rows, :] * f + cu[l, rows, :] * up
+            value = value + cd[l, rows, :] * down
+            value = value + cl[l, rows, :] * left
+            value = value + cr[l, rows, :] * right
             if l + 1 < layers:
-                inflow = inflow + cv[l, rows, :] * (src[l + 1, rows, :] - f)
+                value = value + cv[l, rows, :] * src[l + 1, rows, :]
             if l > 0:
-                inflow = inflow - cv[l - 1, rows, :] * (f - src[l - 1, rows, :])
-            if l == layers - 1:
-                inflow = inflow - AMBIENT_LOSS * f
+                value = value + cv[l - 1, rows, :] * src[l - 1, rows, :]
             if l == 0 and s_ref is not None:
-                inflow = inflow + s_ref[rows, :]
-            dst[l, rows, :] = f + RATE * inflow
+                value = value + RATE * s_ref[rows, :]
+            dst[l, rows, :] = value
 
     chunk_loop(count, body)
 
@@ -154,16 +166,16 @@
     chunk_loop(height // CHUNK, body)
 
 
-def solve_kernel(f_ref, r_ref, s_ref, t_ref, out_ref, grad_ref, gsum_ref, cu, cd, cl, cr, cv, a, b):
+def solve_kernel(f_ref, r_ref, s_ref, t_ref, out_ref, grad_ref, gsum_ref, cu, cd, cl, cr, dg, cv, a, b):
     layers, height, breadth = out_ref.shape
     frame_rows = a.shape[1]
     clear_slack(a)
     clear_slack(b)
-    conductances(r_ref, cu, cd, cl, cr, cv)
+    conductances(r_ref, cu, cd, cl, cr, dg, cv)
     src = f_ref
     for index in range(STEPS):
         dst = a if index % 2 == 0 else b
-        explicit_step(src, dst, cu, cd, cl, cr, cv, s_ref)
+        explicit_step(src, dst, cu, cd, cl, cr, dg, cv, s_ref)
         src = dst
 
     def put(rows, value):
@@ -191,7 +203,7 @@
 
         copy_center(lambda rows, width, v=view: v[0, rows, 0:width], put_sum, height, breadth)
         dst = final if src is start else start
-        explicit_step(src, dst, cu, cd, cl, cr, cv, None)
+        explicit_step(src, dst, cu, cd, cl, cr, dg, cv, None)
         src = dst
 
     def put_grad(rows, value):
@@ -202,7 +214,7 @@
 
 def stencil_scratch(layers, frame_rows, frame_cols):
     whole = pltpu.VMEM((layers, frame_rows, frame_cols), jnp.float32)
-    return [whole] * 4 + [pltpu.VMEM((layers - 1, frame_rows, frame_cols), jnp.float32), whole, whole]
+    return [whole] * 5 + [pltpu.VMEM((layers - 1, frame_rows, frame_cols), jnp.float32), whole, whole]
 
 
 def vmem_specs(count):

time: 292 us -> 292 us (level)
  no operation moved by 1% of the time
where the time goes in v6:
time: 292 us; the launch traced here: 287 us
  starting transfers between devices  67.5 us (23%)
  blocking collectives  67.4 us (23%)
  Pallas kernels  51.9 us (18%)
  waiting for transfers between devices  40.1 us (14%)
  local copies, waits for them, and re-layouts  37.4 us (13%)
  matrix products  13.4 us (5%)
  other arithmetic  7.91 us (3%)
    all_to_all x1, blocking collectives, return_grads(): lax.all_to_all(backward.reshape(row_count * col_count, CAP, -1), ('row',...  67.4 us
    pallas_call x1, Pallas kernels, run_solve(): pl.pallas_call(solve_kernel, out_shape=(field, field, jax.ShapeDtypeStruc...  51.9 us
    ppermute x4, waiting for transfers between devices, framed(): lax.ppermute(jnp.swapaxes(cells[:, :, :HALO], 1, 2), 'col', [(i + 1, i) f...  35.6 us
    ppermute x4, starting transfers between devices, framed(): lax.ppermute(jnp.swapaxes(cells[:, :, breadth - HALO:], 1, 2), 'col', [(i...  23.3 us
    ppermute x4, starting transfers between devices, framed(): lax.ppermute(band[:, height - HALO:], 'row', [(i, i + 1) for i in range(r...  13.3 us
    ppermute x4, starting transfers between devices, framed(): lax.ppermute(band[:, :HALO], 'row', [(i + 1, i) for i in range(rows - 1)])  11.7 us
    all_to_all x1, starting transfers between devices, send_dies(): lax.all_to_all(outbound.reshape(row_count * col_count, CAP, -1), ('row',...  11 us
    ppermute x4, starting transfers between devices, framed(): lax.ppermute(jnp.swapaxes(cells[:, :, :HALO], 1, 2), 'col', [(i + 1, i) f...  8.18 us
  transfers between devices with their start and end apart: 17, of which 6 were waited for; matrix products, arithmetic and copies ran while one was open for 8% of the time, Pallas kernels for 0%

profile of v6, /device:TPU:15, one launch (start us, length us, event | category | flops | bytes accessed | tf_op | source)
XLA Modules:
  0.0 286.8 jit_solution(4942464520399803437)
XLA Ops:
  1.3 0.8 convert_reduce_fusion
  2.1 0.7 multiply_add_fusion
  2.8 2.1 reshape.110
  4.9 0.7 fusion.15
  5.7 3.8 %fusion.2 = f32[256,4224]{1,0:T(8,128)} fusion(f32[64,1]{1,0:T(8,128)S(1)} %copy.34, f32[64,4096]{1,0:T(8,128)S(1)} %reshape.110, s32[64]{0:T(128)S(1)} %multiply_add_fusion), kind=kOutput, calls=%fused_computation.7 | convolution fusion | flops 831299584 | bytes 5374464 | tf_op jit(solution)/shard_map/dot_general | solution.py:278
  9.5 6.0 %reshape.112 = f32[128,2,4224]{2,1,0:T(2,128)} reshape(f32[256,4224]{1,0:T(8,128)} %fusion.2) | data formatting | bytes 8650752 | tf_op jit(solution)/shard_map/reshape | solution.py:239
  15.5 11.0 %all-to-all-start = ((f32[128,2,4224]{2,1,0:T(2,128)}), f32[128,2,4224]{2,1,0:T(2,128)}, u32[]{:S(2)}, u32[]{:S(2)}) async-start(f32[128,2,4224]{2,1,0:T(2,128)} %reshape.112), calls=%async_computation | async-start | bytes 8650752 | tf_op jit(solution)/shard_map/all_to_all | solution.py:238
  26.9 2.1 add_sqrt_fusion
  29.2 2.3 collective-permute-start.4
  31.5 6.9 %collective-permute-start.5 = (f32[4,16,256]{1,2,0:T(8,128)S(1)}, f32[4,16,256]{1,2,0:T(8,128)S(1)}, u32[]{:S(2)}, u32[]{:S(2)}) collective-permute-start(f32[4,16,256]{1,2,0:T(8,128)S(1)} %get-tuple-element.34), channel_id=1, source_target_pairs={{0,1},{1,2},{2,3},{3,4},{4,5},{5,6},{6,7},{7,8},{8,9},{9,10},{10,1... | collective-permute-start | bytes 196616 | tf_op jit(solution)/shard_map/ppermute | solution.py:72
  38.6 1.9 collective-permute-start
  40.5 7.3 %collective-permute-start.1 = (f32[4,16,256]{1,2,0:T(8,128)S(1)}, f32[4,16,256]{1,2,0:T(8,128)S(1)}, u32[]{:S(2)}, u32[]{:S(2)}) collective-permute-start(f32[4,16,256]{1,2,0:T(8,128)S(1)} %get-tuple-element.36), channel_id=1, source_target_pairs={{0,1},{1,2},{2,3},{3,4},{4,5},{5,6},{6,7},{7,8},{8,9},{9,10},{10,1... | collective-permute-start | bytes 196616 | tf_op jit(solution)/shard_map/ppermute | solution.py:72
  47.8 0.8 slice_bitcast_fusion.5
  48.5 1.9 collective-permute-start.12
  51.2 0.7 constant_dynamic-update-slice_fusion.4
  51.8 31.4 %collective-permute-done.4 = f32[4,16,256]{1,2,0:T(8,128)S(1)} collective-permute-done((f32[4,16,256]{1,2,0:T(8,128)S(1)}, f32[4,16,256]{1,2,0:T(8,128)S(1)}, u32[]{:S(2)}, u32[]{:S(2)}) %collective-permute-start.4) | collective-permute-done | bytes 65568 | tf_op jit(solution)/shard_map/ppermute | solution.py:75
  83.2 1.9 collective-permute-start.13
  85.2 3.7 %collective-permute-done = f32[4,16,256]{1,2,0:T(8,128)S(1)} collective-permute-done((f32[4,16,256]{1,2,0:T(8,128)S(1)}, f32[4,16,256]{1,2,0:T(8,128)S(1)}, u32[]{:S(2)}, u32[]{:S(2)}) %collective-permute-start) | collective-permute-done | bytes 65568 | tf_op jit(solution)/shard_map/ppermute | solution.py:75
  88.9 0.8 pad_maximum_fusion.1
  89.7 4.7 %collective-permute-start.6 = (f32[4,16,640]{2,1,0:T(8,128)S(1)}, f32[4,16,640]{2,1,0:T(8,128)S(1)}, u32[]{:S(2)}, u32[]{:S(2)}) collective-permute-start(f32[4,16,640]{2,1,0:T(8,128)S(1)} %get-tuple-element.30), channel_id=1, source_target_pairs={{0,16},{16,32},{32,48},{48,64},{64,80},{80,96},{96,112},{1,17},{17... | collective-permute-start | bytes 491528 | tf_op jit(solution)/shard_map/ppermute | solution.py:80
  94.4 3.2 %collective-permute-start.7 = (f32[4,16,640]{2,1,0:T(8,128)S(1)}, f32[4,16,640]{2,1,0:T(8,128)S(1)}, u32[]{:S(2)}, u32[]{:S(2)}) collective-permute-start(f32[4,16,640]{2,1,0:T(8,128)S(1)} %get-tuple-element.29), channel_id=1, source_target_pairs={{16,0},{32,16},{48,32},{64,48},{80,64},{96,80},{112,96},{17,1},{33... | collective-permute-start | bytes 491528 | tf_op jit(solution)/shard_map/ppermute | solution.py:81
  97.7 2.0 collective-permute-start.2
  99.8 3.4 %collective-permute-start.3 = (f32[4,16,640]{2,1,0:T(8,128)S(1)}, f32[4,16,640]{2,1,0:T(8,128)S(1)}, u32[]{:S(2)}, u32[]{:S(2)}) collective-permute-start(f32[4,16,640]{2,1,0:T(8,128)S(1)} %get-tuple-element.31), channel_id=1, source_target_pairs={{16,0},{32,16},{48,32},{64,48},{80,64},{96,80},{112,96},{17,1},{33... | collective-permute-start | bytes 491528 | tf_op jit(solution)/shard_map/ppermute | solution.py:81
  104.1 1.1 constant_dynamic-update-slice_fusion.3
  105.2 1.7 constant_dynamic-update-slice_fusion.2
  106.9 0.7 constant_dynamic-update-slice_fusion.1
  107.6 0.7 constant_dynamic-update-slice_fusion.f_ref
  108.2 6.2 %reshape.113 = f32[256,4224]{1,0:T(8,128)} reshape(f32[128,2,4224]{2,1,0:T(2,128)} %all-to-all-done) | data formatting | bytes 8650752 | tf_op jit(solution)/shard_map/reshape | solution.py:245
  114.5 1.0 fusion.8
  115.5 3.8 %fusion = f32[32,4096]{1,0:T(8,128)S(1)} fusion(f32[256,4224]{1,0:T(8,128)} %reshape.113, s32[256]{0:T(256)S(1)} %fusion.8), kind=kOutput, calls=%fused_computation.1 | convolution fusion | flops 402661376 | bytes 4719616 | tf_op jit(solution)/shard_map/dot_general | solution.py:284
  120.7 2.1 collective-permute-start.8
  122.8 7.3 %collective-permute-start.9 = (f32[1,16,256]{1,2,0:T(8,128)S(1)}, f32[1,16,256]{1,2,0:T(8,128)S(1)}, u32[]{:S(2)}, u32[]{:S(2)}) collective-permute-start(f32[1,16,256]{1,2,0:T(8,128)S(1)} %get-tuple-element.44), channel_id=1, source_target_pairs={{0,1},{1,2},{2,3},{3,4},{4,5},{5,6},{6,7},{7,8},{8,9},{9,10},{10,1... | collective-permute-start | bytes 49160 | tf_op jit(solution)/shard_map/ppermute | solution.py:72
  130.8 1.2 collective-permute-done.9
  132.0 1.1 pad_maximum_fusion.3
  133.1 2.2 collective-permute-start.14
  135.4 3.1 %collective-permute-start.15 = (f32[1,16,640]{2,1,0:T(8,128)S(1)}, f32[1,16,640]{2,1,0:T(8,128)S(1)}, u32[]{:S(2)}, u32[]{:S(2)}) collective-permute-start(f32[1,16,640]{2,1,0:T(8,128)S(1)} %get-tuple-element.37), channel_id=1, source_target_pairs={{16,0},{32,16},{48,32},{64,48},{80,64},{96,80},{112,96},{17,1},{33... | collective-permute-start | bytes 122888 | tf_op jit(solution)/shard_map/ppermute | solution.py:81
  138.5 4.3 %collective-permute-start.10 = (f32[1,16,640]{2,1,0:T(8,128)S(1)}, f32[1,16,640]{2,1,0:T(8,128)S(1)}, u32[]{:S(2)}, u32[]{:S(2)}) collective-permute-start(f32[1,16,640]{2,1,0:T(8,128)S(1)} %get-tuple-element.40), channel_id=1, source_target_pairs={{0,16},{16,32},{32,48},{48,64},{64,80},{80,96},{96,112},{1,17},{17... | collective-permute-start | bytes 122888 | tf_op jit(solution)/shard_map/ppermute | solution.py:80
  142.8 1.9 collective-permute-start.11
  144.9 2.6 collective-permute-done.11
  147.6 0.9 copy-done.4
  148.4 51.9 %shard_map.94 = (f32[4,256,512]{2,1,0:T(8,128)}, f32[4,256,512]{2,1,0:T(8,128)}, f32[256,512]{1,0:T(8,128)}) custom-call(f32[4,304,640]{2,1,0:T(8,128)} %constant_dynamic-update-slice_fusion.f_ref, f32[4,304,640]{2,1,0:T(8,128)} %copy-done.1, f32[304,640]{1,0:T(8,128)} %bitcast.45, f32[304,640]{1,0:T(8,128)} %bitcast.46), custom_call_target="tpu_custom_call" | custom-call | tf_op jit(solution)/shard_map/pallas_call | solution.py:227
  200.3 1.2 reshape.115
  202.1 1.8 fusion.9
  203.9 3.2 %copy.33 = f32[128,2,4096]{2,1,0:T(2,128)S(1)} copy(f32[128,2,4096]{2,0,1:T(8,128)S(1)} %fusion.9) | data formatting | bytes 8388608 | tf_op jit(solution)/shard_map/dot_general | solution.py:301
  207.2 67.4 %all_to_all.10 = f32[128,2,4096]{2,1,0:T(2,128)} all-to-all(f32[128,2,4096]{2,1,0:T(2,128)S(1)} %copy.33), channel_id=1, replica_groups=mesh['row'=8,'col'=16] {'row','col'}, dimensions={0} | all-to-all | bytes 8388608 | tf_op jit(solution)/shard_map/all_to_all | solution.py:249
  274.6 6.1 %reshape.117 = f32[256,4096]{1,0:T(8,128)} reshape(f32[128,2,4096]{2,1,0:T(2,128)} %all_to_all.10) | data formatting | bytes 8388608 | tf_op jit(solution)/shard_map/reshape | solution.py:256
  280.7 3.9 %convolution_multiply_fusion = f32[64,4096]{1,0:T(8,128)S(1)} fusion(f32[256,4096]{1,0:T(8,128)} %reshape.117, s32[64]{0:T(128)S(1)} %multiply_add_fusion), kind=kOutput, calls=%fused_computation | convolution fusion | flops 805584896 | bytes 5243136 | tf_op jit(solution)/shard_map/dot_general | solution.py:303
  284.7 2.2 reshape.118
  (64 shorter events, 5.8 us)
Async XLA Ops:
  0.6 4.3 %copy-start.8 = (s32[64]{0:T(128)S(1)}, s32[64]{0:T(128)}, u32[]{:S(2)}) copy-start(s32[64]{0:T(128)} %param.12) | copy-start | bytes 772
  15.5 11.1 %copy-start.7 = (f32[4,8]{1,0:T(4,128)S(1)}, f32[4,8]{1,0:T(4,128)}, u32[]{:S(2)}) copy-start(f32[4,8]{1,0:T(4,128)} %param.14) | copy-start | bytes 388
  15.5 11.4 %copy-start.2 = (s32[4,256,512]{2,1,0:T(8,128)S(1)}, s32[4,256,512]{2,1,0:T(8,128)}, u32[]{:S(2)}) copy-start(s32[4,256,512]{2,1,0:T(8,128)} %param.13) | copy-start | bytes 6291460
  15.5 92.8 %all-to-all-start = ((f32[128,2,4224]{2,1,0:T(2,128)}), f32[128,2,4224]{2,1,0:T(2,128)}, u32[]{:S(2)}, u32[]{:S(2)}) async-start(f32[128,2,4224]{2,1,0:T(2,128)} %reshape.112), calls=%async_computation | async-start | bytes 8650752 | tf_op jit(solution)/shard_map/all_to_all | solution.py:238
  26.8 11.5 %copy-start = (f32[4,256,512]{2,1,0:T(8,128)S(1)}, f32[4,256,512]{2,1,0:T(8,128)}, u32[]{:S(2)}) copy-start(f32[4,256,512]{2,1,0:T(8,128)} %param.9) | copy-start | bytes 6291460
  29.0 18.8 %copy-start.3 = (f32[256,512]{1,0:T(8,128)S(1)}, f32[256,512]{1,0:T(8,128)}, u32[]{:S(2)}) copy-start(f32[256,512]{1,0:T(8,128)} %param.15) | copy-start | bytes 1572868
  29.2 54.1 %collective-permute-start.4 = (f32[4,16,256]{1,2,0:T(8,128)S(1)}, f32[4,16,256]{1,2,0:T(8,128)S(1)}, u32[]{:S(2)}, u32[]{:S(2)}) collective-permute-start(f32[4,16,256]{1,2,0:T(8,128)S(1)} %get-tuple-element.33), channel_id=1, source_target_pairs={{1,0},{2,1},{3,2},{4,3},{5,4},{6,5},{7,6},{8,7},{9,8},{10,9},{11,1... | collective-permute-start | bytes 196616 | tf_op jit(solution)/shard_map/ppermute | solution.py:75
  31.5 53.7 %collective-permute-start.5 = (f32[4,16,256]{1,2,0:T(8,128)S(1)}, f32[4,16,256]{1,2,0:T(8,128)S(1)}, u32[]{:S(2)}, u32[]{:S(2)}) collective-permute-start(f32[4,16,256]{1,2,0:T(8,128)S(1)} %get-tuple-element.34), channel_id=1, source_target_pairs={{0,1},{1,2},{2,3},{3,4},{4,5},{5,6},{6,7},{7,8},{8,9},{9,10},{10,1... | collective-permute-start | bytes 196616 | tf_op jit(solution)/shard_map/ppermute | solution.py:72
  38.6 50.3 %collective-permute-start = (f32[4,16,256]{1,2,0:T(8,128)S(1)}, f32[4,16,256]{1,2,0:T(8,128)S(1)}, u32[]{:S(2)}, u32[]{:S(2)}) collective-permute-start(f32[4,16,256]{1,2,0:T(8,128)S(1)} %get-tuple-element.35), channel_id=1, source_target_pairs={{1,0},{2,1},{3,2},{4,3},{5,4},{6,5},{7,6},{8,7},{9,8},{10,9},{11,1... | collective-permute-start | bytes 196616 | tf_op jit(solution)/shard_map/ppermute | solution.py:75
  40.5 48.4 %collective-permute-start.1 = (f32[4,16,256]{1,2,0:T(8,128)S(1)}, f32[4,16,256]{1,2,0:T(8,128)S(1)}, u32[]{:S(2)}, u32[]{:S(2)}) collective-permute-start(f32[4,16,256]{1,2,0:T(8,128)S(1)} %get-tuple-element.36), channel_id=1, source_target_pairs={{0,1},{1,2},{2,3},{3,4},{4,5},{5,6},{6,7},{7,8},{8,9},{9,10},{10,1... | collective-permute-start | bytes 196616 | tf_op jit(solution)/shard_map/ppermute | solution.py:72
  48.5 81.7 %collective-permute-start.12 = (f32[1,16,256]{1,2,0:T(8,128)}, f32[1,16,256]{1,2,0:T(8,128)}, u32[]{:S(2)}, u32[]{:S(2)}) collective-permute-start(f32[1,16,256]{1,2,0:T(8,128)} %get-tuple-element.41), channel_id=1, source_target_pairs={{1,0},{2,1},{3,2},{4,3},{5,4},{6,5},{7,6},{8,7},{9,8},{10,9},{11,1... | collective-permute-start | bytes 49160 | tf_op jit(solution)/shard_map/ppermute | solution.py:75
  83.2 47.0 %collective-permute-start.13 = (f32[1,16,256]{1,2,0:T(8,128)}, f32[1,16,256]{1,2,0:T(8,128)}, u32[]{:S(2)}, u32[]{:S(2)}) collective-permute-start(f32[1,16,256]{1,2,0:T(8,128)} %get-tuple-element.42), channel_id=1, source_target_pairs={{0,1},{1,2},{2,3},{3,4},{4,5},{5,6},{6,7},{7,8},{8,9},{9,10},{10,1... | collective-permute-start | bytes 49160 | tf_op jit(solution)/shard_map/ppermute | solution.py:72
  89.7 10.1 %collective-permute-start.6 = (f32[4,16,640]{2,1,0:T(8,128)S(1)}, f32[4,16,640]{2,1,0:T(8,128)S(1)}, u32[]{:S(2)}, u32[]{:S(2)}) collective-permute-start(f32[4,16,640]{2,1,0:T(8,128)S(1)} %get-tuple-element.30), channel_id=1, source_target_pairs={{0,16},{16,32},{32,48},{48,64},{64,80},{80,96},{96,112},{1,17},{17... | collective-permute-start | bytes 491528 | tf_op jit(solution)/shard_map/ppermute | solution.py:80
  94.4 9.0 %collective-permute-start.7 = (f32[4,16,640]{2,1,0:T(8,128)S(1)}, f32[4,16,640]{2,1,0:T(8,128)S(1)}, u32[]{:S(2)}, u32[]{:S(2)}) collective-permute-start(f32[4,16,640]{2,1,0:T(8,128)S(1)} %get-tuple-element.29), channel_id=1, source_target_pairs={{16,0},{32,16},{48,32},{64,48},{80,64},{96,80},{112,96},{17,1},{33... | collective-permute-start | bytes 491528 | tf_op jit(solution)/shard_map/ppermute | solution.py:81
  97.7 6.4 %collective-permute-start.2 = (f32[4,16,640]{2,1,0:T(8,128)S(1)}, f32[4,16,640]{2,1,0:T(8,128)S(1)}, u32[]{:S(2)}, u32[]{:S(2)}) collective-permute-start(f32[4,16,640]{2,1,0:T(8,128)S(1)} %get-tuple-element.32), channel_id=1, source_target_pairs={{0,16},{16,32},{32,48},{48,64},{64,80},{80,96},{96,112},{1,17},{17... | collective-permute-start | bytes 491528 | tf_op jit(solution)/shard_map/ppermute | solution.py:80
  99.8 7.1 %collective-permute-start.3 = (f32[4,16,640]{2,1,0:T(8,128)S(1)}, f32[4,16,640]{2,1,0:T(8,128)S(1)}, u32[]{:S(2)}, u32[]{:S(2)}) collective-permute-start(f32[4,16,640]{2,1,0:T(8,128)S(1)} %get-tuple-element.31), channel_id=1, source_target_pairs={{16,0},{32,16},{48,32},{64,48},{80,64},{96,80},{112,96},{17,1},{33... | collective-permute-start | bytes 491528 | tf_op jit(solution)/shard_map/ppermute | solution.py:81
  103.5 3.4 %copy-start.1 = (f32[4,304,640]{2,1,0:T(8,128)}, f32[4,304,640]{2,1,0:T(8,128)S(1)}, u32[]{:S(2)}) copy-start(f32[4,304,640]{2,1,0:T(8,128)S(1)} %constant_dynamic-update-slice_fusion.5.r_ref) | copy-start | bytes 9338884
  120.6 24.1 %copy-start.5 = (f32[1,304,640]{2,1,0:T(8,128)S(1)}, f32[1,304,640]{2,1,0:T(8,128)}, u32[]{:S(2)}) copy-start(f32[1,304,640]{2,1,0:T(8,128)} %constant_dynamic-update-slice_fusion.19) | copy-start | bytes 2334724
  120.7 10.0 %collective-permute-start.8 = (f32[1,16,256]{1,2,0:T(8,128)S(1)}, f32[1,16,256]{1,2,0:T(8,128)S(1)}, u32[]{:S(2)}, u32[]{:S(2)}) collective-permute-start(f32[1,16,256]{1,2,0:T(8,128)S(1)} %get-tuple-element.43), channel_id=1, source_target_pairs={{1,0},{2,1},{3,2},{4,3},{5,4},{6,5},{7,6},{8,7},{9,8},{10,9},{11,1... | collective-permute-start | bytes 49160 | tf_op jit(solution)/shard_map/ppermute | solution.py:75
  122.8 9.2 %collective-permute-start.9 = (f32[1,16,256]{1,2,0:T(8,128)S(1)}, f32[1,16,256]{1,2,0:T(8,128)S(1)}, u32[]{:S(2)}, u32[]{:S(2)}) collective-permute-start(f32[1,16,256]{1,2,0:T(8,128)S(1)} %get-tuple-element.44), channel_id=1, source_target_pairs={{0,1},{1,2},{2,3},{3,4},{4,5},{5,6},{6,7},{7,8},{8,9},{9,10},{10,1... | collective-permute-start | bytes 49160 | tf_op jit(solution)/shard_map/ppermute | solution.py:72
  133.1 11.6 %collective-permute-start.14 = (f32[1,16,640]{2,1,0:T(8,128)S(1)}, f32[1,16,640]{2,1,0:T(8,128)S(1)}, u32[]{:S(2)}, u32[]{:S(2)}) collective-permute-start(f32[1,16,640]{2,1,0:T(8,128)S(1)} %get-tuple-element.38), channel_id=1, source_target_pairs={{0,16},{16,32},{32,48},{48,64},{64,80},{80,96},{96,112},{1,17},{17... | collective-permute-start | bytes 122888 | tf_op jit(solution)/shard_map/ppermute | solution.py:80
  135.4 9.5 %collective-permute-start.15 = (f32[1,16,640]{2,1,0:T(8,128)S(1)}, f32[1,16,640]{2,1,0:T(8,128)S(1)}, u32[]{:S(2)}, u32[]{:S(2)}) collective-permute-start(f32[1,16,640]{2,1,0:T(8,128)S(1)} %get-tuple-element.37), channel_id=1, source_target_pairs={{16,0},{32,16},{48,32},{64,48},{80,64},{96,80},{112,96},{17,1},{33... | collective-permute-start | bytes 122888 | tf_op jit(solution)/shard_map/ppermute | solution.py:81
  138.5 6.4 %collective-permute-start.10 = (f32[1,16,640]{2,1,0:T(8,128)S(1)}, f32[1,16,640]{2,1,0:T(8,128)S(1)}, u32[]{:S(2)}, u32[]{:S(2)}) collective-permute-start(f32[1,16,640]{2,1,0:T(8,128)S(1)} %get-tuple-element.40), channel_id=1, source_target_pairs={{0,16},{16,32},{32,48},{48,64},{64,80},{80,96},{96,112},{1,17},{17... | collective-permute-start | bytes 122888 | tf_op jit(solution)/shard_map/ppermute | solution.py:80
  142.8 4.7 %collective-permute-start.11 = (f32[1,16,640]{2,1,0:T(8,128)S(1)}, f32[1,16,640]{2,1,0:T(8,128)S(1)}, u32[]{:S(2)}, u32[]{:S(2)}) collective-permute-start(f32[1,16,640]{2,1,0:T(8,128)S(1)} %get-tuple-element.39), channel_id=1, source_target_pairs={{16,0},{32,16},{48,32},{64,48},{80,64},{96,80},{112,96},{17,1},{33... | collective-permute-start | bytes 122888 | tf_op jit(solution)/shard_map/ppermute | solution.py:81
  144.9 2.6 copy-start.6
  147.6 0.9 copy-start.4

commit v7 on v6

--- a/solution.py
+++ b/solution.py
@@ -61,7 +61,7 @@
 
 HALO = 16
 SLACK = 8
-CHUNK = 16
+CHUNK = 8
 LANE = 128
 
 
@@ -84,7 +84,7 @@
 
 
 def chunk_loop(count, body):
-    lax.fori_loop(0, count, lambda c, carry: (body(c), carry)[1], 0)
+    lax.fori_loop(0, count, lambda c, carry: (body(c), carry)[1], 0, unroll=9)
 
 
 def conductances(r_ref, cu, cd, cl, cr, dg, cv):
@@ -128,24 +128,33 @@
     def body(c):
         lead = pl.multiple_of(c * CHUNK, 8)
         rows = pl.ds(pl.multiple_of(lead + SLACK, 8), CHUNK)
+        above = pl.ds(pl.multiple_of(lead + SLACK - 8, 8), 8)
+        below = pl.ds(pl.multiple_of(lead + SLACK + CHUNK, 8), 8)
+        centre = [src[0, rows, :]] + [None] * (layers - 1)
+        lower = None
         for l in range(layers):
-            win = src[l, pl.ds(lead, CHUNK + 2 * SLACK), :]
-            f = win[SLACK : SLACK + CHUNK]
-            up = pltpu.roll(win, 1, 0)[SLACK : SLACK + CHUNK]
-            down = pltpu.roll(win, CHUNK + 2 * SLACK - 1, 0)[SLACK : SLACK + CHUNK]
+            f = centre[l]
+            win = jnp.concatenate([src[l, above, :], f, src[l, below, :]], axis=0)
+            size = win.shape[0]
+            up = pltpu.roll(win, 1, 0)[8 : 8 + CHUNK]
+            down = pltpu.roll(win, size - 1, 0)[8 : 8 + CHUNK]
             left = pltpu.roll(f, 1, 1)
             right = pltpu.roll(f, frame_cols - 1, 1)
             value = dg[l, rows, :] * f + cu[l, rows, :] * up
             value = value + cd[l, rows, :] * down
             value = value + cl[l, rows, :] * left
             value = value + cr[l, rows, :] * right
+            upper = None
             if l + 1 < layers:
-                value = value + cv[l, rows, :] * src[l + 1, rows, :]
+                centre[l + 1] = src[l + 1, rows, :]
+                upper = cv[l, rows, :]
+                value = value + upper * centre[l + 1]
             if l > 0:
-                value = value + cv[l - 1, rows, :] * src[l - 1, rows, :]
+                value = value + lower * centre[l - 1]
             if l == 0 and s_ref is not None:
                 value = value + RATE * s_ref[rows, :]
             dst[l, rows, :] = value
+            lower = upper
 
     chunk_loop(count, body)
 

time: 292 us -> 279 us (0.955)
  Pallas kernels: 51.9 us -> 39.8 us
    pallas_call x1, Pallas kernels: 51.9 us -> 39.8 us  [run_solve(): pl.pallas_call(solve_kernel, out_shape=(field, field, jax.ShapeDtypeStruc...]
where the time goes in v7:
time: 279 us; the launch traced here: 275 us
  starting transfers between devices  67.7 us (24%)
  blocking collectives  67.4 us (24%)
  waiting for transfers between devices  39.9 us (14%)
  Pallas kernels  39.8 us (14%)
  local copies, waits for them, and re-layouts  37.4 us (13%)
  matrix products  13.4 us (5%)
  other arithmetic  7.91 us (3%)
    all_to_all x1, blocking collectives, return_grads(): lax.all_to_all(backward.reshape(row_count * col_count, CAP, -1), ('row',...  67.4 us
    pallas_call x1, Pallas kernels, run_solve(): pl.pallas_call(solve_kernel, out_shape=(field, field, jax.ShapeDtypeStruc...  39.8 us
    ppermute x4, waiting for transfers between devices, framed(): lax.ppermute(jnp.swapaxes(cells[:, :, :HALO], 1, 2), 'col', [(i + 1, i) f...  35.6 us
    ppermute x4, starting transfers between devices, framed(): lax.ppermute(jnp.swapaxes(cells[:, :, breadth - HALO:], 1, 2), 'col', [(i...  23.3 us
    ppermute x4, starting transfers between devices, framed(): lax.ppermute(band[:, height - HALO:], 'row', [(i, i + 1) for i in range(r...  13.3 us
    ppermute x4, starting transfers between devices, framed(): lax.ppermute(band[:, :HALO], 'row', [(i + 1, i) for i in range(rows - 1)])  11.9 us
    all_to_all x1, starting transfers between devices, send_dies(): lax.all_to_all(outbound.reshape(row_count * col_count, CAP, -1), ('row',...  11 us
    ppermute x4, starting transfers between devices, framed(): lax.ppermute(jnp.swapaxes(cells[:, :, :HALO], 1, 2), 'col', [(i + 1, i) f...  8.18 us
  transfers between devices with their start and end apart: 17, of which 6 were waited for; matrix products, arithmetic and copies ran while one was open for 8% of the time, Pallas kernels for 0%

profile of v7, /device:TPU:15, one launch (start us, length us, event | category | flops | bytes accessed | tf_op | source)
XLA Modules:
  0.0 274.7 jit_solution(1877233561236844461)
XLA Ops:
  1.3 0.8 convert_reduce_fusion
  2.1 0.7 multiply_add_fusion
  2.8 2.1 reshape.110
  4.9 0.7 fusion.15
  5.7 3.8 %fusion.2 = f32[256,4224]{1,0:T(8,128)} fusion(f32[64,1]{1,0:T(8,128)S(1)} %copy.34, f32[64,4096]{1,0:T(8,128)S(1)} %reshape.110, s32[64]{0:T(128)S(1)} %multiply_add_fusion), kind=kOutput, calls=%fused_computation.7 | convolution fusion | flops 831299584 | bytes 5374464 | tf_op jit(solution)/shard_map/dot_general | solution.py:287
  9.5 6.0 %reshape.112 = f32[128,2,4224]{2,1,0:T(2,128)} reshape(f32[256,4224]{1,0:T(8,128)} %fusion.2) | data formatting | bytes 8650752 | tf_op jit(solution)/shard_map/reshape | solution.py:248
  15.5 11.0 %all-to-all-start = ((f32[128,2,4224]{2,1,0:T(2,128)}), f32[128,2,4224]{2,1,0:T(2,128)}, u32[]{:S(2)}, u32[]{:S(2)}) async-start(f32[128,2,4224]{2,1,0:T(2,128)} %reshape.112), calls=%async_computation | async-start | bytes 8650752 | tf_op jit(solution)/shard_map/all_to_all | solution.py:247
  26.9 2.1 add_sqrt_fusion
  29.2 2.3 collective-permute-start.4
  31.5 6.9 %collective-permute-start.5 = (f32[4,16,256]{1,2,0:T(8,128)S(1)}, f32[4,16,256]{1,2,0:T(8,128)S(1)}, u32[]{:S(2)}, u32[]{:S(2)}) collective-permute-start(f32[4,16,256]{1,2,0:T(8,128)S(1)} %get-tuple-element.34), channel_id=1, source_target_pairs={{0,1},{1,2},{2,3},{3,4},{4,5},{5,6},{6,7},{7,8},{8,9},{9,10},{10,1... | collective-permute-start | bytes 196616 | tf_op jit(solution)/shard_map/ppermute | solution.py:72
  38.6 1.9 collective-permute-start
  40.5 7.3 %collective-permute-start.1 = (f32[4,16,256]{1,2,0:T(8,128)S(1)}, f32[4,16,256]{1,2,0:T(8,128)S(1)}, u32[]{:S(2)}, u32[]{:S(2)}) collective-permute-start(f32[4,16,256]{1,2,0:T(8,128)S(1)} %get-tuple-element.36), channel_id=1, source_target_pairs={{0,1},{1,2},{2,3},{3,4},{4,5},{5,6},{6,7},{7,8},{8,9},{9,10},{10,1... | collective-permute-start | bytes 196616 | tf_op jit(solution)/shard_map/ppermute | solution.py:72
  47.8 0.8 slice_bitcast_fusion.5
  48.5 1.9 collective-permute-start.12
  51.2 0.7 constant_dynamic-update-slice_fusion.4
  51.8 31.4 %collective-permute-done.4 = f32[4,16,256]{1,2,0:T(8,128)S(1)} collective-permute-done((f32[4,16,256]{1,2,0:T(8,128)S(1)}, f32[4,16,256]{1,2,0:T(8,128)S(1)}, u32[]{:S(2)}, u32[]{:S(2)}) %collective-permute-start.4) | collective-permute-done | bytes 65568 | tf_op jit(solution)/shard_map/ppermute | solution.py:75
  83.2 1.9 collective-permute-start.13
  85.2 3.7 %collective-permute-done = f32[4,16,256]{1,2,0:T(8,128)S(1)} collective-permute-done((f32[4,16,256]{1,2,0:T(8,128)S(1)}, f32[4,16,256]{1,2,0:T(8,128)S(1)}, u32[]{:S(2)}, u32[]{:S(2)}) %collective-permute-start) | collective-permute-done | bytes 65568 | tf_op jit(solution)/shard_map/ppermute | solution.py:75
  88.9 0.8 pad_maximum_fusion.1
  89.7 4.7 %collective-permute-start.6 = (f32[4,16,640]{2,1,0:T(8,128)S(1)}, f32[4,16,640]{2,1,0:T(8,128)S(1)}, u32[]{:S(2)}, u32[]{:S(2)}) collective-permute-start(f32[4,16,640]{2,1,0:T(8,128)S(1)} %get-tuple-element.30), channel_id=1, source_target_pairs={{0,16},{16,32},{32,48},{48,64},{64,80},{80,96},{96,112},{1,17},{17... | collective-permute-start | bytes 491528 | tf_op jit(solution)/shard_map/ppermute | solution.py:80
  94.4 3.2 %collective-permute-start.7 = (f32[4,16,640]{2,1,0:T(8,128)S(1)}, f32[4,16,640]{2,1,0:T(8,128)S(1)}, u32[]{:S(2)}, u32[]{:S(2)}) collective-permute-start(f32[4,16,640]{2,1,0:T(8,128)S(1)} %get-tuple-element.29), channel_id=1, source_target_pairs={{16,0},{32,16},{48,32},{64,48},{80,64},{96,80},{112,96},{17,1},{33... | collective-permute-start | bytes 491528 | tf_op jit(solution)/shard_map/ppermute | solution.py:81
  97.7 2.0 collective-permute-start.2
  99.8 3.4 %collective-permute-start.3 = (f32[4,16,640]{2,1,0:T(8,128)S(1)}, f32[4,16,640]{2,1,0:T(8,128)S(1)}, u32[]{:S(2)}, u32[]{:S(2)}) collective-permute-start(f32[4,16,640]{2,1,0:T(8,128)S(1)} %get-tuple-element.31), channel_id=1, source_target_pairs={{16,0},{32,16},{48,32},{64,48},{80,64},{96,80},{112,96},{17,1},{33... | collective-permute-start | bytes 491528 | tf_op jit(solution)/shard_map/ppermute | solution.py:81
  104.1 1.1 constant_dynamic-update-slice_fusion.3
  105.2 1.7 constant_dynamic-update-slice_fusion.2
  106.9 0.7 constant_dynamic-update-slice_fusion.1
  107.6 0.7 constant_dynamic-update-slice_fusion.f_ref
  108.2 6.2 %reshape.113 = f32[256,4224]{1,0:T(8,128)} reshape(f32[128,2,4224]{2,1,0:T(2,128)} %all-to-all-done) | data formatting | bytes 8650752 | tf_op jit(solution)/shard_map/reshape | solution.py:254
  114.5 1.0 fusion.8
  115.5 3.8 %fusion = f32[32,4096]{1,0:T(8,128)S(1)} fusion(f32[256,4224]{1,0:T(8,128)} %reshape.113, s32[256]{0:T(256)S(1)} %fusion.8), kind=kOutput, calls=%fused_computation.1 | convolution fusion | flops 402661376 | bytes 4719616 | tf_op jit(solution)/shard_map/dot_general | solution.py:293
  120.7 2.1 collective-permute-start.8
  122.8 7.3 %collective-permute-start.9 = (f32[1,16,256]{1,2,0:T(8,128)S(1)}, f32[1,16,256]{1,2,0:T(8,128)S(1)}, u32[]{:S(2)}, u32[]{:S(2)}) collective-permute-start(f32[1,16,256]{1,2,0:T(8,128)S(1)} %get-tuple-element.44), channel_id=1, source_target_pairs={{0,1},{1,2},{2,3},{3,4},{4,5},{5,6},{6,7},{7,8},{8,9},{9,10},{10,1... | collective-permute-start | bytes 49160 | tf_op jit(solution)/shard_map/ppermute | solution.py:72
  130.8 1.2 collective-permute-done.9
  132.0 1.1 pad_maximum_fusion.3
  133.1 2.2 collective-permute-start.14
  135.4 3.1 %collective-permute-start.15 = (f32[1,16,640]{2,1,0:T(8,128)S(1)}, f32[1,16,640]{2,1,0:T(8,128)S(1)}, u32[]{:S(2)}, u32[]{:S(2)}) collective-permute-start(f32[1,16,640]{2,1,0:T(8,128)S(1)} %get-tuple-element.37), channel_id=1, source_target_pairs={{16,0},{32,16},{48,32},{64,48},{80,64},{96,80},{112,96},{17,1},{33... | collective-permute-start | bytes 122888 | tf_op jit(solution)/shard_map/ppermute | solution.py:81
  138.5 4.3 %collective-permute-start.10 = (f32[1,16,640]{2,1,0:T(8,128)S(1)}, f32[1,16,640]{2,1,0:T(8,128)S(1)}, u32[]{:S(2)}, u32[]{:S(2)}) collective-permute-start(f32[1,16,640]{2,1,0:T(8,128)S(1)} %get-tuple-element.40), channel_id=1, source_target_pairs={{0,16},{16,32},{32,48},{48,64},{64,80},{80,96},{96,112},{1,17},{17... | collective-permute-start | bytes 122888 | tf_op jit(solution)/shard_map/ppermute | solution.py:80
  142.8 2.1 collective-permute-start.11
  145.2 2.4 collective-permute-done.11
  147.6 0.9 copy-done.4
  148.4 39.8 %shard_map.94 = (f32[4,256,512]{2,1,0:T(8,128)}, f32[4,256,512]{2,1,0:T(8,128)}, f32[256,512]{1,0:T(8,128)}) custom-call(f32[4,304,640]{2,1,0:T(8,128)} %constant_dynamic-update-slice_fusion.f_ref, f32[4,304,640]{2,1,0:T(8,128)} %copy-done.1, f32[304,640]{1,0:T(8,128)} %bitcast.45, f32[304,640]{1,0:T(8,128)} %bitcast.46), custom_call_target="tpu_custom_call" | custom-call | tf_op jit(solution)/shard_map/pallas_call | solution.py:236
  188.2 1.2 reshape.115
  190.0 1.8 fusion.9
  191.8 3.2 %copy.33 = f32[128,2,4096]{2,1,0:T(2,128)S(1)} copy(f32[128,2,4096]{2,0,1:T(8,128)S(1)} %fusion.9) | data formatting | bytes 8388608 | tf_op jit(solution)/shard_map/dot_general | solution.py:310
  195.1 67.4 %all_to_all.10 = f32[128,2,4096]{2,1,0:T(2,128)} all-to-all(f32[128,2,4096]{2,1,0:T(2,128)S(1)} %copy.33), channel_id=1, replica_groups=mesh['row'=8,'col'=16] {'row','col'}, dimensions={0} | all-to-all | bytes 8388608 | tf_op jit(solution)/shard_map/all_to_all | solution.py:258
  262.5 6.1 %reshape.117 = f32[256,4096]{1,0:T(8,128)} reshape(f32[128,2,4096]{2,1,0:T(2,128)} %all_to_all.10) | data formatting | bytes 8388608 | tf_op jit(solution)/shard_map/reshape | solution.py:265
  268.6 3.9 %convolution_multiply_fusion = f32[64,4096]{1,0:T(8,128)S(1)} fusion(f32[256,4096]{1,0:T(8,128)} %reshape.117, s32[64]{0:T(128)S(1)} %multiply_add_fusion), kind=kOutput, calls=%fused_computation | convolution fusion | flops 805584896 | bytes 5243136 | tf_op jit(solution)/shard_map/dot_general | solution.py:312
  272.6 2.2 reshape.118
  (64 shorter events, 5.8 us)
Async XLA Ops:
  0.6 4.3 %copy-start.8 = (s32[64]{0:T(128)S(1)}, s32[64]{0:T(128)}, u32[]{:S(2)}) copy-start(s32[64]{0:T(128)} %param.12) | copy-start | bytes 772
  15.5 11.1 %copy-start.7 = (f32[4,8]{1,0:T(4,128)S(1)}, f32[4,8]{1,0:T(4,128)}, u32[]{:S(2)}) copy-start(f32[4,8]{1,0:T(4,128)} %param.14) | copy-start | bytes 388
  15.5 11.4 %copy-start.2 = (s32[4,256,512]{2,1,0:T(8,128)S(1)}, s32[4,256,512]{2,1,0:T(8,128)}, u32[]{:S(2)}) copy-start(s32[4,256,512]{2,1,0:T(8,128)} %param.13) | copy-start | bytes 6291460
  15.5 92.8 %all-to-all-start = ((f32[128,2,4224]{2,1,0:T(2,128)}), f32[128,2,4224]{2,1,0:T(2,128)}, u32[]{:S(2)}, u32[]{:S(2)}) async-start(f32[128,2,4224]{2,1,0:T(2,128)} %reshape.112), calls=%async_computation | async-start | bytes 8650752 | tf_op jit(solution)/shard_map/all_to_all | solution.py:247
  26.8 11.5 %copy-start = (f32[4,256,512]{2,1,0:T(8,128)S(1)}, f32[4,256,512]{2,1,0:T(8,128)}, u32[]{:S(2)}) copy-start(f32[4,256,512]{2,1,0:T(8,128)} %param.9) | copy-start | bytes 6291460
  29.0 18.8 %copy-start.3 = (f32[256,512]{1,0:T(8,128)S(1)}, f32[256,512]{1,0:T(8,128)}, u32[]{:S(2)}) copy-start(f32[256,512]{1,0:T(8,128)} %param.15) | copy-start | bytes 1572868
  29.2 54.1 %collective-permute-start.4 = (f32[4,16,256]{1,2,0:T(8,128)S(1)}, f32[4,16,256]{1,2,0:T(8,128)S(1)}, u32[]{:S(2)}, u32[]{:S(2)}) collective-permute-start(f32[4,16,256]{1,2,0:T(8,128)S(1)} %get-tuple-element.33), channel_id=1, source_target_pairs={{1,0},{2,1},{3,2},{4,3},{5,4},{6,5},{7,6},{8,7},{9,8},{10,9},{11,1... | collective-permute-start | bytes 196616 | tf_op jit(solution)/shard_map/ppermute | solution.py:75
  31.5 53.7 %collective-permute-start.5 = (f32[4,16,256]{1,2,0:T(8,128)S(1)}, f32[4,16,256]{1,2,0:T(8,128)S(1)}, u32[]{:S(2)}, u32[]{:S(2)}) collective-permute-start(f32[4,16,256]{1,2,0:T(8,128)S(1)} %get-tuple-element.34), channel_id=1, source_target_pairs={{0,1},{1,2},{2,3},{3,4},{4,5},{5,6},{6,7},{7,8},{8,9},{9,10},{10,1... | collective-permute-start | bytes 196616 | tf_op jit(solution)/shard_map/ppermute | solution.py:72
  38.6 50.3 %collective-permute-start = (f32[4,16,256]{1,2,0:T(8,128)S(1)}, f32[4,16,256]{1,2,0:T(8,128)S(1)}, u32[]{:S(2)}, u32[]{:S(2)}) collective-permute-start(f32[4,16,256]{1,2,0:T(8,128)S(1)} %get-tuple-element.35), channel_id=1, source_target_pairs={{1,0},{2,1},{3,2},{4,3},{5,4},{6,5},{7,6},{8,7},{9,8},{10,9},{11,1... | collective-permute-start | bytes 196616 | tf_op jit(solution)/shard_map/ppermute | solution.py:75
  40.5 48.4 %collective-permute-start.1 = (f32[4,16,256]{1,2,0:T(8,128)S(1)}, f32[4,16,256]{1,2,0:T(8,128)S(1)}, u32[]{:S(2)}, u32[]{:S(2)}) collective-permute-start(f32[4,16,256]{1,2,0:T(8,128)S(1)} %get-tuple-element.36), channel_id=1, source_target_pairs={{0,1},{1,2},{2,3},{3,4},{4,5},{5,6},{6,7},{7,8},{8,9},{9,10},{10,1... | collective-permute-start | bytes 196616 | tf_op jit(solution)/shard_map/ppermute | solution.py:72
  48.5 81.7 %collective-permute-start.12 = (f32[1,16,256]{1,2,0:T(8,128)}, f32[1,16,256]{1,2,0:T(8,128)}, u32[]{:S(2)}, u32[]{:S(2)}) collective-permute-start(f32[1,16,256]{1,2,0:T(8,128)} %get-tuple-element.41), channel_id=1, source_target_pairs={{1,0},{2,1},{3,2},{4,3},{5,4},{6,5},{7,6},{8,7},{9,8},{10,9},{11,1... | collective-permute-start | bytes 49160 | tf_op jit(solution)/shard_map/ppermute | solution.py:75
  83.2 47.0 %collective-permute-start.13 = (f32[1,16,256]{1,2,0:T(8,128)}, f32[1,16,256]{1,2,0:T(8,128)}, u32[]{:S(2)}, u32[]{:S(2)}) collective-permute-start(f32[1,16,256]{1,2,0:T(8,128)} %get-tuple-element.42), channel_id=1, source_target_pairs={{0,1},{1,2},{2,3},{3,4},{4,5},{5,6},{6,7},{7,8},{8,9},{9,10},{10,1... | collective-permute-start | bytes 49160 | tf_op jit(solution)/shard_map/ppermute | solution.py:72
  89.7 10.1 %collective-permute-start.6 = (f32[4,16,640]{2,1,0:T(8,128)S(1)}, f32[4,16,640]{2,1,0:T(8,128)S(1)}, u32[]{:S(2)}, u32[]{:S(2)}) collective-permute-start(f32[4,16,640]{2,1,0:T(8,128)S(1)} %get-tuple-element.30), channel_id=1, source_target_pairs={{0,16},{16,32},{32,48},{48,64},{64,80},{80,96},{96,112},{1,17},{17... | collective-permute-start | bytes 491528 | tf_op jit(solution)/shard_map/ppermute | solution.py:80
  94.4 9.0 %collective-permute-start.7 = (f32[4,16,640]{2,1,0:T(8,128)S(1)}, f32[4,16,640]{2,1,0:T(8,128)S(1)}, u32[]{:S(2)}, u32[]{:S(2)}) collective-permute-start(f32[4,16,640]{2,1,0:T(8,128)S(1)} %get-tuple-element.29), channel_id=1, source_target_pairs={{16,0},{32,16},{48,32},{64,48},{80,64},{96,80},{112,96},{17,1},{33... | collective-permute-start | bytes 491528 | tf_op jit(solution)/shard_map/ppermute | solution.py:81
  97.7 6.4 %collective-permute-start.2 = (f32[4,16,640]{2,1,0:T(8,128)S(1)}, f32[4,16,640]{2,1,0:T(8,128)S(1)}, u32[]{:S(2)}, u32[]{:S(2)}) collective-permute-start(f32[4,16,640]{2,1,0:T(8,128)S(1)} %get-tuple-element.32), channel_id=1, source_target_pairs={{0,16},{16,32},{32,48},{48,64},{64,80},{80,96},{96,112},{1,17},{17... | collective-permute-start | bytes 491528 | tf_op jit(solution)/shard_map/ppermute | solution.py:80
  99.8 7.1 %collective-permute-start.3 = (f32[4,16,640]{2,1,0:T(8,128)S(1)}, f32[4,16,640]{2,1,0:T(8,128)S(1)}, u32[]{:S(2)}, u32[]{:S(2)}) collective-permute-start(f32[4,16,640]{2,1,0:T(8,128)S(1)} %get-tuple-element.31), channel_id=1, source_target_pairs={{16,0},{32,16},{48,32},{64,48},{80,64},{96,80},{112,96},{17,1},{33... | collective-permute-start | bytes 491528 | tf_op jit(solution)/shard_map/ppermute | solution.py:81
  103.5 3.4 %copy-start.1 = (f32[4,304,640]{2,1,0:T(8,128)}, f32[4,304,640]{2,1,0:T(8,128)S(1)}, u32[]{:S(2)}) copy-start(f32[4,304,640]{2,1,0:T(8,128)S(1)} %constant_dynamic-update-slice_fusion.5.r_ref) | copy-start | bytes 9338884
  120.6 24.3 %copy-start.5 = (f32[1,304,640]{2,1,0:T(8,128)S(1)}, f32[1,304,640]{2,1,0:T(8,128)}, u32[]{:S(2)}) copy-start(f32[1,304,640]{2,1,0:T(8,128)} %constant_dynamic-update-slice_fusion.19) | copy-start | bytes 2334724
  120.7 10.0 %collective-permute-start.8 = (f32[1,16,256]{1,2,0:T(8,128)S(1)}, f32[1,16,256]{1,2,0:T(8,128)S(1)}, u32[]{:S(2)}, u32[]{:S(2)}) collective-permute-start(f32[1,16,256]{1,2,0:T(8,128)S(1)} %get-tuple-element.43), channel_id=1, source_target_pairs={{1,0},{2,1},{3,2},{4,3},{5,4},{6,5},{7,6},{8,7},{9,8},{10,9},{11,1... | collective-permute-start | bytes 49160 | tf_op jit(solution)/shard_map/ppermute | solution.py:75
  122.8 9.2 %collective-permute-start.9 = (f32[1,16,256]{1,2,0:T(8,128)S(1)}, f32[1,16,256]{1,2,0:T(8,128)S(1)}, u32[]{:S(2)}, u32[]{:S(2)}) collective-permute-start(f32[1,16,256]{1,2,0:T(8,128)S(1)} %get-tuple-element.44), channel_id=1, source_target_pairs={{0,1},{1,2},{2,3},{3,4},{4,5},{5,6},{6,7},{7,8},{8,9},{9,10},{10,1... | collective-permute-start | bytes 49160 | tf_op jit(solution)/shard_map/ppermute | solution.py:72
  133.1 11.8 %collective-permute-start.14 = (f32[1,16,640]{2,1,0:T(8,128)S(1)}, f32[1,16,640]{2,1,0:T(8,128)S(1)}, u32[]{:S(2)}, u32[]{:S(2)}) collective-permute-start(f32[1,16,640]{2,1,0:T(8,128)S(1)} %get-tuple-element.38), channel_id=1, source_target_pairs={{0,16},{16,32},{32,48},{48,64},{64,80},{80,96},{96,112},{1,17},{17... | collective-permute-start | bytes 122888 | tf_op jit(solution)/shard_map/ppermute | solution.py:80
  135.4 9.7 %collective-permute-start.15 = (f32[1,16,640]{2,1,0:T(8,128)S(1)}, f32[1,16,640]{2,1,0:T(8,128)S(1)}, u32[]{:S(2)}, u32[]{:S(2)}) collective-permute-start(f32[1,16,640]{2,1,0:T(8,128)S(1)} %get-tuple-element.37), channel_id=1, source_target_pairs={{16,0},{32,16},{48,32},{64,48},{80,64},{96,80},{112,96},{17,1},{33... | collective-permute-start | bytes 122888 | tf_op jit(solution)/shard_map/ppermute | solution.py:81
  138.5 6.6 %collective-permute-start.10 = (f32[1,16,640]{2,1,0:T(8,128)S(1)}, f32[1,16,640]{2,1,0:T(8,128)S(1)}, u32[]{:S(2)}, u32[]{:S(2)}) collective-permute-start(f32[1,16,640]{2,1,0:T(8,128)S(1)} %get-tuple-element.40), channel_id=1, source_target_pairs={{0,16},{16,32},{32,48},{48,64},{64,80},{80,96},{96,112},{1,17},{17... | collective-permute-start | bytes 122888 | tf_op jit(solution)/shard_map/ppermute | solution.py:80
  142.8 4.7 %collective-permute-start.11 = (f32[1,16,640]{2,1,0:T(8,128)S(1)}, f32[1,16,640]{2,1,0:T(8,128)S(1)}, u32[]{:S(2)}, u32[]{:S(2)}) collective-permute-start(f32[1,16,640]{2,1,0:T(8,128)S(1)} %get-tuple-element.39), channel_id=1, source_target_pairs={{16,0},{32,16},{48,32},{64,48},{80,64},{96,80},{112,96},{17,1},{33... | collective-permute-start | bytes 122888 | tf_op jit(solution)/shard_map/ppermute | solution.py:81
  145.2 2.4 copy-start.6
  147.6 0.9 copy-start.4

commit v8 on v7

--- a/solution.py
+++ b/solution.py
@@ -69,22 +69,41 @@
     depth, height, breadth = cells.shape
     cols = lax.axis_size("col")
     rows = lax.axis_size("row")
+    both = ("row", "col")
+
+    def diagonal(block, dr, dc):
+        pairs = [
+            ((r - dr) * cols + (c - dc), r * cols + c)
+            for r in range(max(dr, 0), rows + min(dr, 0))
+            for c in range(max(dc, 0), cols + min(dc, 0))
+        ]
+        return lax.ppermute(block, both, pairs)
+
+    last_rows = cells[:, height - HALO :]
+    first_rows = cells[:, :HALO]
+    top = lax.ppermute(last_rows, "row", [(i, i + 1) for i in range(rows - 1)])
+    bottom = lax.ppermute(first_rows, "row", [(i + 1, i) for i in range(rows - 1)])
     left = lax.ppermute(
         jnp.swapaxes(cells[:, :, breadth - HALO :], 1, 2), "col", [(i, i + 1) for i in range(cols - 1)]
     )
     right = lax.ppermute(jnp.swapaxes(cells[:, :, :HALO], 1, 2), "col", [(i + 1, i) for i in range(cols - 1)])
-    left = jnp.swapaxes(left, 1, 2)
-    right = jnp.swapaxes(right, 1, 2)
-    gap = jnp.zeros((depth, height, LANE - 2 * HALO), cells.dtype)
-    band = jnp.concatenate([cells, right, gap, left], axis=2)
-    top = lax.ppermute(band[:, height - HALO :], "row", [(i, i + 1) for i in range(rows - 1)])
-    bottom = lax.ppermute(band[:, :HALO], "row", [(i + 1, i) for i in range(rows - 1)])
+    top_left = diagonal(last_rows[:, :, breadth - HALO :], 1, 1)
+    top_right = diagonal(last_rows[:, :, :HALO], 1, -1)
+    bottom_left = diagonal(first_rows[:, :, breadth - HALO :], -1, 1)
+    bottom_right = diagonal(first_rows[:, :, :HALO], -1, -1)
+
+    def gap(count):
+        return jnp.zeros((depth, count, LANE - 2 * HALO), cells.dtype)
+
+    band = jnp.concatenate([cells, jnp.swapaxes(right, 1, 2), gap(height), jnp.swapaxes(left, 1, 2)], axis=2)
+    upper = jnp.concatenate([top, top_right, gap(HALO), top_left], axis=2)
+    lower = jnp.concatenate([bottom, bottom_right, gap(HALO), bottom_left], axis=2)
     pad = jnp.zeros((depth, SLACK, band.shape[2]), cells.dtype)
-    return jnp.concatenate([pad, top, band, bottom, pad], axis=1)
-
-
-def chunk_loop(count, body):
-    lax.fori_loop(0, count, lambda c, carry: (body(c), carry)[1], 0, unroll=9)
+    return jnp.concatenate([pad, upper, band, lower, pad], axis=1)
+
+
+def chunk_loop(count, body, unroll=1):
+    lax.fori_loop(0, count, lambda c, carry: (body(c), carry)[1], 0, unroll=unroll)
 
 
 def conductances(r_ref, cu, cd, cl, cr, dg, cv):
@@ -156,7 +175,7 @@
             dst[l, rows, :] = value
             lower = upper
 
-    chunk_loop(count, body)
+    chunk_loop(count, body, 6)
 
 
 def clear_slack(buf):

time: 279 us -> 344 us (1.23)
  starting transfers between devices: 67.7 us -> 145 us
  waiting for transfers between devices: 39.9 us -> 24.5 us
  other arithmetic: 7.91 us -> 13.2 us
  blocking collectives: 67.4 us -> 63.3 us
    ppermute x8 -> x24, starting transfers between devices: 25.2 us -> 99.3 us  [the longest x16 74.7 us: diagonal(): return lax.ppermute(block, both, pairs)]
    ppermute x4, waiting for transfers between devices: 35.6 us -> 0.01 us  [framed(): lax.ppermute(jnp.swapaxes(cells[:, :, :HALO], 1, 2), 'col', [(i + 1, i) f...]
    ppermute x8 -> x24, waiting for transfers between devices: 3.01 us -> 24.5 us  [the longest x16 24.5 us: diagonal(): return lax.ppermute(block, both, pairs)]
    unnamed x0 -> x6, other arithmetic: none -> 7.92 us
    unnamed x35 -> x15, local copies, waits for them, and re-layouts: 6.09 us -> 1.72 us
    all_to_all x1, blocking collectives: 67.4 us -> 63.3 us  [return_grads(): lax.all_to_all(backward.reshape(row_count * col_count, CAP, -1), ('row',...]
  transfers between devices with their start and end apart: 17 -> 33, of which waited for: 6 -> 3; matrix products, arithmetic and copies ran while one was open for 8% -> 8% of each run, Pallas kernels for 0% -> 0%
where the time goes in v8:
time: 344 us; the launch traced here: 339 us
  starting transfers between devices  145 us (42%)
  blocking collectives  63.3 us (18%)
  Pallas kernels  43.1 us (13%)
  local copies, waits for them, and re-layouts  35.3 us (10%)
  waiting for transfers between devices  24.5 us (7%)
  matrix products  13.4 us (4%)
  other arithmetic  13.2 us (4%)
    ppermute x16, starting transfers between devices, diagonal(): return lax.ppermute(block, both, pairs)  74.7 us
    all_to_all x1, blocking collectives, return_grads(): lax.all_to_all(backward.reshape(row_count * col_count, CAP, -1), ('row',...  63.3 us
    pallas_call x1, Pallas kernels, run_solve(): pl.pallas_call(solve_kernel, out_shape=(field, field, jax.ShapeDtypeStruc...  43.1 us
    ppermute x4, starting transfers between devices, framed(): lax.ppermute(jnp.swapaxes(cells[:, :, breadth - HALO:], 1, 2), 'col', [(i...  26.2 us
    ppermute x16, waiting for transfers between devices, diagonal(): return lax.ppermute(block, both, pairs)  24.5 us
    ppermute x4, starting transfers between devices, framed(): top = lax.ppermute(last_rows, 'row', [(i, i + 1) for i in range(rows - 1)])  16.8 us
    all_to_all x1, starting transfers between devices, send_dies(): lax.all_to_all(outbound.reshape(row_count * col_count, CAP, -1), ('row',...  11 us
    ppermute x4, starting transfers between devices, framed(): lax.ppermute(jnp.swapaxes(cells[:, :, :HALO], 1, 2), 'col', [(i + 1, i) f...  8.17 us
  transfers between devices with their start and end apart: 33, of which 3 were waited for; matrix products, arithmetic and copies ran while one was open for 8% of the time, Pallas kernels for 0%

profile of v8, /device:TPU:15, one launch (start us, length us, event | category | flops | bytes accessed | tf_op | source)
XLA Modules:
  0.0 338.7 jit_solution(6872510860252517420)
XLA Ops:
  2.7 2.1 reshape.110
  4.9 3.9 %fusion.2 = f32[256,4224]{1,0:T(8,128)} fusion(f32[64,1]{1,0:T(8,128)S(1)} %copy.34, f32[64,4096]{1,0:T(8,128)S(1)} %reshape.110, s32[64]{0:T(128)S(1)} %multiply_add_fusion), kind=kOutput, calls=%fused_computation.7 | convolution fusion | flops 831299584 | bytes 5374464 | tf_op jit(solution)/shard_map/dot_general | solution.py:306
  8.8 6.0 %reshape.112 = f32[128,2,4224]{2,1,0:T(2,128)} reshape(f32[256,4224]{1,0:T(8,128)} %fusion.2) | data formatting | bytes 8650752 | tf_op jit(solution)/shard_map/reshape | solution.py:267
  14.8 11.0 %all-to-all-start = ((f32[128,2,4224]{2,1,0:T(2,128)}), f32[128,2,4224]{2,1,0:T(2,128)}, u32[]{:S(2)}, u32[]{:S(2)}) async-start(f32[128,2,4224]{2,1,0:T(2,128)} %reshape.112), calls=%async_computation | async-start | bytes 8650752 | tf_op jit(solution)/shard_map/all_to_all | solution.py:266
  26.2 2.1 add_sqrt_fusion
  28.4 6.3 %collective-permute-start.10 = (f32[4,16,16]{2,1,0:T(8,128)S(1)}, f32[4,16,16]{2,1,0:T(8,128)S(1)}, u32[]{:S(2)}, u32[]{:S(2)}) collective-permute-start(f32[4,16,16]{2,1,0:T(8,128)S(1)} %get-tuple-element.33), channel_id=1, source_target_pairs={{0,17},{1,18},{2,19},{3,20},{4,21},{5,22},{6,23},{7,24},{8,25},{9,... | collective-permute-start | bytes 12296 | tf_op jit(solution)/shard_map/ppermute | solution.py:80
  34.7 1.9 collective-permute-start.9
  36.6 2.9 collective-permute-start.8
  39.6 7.7 %collective-permute-start.2 = (f32[4,16,16]{2,1,0:T(8,128)S(1)}, f32[4,16,16]{2,1,0:T(8,128)S(1)}, u32[]{:S(2)}, u32[]{:S(2)}) collective-permute-start(f32[4,16,16]{2,1,0:T(8,128)S(1)} %get-tuple-element.40), channel_id=1, source_target_pairs={{0,17},{1,18},{2,19},{3,20},{4,21},{5,22},{6,23},{7,24},{8,25},{9,... | collective-permute-start | bytes 12296 | tf_op jit(solution)/shard_map/ppermute | solution.py:80
  47.3 4.7 %collective-permute-start = (f32[4,16,512]{2,1,0:T(8,128)S(1)}, f32[4,16,512]{2,1,0:T(8,128)S(1)}, u32[]{:S(2)}, u32[]{:S(2)}) collective-permute-start(f32[4,16,512]{2,1,0:T(8,128)S(1)} %get-tuple-element.38), channel_id=1, source_target_pairs={{0,16},{16,32},{32,48},{48,64},{64,80},{80,96},{96,112},{1,17},{17... | collective-permute-start | bytes 393224 | tf_op jit(solution)/shard_map/ppermute | solution.py:84
  54.5 19.7 %collective-permute-done.10 = f32[4,16,16]{2,1,0:T(8,128)S(1)} collective-permute-done((f32[4,16,16]{2,1,0:T(8,128)S(1)}, f32[4,16,16]{2,1,0:T(8,128)S(1)}, u32[]{:S(2)}, u32[]{:S(2)}) %collective-permute-start.10) | collective-permute-done | bytes 4128 | tf_op jit(solution)/shard_map/ppermute | solution.py:80
  74.2 2.2 collective-permute-start.1
  77.2 8.9 %collective-permute-start.12 = (f32[4,16,256]{1,2,0:T(8,128)S(1)}, f32[4,16,256]{1,2,0:T(8,128)S(1)}, u32[]{:S(2)}, u32[]{:S(2)}) collective-permute-start(f32[4,16,256]{1,2,0:T(8,128)S(1)} %get-tuple-element.36), channel_id=1, source_target_pairs={{0,1},{1,2},{2,3},{3,4},{4,5},{5,6},{6,7},{7,8},{8,9},{9,10},{10,1... | collective-permute-start | bytes 196616 | tf_op jit(solution)/shard_map/ppermute | solution.py:86
  86.1 1.9 collective-permute-start.11
  88.0 7.3 %collective-permute-start.4 = (f32[4,16,256]{1,2,0:T(8,128)S(1)}, f32[4,16,256]{1,2,0:T(8,128)S(1)}, u32[]{:S(2)}, u32[]{:S(2)}) collective-permute-start(f32[4,16,256]{1,2,0:T(8,128)S(1)} %get-tuple-element.44), channel_id=1, source_target_pairs={{0,1},{1,2},{2,3},{3,4},{4,5},{5,6},{6,7},{7,8},{8,9},{9,10},{10,1... | collective-permute-start | bytes 196616 | tf_op jit(solution)/shard_map/ppermute | solution.py:86
  95.3 1.9 collective-permute-start.3
  97.3 6.2 %collective-permute-start.15 = (f32[4,16,16]{2,1,0:T(8,128)S(1)}, f32[4,16,16]{2,1,0:T(8,128)S(1)}, u32[]{:S(2)}, u32[]{:S(2)}) collective-permute-start(f32[4,16,16]{2,1,0:T(8,128)S(1)} %get-tuple-element.32), channel_id=1, source_target_pairs={{16,1},{17,2},{18,3},{19,4},{20,5},{21,6},{22,7},{23,8},{24,9},{25... | collective-permute-start | bytes 12296 | tf_op jit(solution)/shard_map/ppermute | solution.py:80
  104.4 1.9 collective-permute-start.14
  106.4 1.9 collective-permute-start.13
  108.3 7.6 %collective-permute-start.7 = (f32[4,16,16]{2,1,0:T(8,128)S(1)}, f32[4,16,16]{2,1,0:T(8,128)S(1)}, u32[]{:S(2)}, u32[]{:S(2)}) collective-permute-start(f32[4,16,16]{2,1,0:T(8,128)S(1)} %get-tuple-element.42), channel_id=1, source_target_pairs={{16,1},{17,2},{18,3},{19,4},{20,5},{21,6},{22,7},{23,8},{24,9},{25... | collective-permute-start | bytes 12296 | tf_op jit(solution)/shard_map/ppermute | solution.py:80
  115.9 1.9 collective-permute-start.6
  117.9 1.9 collective-permute-start.5
  119.8 3.1 maximum_dynamic-update-slice_fusion.1
  122.9 8.1 %collective-permute-start.26 = (f32[1,16,16]{2,1,0:T(8,128)}, f32[1,16,16]{2,1,0:T(8,128)S(1)}, u32[]{:S(2)}, u32[]{:S(2)}) collective-permute-start(f32[1,16,16]{2,1,0:T(8,128)} %get-tuple-element.49), channel_id=1, source_target_pairs={{0,17},{1,18},{2,19},{3,20},{4,21},{5,22},{6,23},{7,24},{8,25},{9,... | collective-permute-start | bytes 3080 | tf_op jit(solution)/shard_map/ppermute | solution.py:80
  131.0 1.9 collective-permute-start.25
  133.0 5.8 %collective-permute-start.24 = (f32[1,16,512]{2,1,0:T(8,128)S(1)}, f32[1,16,512]{2,1,0:T(8,128)}, u32[]{:S(2)}, u32[]{:S(2)}) collective-permute-start(f32[1,16,512]{2,1,0:T(8,128)S(1)} %get-tuple-element.46), channel_id=1, source_target_pairs={{0,16},{16,32},{32,48},{48,64},{64,80},{80,96},{96,112},{1,17},{17... | collective-permute-start | bytes 98312 | tf_op jit(solution)/shard_map/ppermute | solution.py:84
  140.9 6.2 %reshape.113 = f32[256,4224]{1,0:T(8,128)} reshape(f32[128,2,4224]{2,1,0:T(2,128)} %all-to-all-done) | data formatting | bytes 8650752 | tf_op jit(solution)/shard_map/reshape | solution.py:273
  148.2 3.8 %fusion = f32[32,4096]{1,0:T(8,128)S(1)} fusion(f32[256,4224]{1,0:T(8,128)} %reshape.113, s32[256]{0:T(256)S(1)} %fusion.8), kind=kOutput, calls=%fused_computation.1 | convolution fusion | flops 402661376 | bytes 4719616 | tf_op jit(solution)/shard_map/dot_general | solution.py:312
  153.5 10.7 %collective-permute-start.18 = (f32[1,16,16]{2,1,0:T(8,128)S(1)}, f32[1,16,16]{2,1,0:T(8,128)S(1)}, u32[]{:S(2)}, u32[]{:S(2)}) collective-permute-start(f32[1,16,16]{2,1,0:T(8,128)S(1)} %get-tuple-element.57), channel_id=1, source_target_pairs={{0,17},{1,18},{2,19},{3,20},{4,21},{5,22},{6,23},{7,24},{8,25},{9,... | collective-permute-start | bytes 3080 | tf_op jit(solution)/shard_map/ppermute | solution.py:80
  164.3 1.9 collective-permute-start.17
  166.2 3.5 %collective-permute-start.16 = (f32[1,16,512]{2,1,0:T(8,128)S(1)}, f32[1,16,512]{2,1,0:T(8,128)S(1)}, u32[]{:S(2)}, u32[]{:S(2)}) collective-permute-start(f32[1,16,512]{2,1,0:T(8,128)S(1)} %get-tuple-element.54), channel_id=1, source_target_pairs={{0,16},{16,32},{32,48},{48,64},{64,80},{80,96},{96,112},{1,17},{17... | collective-permute-start | bytes 98312 | tf_op jit(solution)/shard_map/ppermute | solution.py:84
  169.9 8.1 %collective-permute-start.28 = (f32[1,16,256]{1,2,0:T(8,128)}, f32[1,16,256]{1,2,0:T(8,128)S(1)}, u32[]{:S(2)}, u32[]{:S(2)}) collective-permute-start(f32[1,16,256]{1,2,0:T(8,128)} %get-tuple-element.52), channel_id=1, source_target_pairs={{0,1},{1,2},{2,3},{3,4},{4,5},{5,6},{6,7},{7,8},{8,9},{9,10},{10,1... | collective-permute-start | bytes 49160 | tf_op jit(solution)/shard_map/ppermute | solution.py:86
  178.0 1.9 collective-permute-start.27
  179.9 7.6 %collective-permute-start.31 = (f32[1,16,16]{2,1,0:T(8,128)}, f32[1,16,16]{2,1,0:T(8,128)S(1)}, u32[]{:S(2)}, u32[]{:S(2)}) collective-permute-start(f32[1,16,16]{2,1,0:T(8,128)} %get-tuple-element.48), channel_id=1, source_target_pairs={{16,1},{17,2},{18,3},{19,4},{20,5},{21,6},{22,7},{23,8},{24,9},{25... | collective-permute-start | bytes 3080 | tf_op jit(solution)/shard_map/ppermute | solution.py:80
  187.6 1.9 collective-permute-start.20
  189.5 2.4 collective-permute-start.19
  193.4 1.9 collective-permute-start.30
  195.3 1.9 collective-permute-start.29
  197.2 4.9 %collective-permute-start.23 = (f32[1,16,16]{2,1,0:T(8,128)S(1)}, f32[1,16,16]{2,1,0:T(8,128)S(1)}, u32[]{:S(2)}, u32[]{:S(2)}) collective-permute-start(f32[1,16,16]{2,1,0:T(8,128)S(1)} %get-tuple-element.56), channel_id=1, source_target_pairs={{16,1},{17,2},{18,3},{19,4},{20,5},{21,6},{22,7},{23,8},{24,9},{25... | collective-permute-start | bytes 3080 | tf_op jit(solution)/shard_map/ppermute | solution.py:80
  202.1 1.9 collective-permute-start.22
  204.1 1.9 collective-permute-start.21
  207.0 4.6 %collective-permute-done.22 = f32[1,16,16]{2,1,0:T(8,128)S(1)} collective-permute-done((f32[1,16,16]{2,1,0:T(8,128)S(1)}, f32[1,16,16]{2,1,0:T(8,128)S(1)}, u32[]{:S(2)}, u32[]{:S(2)}) %collective-permute-start.22) | collective-permute-done | bytes 1056 | tf_op jit(solution)/shard_map/ppermute | solution.py:80
  213.2 43.1 %shard_map.94 = (f32[4,256,512]{2,1,0:T(8,128)}, f32[4,256,512]{2,1,0:T(8,128)}, f32[256,512]{1,0:T(8,128)}) custom-call(f32[4,304,640]{2,1,0:T(8,128)} %constant_dynamic-update-slice_fusion.f_ref, f32[4,304,640]{2,1,0:T(8,128)} %constant_dynamic-update-slice_fusion.2.r_ref, f32[304,640]{1,0:T(8,128)} %bitcast.47, f32[304,640]{1,0:T(8,128)} %bitcast.48), custom_call_target="tpu_custom_call" | custom-call | tf_op jit(solution)/shard_map/pallas_call | solution.py:255
  259.9 3.2 copy.33
  263.1 63.3 %all_to_all.10 = f32[128,2,4096]{2,1,0:T(2,128)} all-to-all(f32[128,2,4096]{2,1,0:T(2,128)S(1)} %copy.33), channel_id=1, replica_groups=mesh['row'=8,'col'=16] {'row','col'}, dimensions={0} | all-to-all | bytes 8388608 | tf_op jit(solution)/shard_map/all_to_all | solution.py:277
  326.5 6.2 %reshape.117 = f32[256,4096]{1,0:T(8,128)} reshape(f32[128,2,4096]{2,1,0:T(2,128)} %all_to_all.10) | data formatting | bytes 8388608 | tf_op jit(solution)/shard_map/reshape | solution.py:284
  332.6 3.9 %convolution_multiply_fusion = f32[64,4096]{1,0:T(8,128)S(1)} fusion(f32[256,4096]{1,0:T(8,128)} %reshape.117, s32[64]{0:T(128)S(1)} %multiply_add_fusion), kind=kOutput, calls=%fused_computation | convolution fusion | flops 805584896 | bytes 5243136 | tf_op jit(solution)/shard_map/dot_general | solution.py:331
  336.6 2.2 reshape.118
  (84 shorter events, 19.4 us)
Async XLA Ops:
  0.6 4.2 %copy-start.5 = (s32[64,1]{0,1:T(1,128)S(1)}, s32[64,1]{0,1:T(1,128)}, u32[]{:S(2)}) copy-start(s32[64,1]{0,1:T(1,128)} %param.11) | copy-start | bytes 772
  14.8 11.1 %copy-start.4 = (f32[4,8]{1,0:T(4,128)S(1)}, f32[4,8]{1,0:T(4,128)}, u32[]{:S(2)}) copy-start(f32[4,8]{1,0:T(4,128)} %param.14) | copy-start | bytes 388
  14.8 11.4 %copy-start.1 = (s32[4,256,512]{2,1,0:T(8,128)S(1)}, s32[4,256,512]{2,1,0:T(8,128)}, u32[]{:S(2)}) copy-start(s32[4,256,512]{2,1,0:T(8,128)} %param.13) | copy-start | bytes 6291460
  14.8 126.2 %all-to-all-start = ((f32[128,2,4224]{2,1,0:T(2,128)}), f32[128,2,4224]{2,1,0:T(2,128)}, u32[]{:S(2)}, u32[]{:S(2)}) async-start(f32[128,2,4224]{2,1,0:T(2,128)} %reshape.112), calls=%async_computation | async-start | bytes 8650752 | tf_op jit(solution)/shard_map/all_to_all | solution.py:266
  25.9 13.6 %copy-start = (f32[4,256,512]{2,1,0:T(8,128)S(1)}, f32[4,256,512]{2,1,0:T(8,128)}, u32[]{:S(2)}) copy-start(f32[4,256,512]{2,1,0:T(8,128)} %param.9) | copy-start | bytes 6291460
  26.2 25.8 %copy-start.2 = (f32[256,512]{1,0:T(8,128)S(1)}, f32[256,512]{1,0:T(8,128)}, u32[]{:S(2)}) copy-start(f32[256,512]{1,0:T(8,128)} %param.15) | copy-start | bytes 1572868
  28.4 45.9 %collective-permute-start.10 = (f32[4,16,16]{2,1,0:T(8,128)S(1)}, f32[4,16,16]{2,1,0:T(8,128)S(1)}, u32[]{:S(2)}, u32[]{:S(2)}) collective-permute-start(f32[4,16,16]{2,1,0:T(8,128)S(1)} %get-tuple-element.33), channel_id=1, source_target_pairs={{0,17},{1,18},{2,19},{3,20},{4,21},{5,22},{6,23},{7,24},{8,25},{9,... | collective-permute-start | bytes 12296 | tf_op jit(solution)/shard_map/ppermute | solution.py:80
  34.7 42.5 %collective-permute-start.9 = (f32[4,16,16]{2,1,0:T(8,128)S(1)}, f32[4,16,16]{2,1,0:T(8,128)S(1)}, u32[]{:S(2)}, u32[]{:S(2)}) collective-permute-start(f32[4,16,16]{2,1,0:T(8,128)S(1)} %get-tuple-element.34), channel_id=1, source_target_pairs={{1,16},{2,17},{3,18},{4,19},{5,20},{6,21},{7,22},{8,23},{9,24},{10... | collective-permute-start | bytes 12296 | tf_op jit(solution)/shard_map/ppermute | solution.py:80
  36.6 58.7 %collective-permute-start.8 = (f32[4,16,512]{2,1,0:T(8,128)S(1)}, f32[4,16,512]{2,1,0:T(8,128)S(1)}, u32[]{:S(2)}, u32[]{:S(2)}) collective-permute-start(f32[4,16,512]{2,1,0:T(8,128)S(1)} %get-tuple-element.30), channel_id=1, source_target_pairs={{0,16},{16,32},{32,48},{48,64},{64,80},{80,96},{96,112},{1,17},{17... | collective-permute-start | bytes 393224 | tf_op jit(solution)/shard_map/ppermute | solution.py:84
  39.6 46.5 %collective-permute-start.2 = (f32[4,16,16]{2,1,0:T(8,128)S(1)}, f32[4,16,16]{2,1,0:T(8,128)S(1)}, u32[]{:S(2)}, u32[]{:S(2)}) collective-permute-start(f32[4,16,16]{2,1,0:T(8,128)S(1)} %get-tuple-element.40), channel_id=1, source_target_pairs={{0,17},{1,18},{2,19},{3,20},{4,21},{5,22},{6,23},{7,24},{8,25},{9,... | collective-permute-start | bytes 12296 | tf_op jit(solution)/shard_map/ppermute | solution.py:80
  47.3 50.0 %collective-permute-start = (f32[4,16,512]{2,1,0:T(8,128)S(1)}, f32[4,16,512]{2,1,0:T(8,128)S(1)}, u32[]{:S(2)}, u32[]{:S(2)}) collective-permute-start(f32[4,16,512]{2,1,0:T(8,128)S(1)} %get-tuple-element.38), channel_id=1, source_target_pairs={{0,16},{16,32},{32,48},{48,64},{64,80},{80,96},{96,112},{1,17},{17... | collective-permute-start | bytes 393224 | tf_op jit(solution)/shard_map/ppermute | solution.py:84
  74.2 13.8 %collective-permute-start.1 = (f32[4,16,16]{2,1,0:T(8,128)S(1)}, f32[4,16,16]{2,1,0:T(8,128)S(1)}, u32[]{:S(2)}, u32[]{:S(2)}) collective-permute-start(f32[4,16,16]{2,1,0:T(8,128)S(1)} %get-tuple-element.41), channel_id=1, source_target_pairs={{1,16},{2,17},{3,18},{4,19},{5,20},{6,21},{7,22},{8,23},{9,24},{10... | collective-permute-start | bytes 12296 | tf_op jit(solution)/shard_map/ppermute | solution.py:80
  77.2 29.2 %collective-permute-start.12 = (f32[4,16,256]{1,2,0:T(8,128)S(1)}, f32[4,16,256]{1,2,0:T(8,128)S(1)}, u32[]{:S(2)}, u32[]{:S(2)}) collective-permute-start(f32[4,16,256]{1,2,0:T(8,128)S(1)} %get-tuple-element.36), channel_id=1, source_target_pairs={{0,1},{1,2},{2,3},{3,4},{4,5},{5,6},{6,7},{7,8},{8,9},{9,10},{10,1... | collective-permute-start | bytes 196616 | tf_op jit(solution)/shard_map/ppermute | solution.py:86
  86.1 22.2 %collective-permute-start.11 = (f32[4,16,256]{1,2,0:T(8,128)S(1)}, f32[4,16,256]{1,2,0:T(8,128)S(1)}, u32[]{:S(2)}, u32[]{:S(2)}) collective-permute-start(f32[4,16,256]{1,2,0:T(8,128)S(1)} %get-tuple-element.35), channel_id=1, source_target_pairs={{1,0},{2,1},{3,2},{4,3},{5,4},{6,5},{7,6},{8,7},{9,8},{10,9},{11,1... | collective-permute-start | bytes 196616 | tf_op jit(solution)/shard_map/ppermute | solution.py:89
  88.0 27.9 %collective-permute-start.4 = (f32[4,16,256]{1,2,0:T(8,128)S(1)}, f32[4,16,256]{1,2,0:T(8,128)S(1)}, u32[]{:S(2)}, u32[]{:S(2)}) collective-permute-start(f32[4,16,256]{1,2,0:T(8,128)S(1)} %get-tuple-element.44), channel_id=1, source_target_pairs={{0,1},{1,2},{2,3},{3,4},{4,5},{5,6},{6,7},{7,8},{8,9},{9,10},{10,1... | collective-permute-start | bytes 196616 | tf_op jit(solution)/shard_map/ppermute | solution.py:86
  95.3 22.6 %collective-permute-start.3 = (f32[4,16,256]{1,2,0:T(8,128)S(1)}, f32[4,16,256]{1,2,0:T(8,128)S(1)}, u32[]{:S(2)}, u32[]{:S(2)}) collective-permute-start(f32[4,16,256]{1,2,0:T(8,128)S(1)} %get-tuple-element.43), channel_id=1, source_target_pairs={{1,0},{2,1},{3,2},{4,3},{5,4},{6,5},{7,6},{8,7},{9,8},{10,9},{11,1... | collective-permute-start | bytes 196616 | tf_op jit(solution)/shard_map/ppermute | solution.py:89
  97.3 7.2 %collective-permute-start.15 = (f32[4,16,16]{2,1,0:T(8,128)S(1)}, f32[4,16,16]{2,1,0:T(8,128)S(1)}, u32[]{:S(2)}, u32[]{:S(2)}) collective-permute-start(f32[4,16,16]{2,1,0:T(8,128)S(1)} %get-tuple-element.32), channel_id=1, source_target_pairs={{16,1},{17,2},{18,3},{19,4},{20,5},{21,6},{22,7},{23,8},{24,9},{25... | collective-permute-start | bytes 12296 | tf_op jit(solution)/shard_map/ppermute | solution.py:80
  104.4 18.4 %collective-permute-start.14 = (f32[4,16,16]{2,1,0:T(8,128)S(1)}, f32[4,16,16]{2,1,0:T(8,128)S(1)}, u32[]{:S(2)}, u32[]{:S(2)}) collective-permute-start(f32[4,16,16]{2,1,0:T(8,128)S(1)} %get-tuple-element.31), channel_id=1, source_target_pairs={{17,0},{18,1},{19,2},{20,3},{21,4},{22,5},{23,6},{24,7},{25,8},{26... | collective-permute-start | bytes 12296 | tf_op jit(solution)/shard_map/ppermute | solution.py:80
  106.4 32.4 %collective-permute-start.13 = (f32[4,16,512]{2,1,0:T(8,128)S(1)}, f32[4,16,512]{2,1,0:T(8,128)S(1)}, u32[]{:S(2)}, u32[]{:S(2)}) collective-permute-start(f32[4,16,512]{2,1,0:T(8,128)S(1)} %get-tuple-element.29), channel_id=1, source_target_pairs={{16,0},{32,16},{48,32},{64,48},{80,64},{96,80},{112,96},{17,1},{33... | collective-permute-start | bytes 393224 | tf_op jit(solution)/shard_map/ppermute | solution.py:85
  108.3 22.7 %collective-permute-start.7 = (f32[4,16,16]{2,1,0:T(8,128)S(1)}, f32[4,16,16]{2,1,0:T(8,128)S(1)}, u32[]{:S(2)}, u32[]{:S(2)}) collective-permute-start(f32[4,16,16]{2,1,0:T(8,128)S(1)} %get-tuple-element.42), channel_id=1, source_target_pairs={{16,1},{17,2},{18,3},{19,4},{20,5},{21,6},{22,7},{23,8},{24,9},{25... | collective-permute-start | bytes 12296 | tf_op jit(solution)/shard_map/ppermute | solution.py:80
  115.9 17.0 %collective-permute-start.6 = (f32[4,16,16]{2,1,0:T(8,128)S(1)}, f32[4,16,16]{2,1,0:T(8,128)S(1)}, u32[]{:S(2)}, u32[]{:S(2)}) collective-permute-start(f32[4,16,16]{2,1,0:T(8,128)S(1)} %get-tuple-element.39), channel_id=1, source_target_pairs={{17,0},{18,1},{19,2},{20,3},{21,4},{22,5},{23,6},{24,7},{25,8},{26... | collective-permute-start | bytes 12296 | tf_op jit(solution)/shard_map/ppermute | solution.py:80
  117.9 20.9 %collective-permute-start.5 = (f32[4,16,512]{2,1,0:T(8,128)S(1)}, f32[4,16,512]{2,1,0:T(8,128)S(1)}, u32[]{:S(2)}, u32[]{:S(2)}) collective-permute-start(f32[4,16,512]{2,1,0:T(8,128)S(1)} %get-tuple-element.37), channel_id=1, source_target_pairs={{16,0},{32,16},{48,32},{64,48},{80,64},{96,80},{112,96},{17,1},{33... | collective-permute-start | bytes 393224 | tf_op jit(solution)/shard_map/ppermute | solution.py:85
  122.9 43.3 %collective-permute-start.26 = (f32[1,16,16]{2,1,0:T(8,128)}, f32[1,16,16]{2,1,0:T(8,128)S(1)}, u32[]{:S(2)}, u32[]{:S(2)}) collective-permute-start(f32[1,16,16]{2,1,0:T(8,128)} %get-tuple-element.49), channel_id=1, source_target_pairs={{0,17},{1,18},{2,19},{3,20},{4,21},{5,22},{6,23},{7,24},{8,25},{9,... | collective-permute-start | bytes 3080 | tf_op jit(solution)/shard_map/ppermute | solution.py:80
  131.0 38.9 %collective-permute-start.25 = (f32[1,16,16]{2,1,0:T(8,128)}, f32[1,16,16]{2,1,0:T(8,128)S(1)}, u32[]{:S(2)}, u32[]{:S(2)}) collective-permute-start(f32[1,16,16]{2,1,0:T(8,128)} %get-tuple-element.50), channel_id=1, source_target_pairs={{1,16},{2,17},{3,18},{4,19},{5,20},{6,21},{7,22},{8,23},{9,24},{10... | collective-permute-start | bytes 3080 | tf_op jit(solution)/shard_map/ppermute | solution.py:80
  133.0 45.0 %collective-permute-start.24 = (f32[1,16,512]{2,1,0:T(8,128)S(1)}, f32[1,16,512]{2,1,0:T(8,128)}, u32[]{:S(2)}, u32[]{:S(2)}) collective-permute-start(f32[1,16,512]{2,1,0:T(8,128)S(1)} %get-tuple-element.46), channel_id=1, source_target_pairs={{0,16},{16,32},{32,48},{48,64},{64,80},{80,96},{96,112},{1,17},{17... | collective-permute-start | bytes 98312 | tf_op jit(solution)/shard_map/ppermute | solution.py:84
  153.5 26.4 %collective-permute-start.18 = (f32[1,16,16]{2,1,0:T(8,128)S(1)}, f32[1,16,16]{2,1,0:T(8,128)S(1)}, u32[]{:S(2)}, u32[]{:S(2)}) collective-permute-start(f32[1,16,16]{2,1,0:T(8,128)S(1)} %get-tuple-element.57), channel_id=1, source_target_pairs={{0,17},{1,18},{2,19},{3,20},{4,21},{5,22},{6,23},{7,24},{8,25},{9,... | collective-permute-start | bytes 3080 | tf_op jit(solution)/shard_map/ppermute | solution.py:80
  164.3 23.3 %collective-permute-start.17 = (f32[1,16,16]{2,1,0:T(8,128)S(1)}, f32[1,16,16]{2,1,0:T(8,128)S(1)}, u32[]{:S(2)}, u32[]{:S(2)}) collective-permute-start(f32[1,16,16]{2,1,0:T(8,128)S(1)} %get-tuple-element.58), channel_id=1, source_target_pairs={{1,16},{2,17},{3,18},{4,19},{5,20},{6,21},{7,22},{8,23},{9,24},{10... | collective-permute-start | bytes 3080 | tf_op jit(solution)/shard_map/ppermute | solution.py:80
  166.2 23.3 %collective-permute-start.16 = (f32[1,16,512]{2,1,0:T(8,128)S(1)}, f32[1,16,512]{2,1,0:T(8,128)S(1)}, u32[]{:S(2)}, u32[]{:S(2)}) collective-permute-start(f32[1,16,512]{2,1,0:T(8,128)S(1)} %get-tuple-element.54), channel_id=1, source_target_pairs={{0,16},{16,32},{32,48},{48,64},{64,80},{80,96},{96,112},{1,17},{17... | collective-permute-start | bytes 98312 | tf_op jit(solution)/shard_map/ppermute | solution.py:84
  169.9 25.4 %collective-permute-start.28 = (f32[1,16,256]{1,2,0:T(8,128)}, f32[1,16,256]{1,2,0:T(8,128)S(1)}, u32[]{:S(2)}, u32[]{:S(2)}) collective-permute-start(f32[1,16,256]{1,2,0:T(8,128)} %get-tuple-element.52), channel_id=1, source_target_pairs={{0,1},{1,2},{2,3},{3,4},{4,5},{5,6},{6,7},{7,8},{8,9},{9,10},{10,1... | collective-permute-start | bytes 49160 | tf_op jit(solution)/shard_map/ppermute | solution.py:86
  178.0 19.2 %collective-permute-start.27 = (f32[1,16,256]{1,2,0:T(8,128)}, f32[1,16,256]{1,2,0:T(8,128)S(1)}, u32[]{:S(2)}, u32[]{:S(2)}) collective-permute-start(f32[1,16,256]{1,2,0:T(8,128)} %get-tuple-element.51), channel_id=1, source_target_pairs={{1,0},{2,1},{3,2},{4,3},{5,4},{6,5},{7,6},{8,7},{9,8},{10,9},{11,1... | collective-permute-start | bytes 49160 | tf_op jit(solution)/shard_map/ppermute | solution.py:89
  179.9 13.4 %collective-permute-start.31 = (f32[1,16,16]{2,1,0:T(8,128)}, f32[1,16,16]{2,1,0:T(8,128)S(1)}, u32[]{:S(2)}, u32[]{:S(2)}) collective-permute-start(f32[1,16,16]{2,1,0:T(8,128)} %get-tuple-element.48), channel_id=1, source_target_pairs={{16,1},{17,2},{18,3},{19,4},{20,5},{21,6},{22,7},{23,8},{24,9},{25... | collective-permute-start | bytes 3080 | tf_op jit(solution)/shard_map/ppermute | solution.py:80
  187.6 14.6 %collective-permute-start.20 = (f32[1,16,256]{1,2,0:T(8,128)S(1)}, f32[1,16,256]{1,2,0:T(8,128)S(1)}, u32[]{:S(2)}, u32[]{:S(2)}) collective-permute-start(f32[1,16,256]{1,2,0:T(8,128)S(1)} %get-tuple-element.60), channel_id=1, source_target_pairs={{0,1},{1,2},{2,3},{3,4},{4,5},{5,6},{6,7},{7,8},{8,9},{9,10},{10,1... | collective-permute-start | bytes 49160 | tf_op jit(solution)/shard_map/ppermute | solution.py:86
  189.5 14.6 %collective-permute-start.19 = (f32[1,16,256]{1,2,0:T(8,128)S(1)}, f32[1,16,256]{1,2,0:T(8,128)S(1)}, u32[]{:S(2)}, u32[]{:S(2)}) collective-permute-start(f32[1,16,256]{1,2,0:T(8,128)S(1)} %get-tuple-element.59), channel_id=1, source_target_pairs={{1,0},{2,1},{3,2},{4,3},{5,4},{6,5},{7,6},{8,7},{9,8},{10,9},{11,1... | collective-permute-start | bytes 49160 | tf_op jit(solution)/shard_map/ppermute | solution.py:89
  193.4 13.6 %collective-permute-start.30 = (f32[1,16,16]{2,1,0:T(8,128)}, f32[1,16,16]{2,1,0:T(8,128)S(1)}, u32[]{:S(2)}, u32[]{:S(2)}) collective-permute-start(f32[1,16,16]{2,1,0:T(8,128)} %get-tuple-element.47), channel_id=1, source_target_pairs={{17,0},{18,1},{19,2},{20,3},{21,4},{22,5},{23,6},{24,7},{25,8},{26... | collective-permute-start | bytes 3080 | tf_op jit(solution)/shard_map/ppermute | solution.py:80
  195.3 11.7 %collective-permute-start.29 = (f32[1,16,512]{2,1,0:T(8,128)S(1)}, f32[1,16,512]{2,1,0:T(8,128)S(1)}, u32[]{:S(2)}, u32[]{:S(2)}) collective-permute-start(f32[1,16,512]{2,1,0:T(8,128)S(1)} %get-tuple-element.45), channel_id=1, source_target_pairs={{16,0},{32,16},{48,32},{64,48},{80,64},{96,80},{112,96},{17,1},{33... | collective-permute-start | bytes 98312 | tf_op jit(solution)/shard_map/ppermute | solution.py:85
  197.2 9.8 %collective-permute-start.23 = (f32[1,16,16]{2,1,0:T(8,128)S(1)}, f32[1,16,16]{2,1,0:T(8,128)S(1)}, u32[]{:S(2)}, u32[]{:S(2)}) collective-permute-start(f32[1,16,16]{2,1,0:T(8,128)S(1)} %get-tuple-element.56), channel_id=1, source_target_pairs={{16,1},{17,2},{18,3},{19,4},{20,5},{21,6},{22,7},{23,8},{24,9},{25... | collective-permute-start | bytes 3080 | tf_op jit(solution)/shard_map/ppermute | solution.py:80
  202.1 9.5 %collective-permute-start.22 = (f32[1,16,16]{2,1,0:T(8,128)S(1)}, f32[1,16,16]{2,1,0:T(8,128)S(1)}, u32[]{:S(2)}, u32[]{:S(2)}) collective-permute-start(f32[1,16,16]{2,1,0:T(8,128)S(1)} %get-tuple-element.55), channel_id=1, source_target_pairs={{17,0},{18,1},{19,2},{20,3},{21,4},{22,5},{23,6},{24,7},{25,8},{26... | collective-permute-start | bytes 3080 | tf_op jit(solution)/shard_map/ppermute | solution.py:80
  204.1 7.5 %collective-permute-start.21 = (f32[1,16,512]{2,1,0:T(8,128)S(1)}, f32[1,16,512]{2,1,0:T(8,128)S(1)}, u32[]{:S(2)}, u32[]{:S(2)}) collective-permute-start(f32[1,16,512]{2,1,0:T(8,128)S(1)} %get-tuple-element.53), channel_id=1, source_target_pairs={{16,0},{32,16},{48,32},{64,48},{80,64},{96,80},{112,96},{17,1},{33... | collective-permute-start | bytes 98312 | tf_op jit(solution)/shard_map/ppermute | solution.py:85
  212.3 0.9 copy-start.3

commit v9 on v7

--- a/solution.py
+++ b/solution.py
@@ -307,9 +307,11 @@
         .transpose(0, 2, 1, 3)
         .reshape(tile_rows * tile_cols, TILE * TILE)
     )
-    backward = jnp.dot(recv_hot.T, grad_tiles, precision=highest)
-    returned = return_grads(backward, row_count, col_count)
-    die_grad = (RATE * jnp.dot(send_hot.T, returned, precision=highest)).reshape(
+    recv_hot = recv_hot.reshape(tile_rows * tile_cols, row_count * col_count, CAP)
+    backward = jnp.einsum("tdc,tn->dcn", recv_hot, grad_tiles, precision=highest)
+    returned = lax.all_to_all(backward, ("row", "col"), split_axis=0, concat_axis=0, tiled=True)
+    send_hot = send_hot.reshape(row_count * col_count, CAP, die_count)
+    die_grad = (RATE * jnp.einsum("dck,dcn->kn", send_hot, returned, precision=highest)).reshape(
         die_count, TILE, TILE
     )
     return (heat_field, adjoint, die_grad)

time: 279 us -> 277 us (level)
  blocking collectives: 67.4 us -> 0 us
  waiting for transfers between devices: 39.9 us -> 89.8 us
  starting transfers between devices: 67.7 us -> 84.7 us
  local copies, waits for them, and re-layouts: 37.4 us -> 33.5 us
    all_to_all x1 -> x0, blocking collectives: 67.4 us -> none  [return_grads(): lax.all_to_all(backward.reshape(row_count * col_count, CAP, -1), ('row',...]
    all_to_all x0 -> x1, waiting for transfers between devices: none -> 50.6 us  [on_device(): lax.all_to_all(backward, ('row', 'col'), split_axis=0, concat_axis=0, til...]
    all_to_all x0 -> x1, starting transfers between devices: none -> 17 us  [on_device(): lax.all_to_all(backward, ('row', 'col'), split_axis=0, concat_axis=0, til...]
    reshape x2 -> x1, local copies, waits for them, and re-layouts: 8.25 us -> 2.16 us  [on_device(): (RATE * jnp.einsum('dck,dcn->kn', send_hot, returned, precision=highest))...]
  transfers between devices with their start and end apart: 17 -> 18, of which waited for: 6 -> 6; matrix products, arithmetic and copies ran while one was open for 8% -> 8% of each run, Pallas kernels for 0% -> 0%
where the time goes in v9:
time: 277 us; the launch traced here: 272 us
  waiting for transfers between devices  89.8 us (32%)
  starting transfers between devices  84.7 us (31%)
  Pallas kernels  39.8 us (14%)
  local copies, waits for them, and re-layouts  33.5 us (12%)
  matrix products  15.6 us (6%)
  other arithmetic  7.76 us (3%)
    all_to_all x1, waiting for transfers between devices, on_device(): lax.all_to_all(backward, ('row', 'col'), split_axis=0, concat_axis=0, til...  50.6 us
    pallas_call x1, Pallas kernels, run_solve(): pl.pallas_call(solve_kernel, out_shape=(field, field, jax.ShapeDtypeStruc...  39.8 us
    ppermute x4, waiting for transfers between devices, framed(): lax.ppermute(jnp.swapaxes(cells[:, :, :HALO], 1, 2), 'col', [(i + 1, i) f...  35.1 us
    ppermute x4, starting transfers between devices, framed(): lax.ppermute(jnp.swapaxes(cells[:, :, breadth - HALO:], 1, 2), 'col', [(i...  23.3 us
    all_to_all x1, starting transfers between devices, on_device(): lax.all_to_all(backward, ('row', 'col'), split_axis=0, concat_axis=0, til...  17 us
    ppermute x4, starting transfers between devices, framed(): lax.ppermute(band[:, height - HALO:], 'row', [(i, i + 1) for i in range(r...  13.4 us
    ppermute x4, starting transfers between devices, framed(): lax.ppermute(band[:, :HALO], 'row', [(i + 1, i) for i in range(rows - 1)])  11.8 us
    all_to_all x1, starting transfers between devices, send_dies(): lax.all_to_all(outbound.reshape(row_count * col_count, CAP, -1), ('row',...  11 us
  transfers between devices with their start and end apart: 18, of which 6 were waited for; matrix products, arithmetic and copies ran while one was open for 8% of the time, Pallas kernels for 0%

profile of v9, /device:TPU:15, one launch (start us, length us, event | category | flops | bytes accessed | tf_op | source)
XLA Modules:
  0.0 272.4 jit_solution(3791488379935186070)
XLA Ops:
  1.3 0.8 convert_reduce_fusion
  2.1 0.7 multiply_add_fusion.1
  2.8 2.1 reshape.123
  4.9 0.7 fusion.21
  5.7 3.8 %fusion.4 = f32[256,4224]{1,0:T(8,128)} fusion(f32[64,1]{1,0:T(8,128)S(1)} %copy.32, f32[64,4096]{1,0:T(8,128)S(1)} %reshape.123, s32[64]{0:T(128)S(1)} %multiply_add_fusion.1), kind=kOutput, calls=%fused_computation.9 | convolution fusion | flops 831299584 | bytes 5374464 | tf_op jit(solution)/shard_map/dot_general | solution.py:287
  9.5 6.0 %reshape.125 = f32[128,2,4224]{2,1,0:T(2,128)} reshape(f32[256,4224]{1,0:T(8,128)} %fusion.4) | data formatting | bytes 8650752 | tf_op jit(solution)/shard_map/reshape | solution.py:248
  15.5 11.0 %all-to-all-start = ((f32[128,2,4224]{2,1,0:T(2,128)}), f32[128,2,4224]{2,1,0:T(2,128)}, u32[]{:S(2)}, u32[]{:S(2)}) async-start(f32[128,2,4224]{2,1,0:T(2,128)} %reshape.125), calls=%async_computation | async-start | bytes 8650752 | tf_op jit(solution)/shard_map/all_to_all | solution.py:247
  26.9 2.1 add_sqrt_fusion
  29.2 2.3 collective-permute-start.4
  31.5 6.9 %collective-permute-start.5 = (f32[4,16,256]{1,2,0:T(8,128)S(1)}, f32[4,16,256]{1,2,0:T(8,128)S(1)}, u32[]{:S(2)}, u32[]{:S(2)}) collective-permute-start(f32[4,16,256]{1,2,0:T(8,128)S(1)} %get-tuple-element.34), channel_id=1, source_target_pairs={{0,1},{1,2},{2,3},{3,4},{4,5},{5,6},{6,7},{7,8},{8,9},{9,10},{10,1... | collective-permute-start | bytes 196616 | tf_op jit(solution)/shard_map/ppermute | solution.py:72
  38.6 1.9 collective-permute-start
  40.5 7.3 %collective-permute-start.1 = (f32[4,16,256]{1,2,0:T(8,128)S(1)}, f32[4,16,256]{1,2,0:T(8,128)S(1)}, u32[]{:S(2)}, u32[]{:S(2)}) collective-permute-start(f32[4,16,256]{1,2,0:T(8,128)S(1)} %get-tuple-element.36), channel_id=1, source_target_pairs={{0,1},{1,2},{2,3},{3,4},{4,5},{5,6},{6,7},{7,8},{8,9},{9,10},{10,1... | collective-permute-start | bytes 196616 | tf_op jit(solution)/shard_map/ppermute | solution.py:72
  47.8 0.8 slice_bitcast_fusion.5
  48.6 1.9 collective-permute-start.12
  51.2 0.7 constant_dynamic-update-slice_fusion.4
  51.8 31.4 %collective-permute-done.4 = f32[4,16,256]{1,2,0:T(8,128)S(1)} collective-permute-done((f32[4,16,256]{1,2,0:T(8,128)S(1)}, f32[4,16,256]{1,2,0:T(8,128)S(1)}, u32[]{:S(2)}, u32[]{:S(2)}) %collective-permute-start.4) | collective-permute-done | bytes 65568 | tf_op jit(solution)/shard_map/ppermute | solution.py:75
  83.3 1.9 collective-permute-start.13
  85.2 3.7 %collective-permute-done = f32[4,16,256]{1,2,0:T(8,128)S(1)} collective-permute-done((f32[4,16,256]{1,2,0:T(8,128)S(1)}, f32[4,16,256]{1,2,0:T(8,128)S(1)}, u32[]{:S(2)}, u32[]{:S(2)}) %collective-permute-start) | collective-permute-done | bytes 65568 | tf_op jit(solution)/shard_map/ppermute | solution.py:75
  88.9 0.8 pad_maximum_fusion.1
  89.7 4.7 %collective-permute-start.6 = (f32[4,16,640]{2,1,0:T(8,128)S(1)}, f32[4,16,640]{2,1,0:T(8,128)S(1)}, u32[]{:S(2)}, u32[]{:S(2)}) collective-permute-start(f32[4,16,640]{2,1,0:T(8,128)S(1)} %get-tuple-element.30), channel_id=1, source_target_pairs={{0,16},{16,32},{32,48},{48,64},{64,80},{80,96},{96,112},{1,17},{17... | collective-permute-start | bytes 491528 | tf_op jit(solution)/shard_map/ppermute | solution.py:80
  94.5 3.2 %collective-permute-start.7 = (f32[4,16,640]{2,1,0:T(8,128)S(1)}, f32[4,16,640]{2,1,0:T(8,128)S(1)}, u32[]{:S(2)}, u32[]{:S(2)}) collective-permute-start(f32[4,16,640]{2,1,0:T(8,128)S(1)} %get-tuple-element.29), channel_id=1, source_target_pairs={{16,0},{32,16},{48,32},{64,48},{80,64},{96,80},{112,96},{17,1},{33... | collective-permute-start | bytes 491528 | tf_op jit(solution)/shard_map/ppermute | solution.py:81
  97.7 2.0 collective-permute-start.2
  99.8 3.4 %collective-permute-start.3 = (f32[4,16,640]{2,1,0:T(8,128)S(1)}, f32[4,16,640]{2,1,0:T(8,128)S(1)}, u32[]{:S(2)}, u32[]{:S(2)}) collective-permute-start(f32[4,16,640]{2,1,0:T(8,128)S(1)} %get-tuple-element.31), channel_id=1, source_target_pairs={{16,0},{32,16},{48,32},{64,48},{80,64},{96,80},{112,96},{17,1},{33... | collective-permute-start | bytes 491528 | tf_op jit(solution)/shard_map/ppermute | solution.py:81
  104.1 1.1 constant_dynamic-update-slice_fusion.3
  105.2 1.7 constant_dynamic-update-slice_fusion.2
  106.9 0.7 constant_dynamic-update-slice_fusion.1
  107.6 6.3 %reshape.126 = f32[256,4224]{1,0:T(8,128)} reshape(f32[128,2,4224]{2,1,0:T(2,128)} %all-to-all-done) | data formatting | bytes 8650752 | tf_op jit(solution)/shard_map/reshape | solution.py:254
  113.9 1.0 fusion.10
  114.9 3.8 %fusion.1 = f32[32,4096]{1,0:T(8,128)S(1)} fusion(f32[256,4224]{1,0:T(8,128)} %reshape.126, s32[256]{0:T(256)S(1)} %fusion.10), kind=kOutput, calls=%fused_computation.2 | convolution fusion | flops 402661376 | bytes 4719616 | tf_op jit(solution)/shard_map/dot_general | solution.py:293
  120.1 2.1 collective-permute-start.8
  122.2 7.3 %collective-permute-start.9 = (f32[1,16,256]{1,2,0:T(8,128)S(1)}, f32[1,16,256]{1,2,0:T(8,128)S(1)}, u32[]{:S(2)}, u32[]{:S(2)}) collective-permute-start(f32[1,16,256]{1,2,0:T(8,128)S(1)} %get-tuple-element.44), channel_id=1, source_target_pairs={{0,1},{1,2},{2,3},{3,4},{4,5},{5,6},{6,7},{7,8},{8,9},{9,10},{10,1... | collective-permute-start | bytes 49160 | tf_op jit(solution)/shard_map/ppermute | solution.py:72
  129.4 0.6 constant_dynamic-update-slice_fusion.f_ref
  130.3 1.0 collective-permute-done.9
  131.4 1.1 pad_maximum_fusion.3
  132.5 2.3 collective-permute-start.14
  134.7 3.0 %collective-permute-start.15 = (f32[1,16,640]{2,1,0:T(8,128)S(1)}, f32[1,16,640]{2,1,0:T(8,128)S(1)}, u32[]{:S(2)}, u32[]{:S(2)}) collective-permute-start(f32[1,16,640]{2,1,0:T(8,128)S(1)} %get-tuple-element.37), channel_id=1, source_target_pairs={{16,0},{32,16},{48,32},{64,48},{80,64},{96,80},{112,96},{17,1},{33... | collective-permute-start | bytes 122888 | tf_op jit(solution)/shard_map/ppermute | solution.py:81
  137.8 4.4 %collective-permute-start.10 = (f32[1,16,640]{2,1,0:T(8,128)S(1)}, f32[1,16,640]{2,1,0:T(8,128)S(1)}, u32[]{:S(2)}, u32[]{:S(2)}) collective-permute-start(f32[1,16,640]{2,1,0:T(8,128)S(1)} %get-tuple-element.40), channel_id=1, source_target_pairs={{0,16},{16,32},{32,48},{48,64},{64,80},{80,96},{96,112},{1,17},{17... | collective-permute-start | bytes 122888 | tf_op jit(solution)/shard_map/ppermute | solution.py:80
  142.2 2.1 collective-permute-start.11
  144.5 2.4 collective-permute-done.11
  146.9 0.9 copy-done.4
  147.8 39.8 %shard_map.94 = (f32[4,256,512]{2,1,0:T(8,128)}, f32[4,256,512]{2,1,0:T(8,128)}, f32[256,512]{1,0:T(8,128)}) custom-call(f32[4,304,640]{2,1,0:T(8,128)} %constant_dynamic-update-slice_fusion.f_ref, f32[4,304,640]{2,1,0:T(8,128)} %copy-done.1, f32[304,640]{1,0:T(8,128)} %bitcast.53, f32[304,640]{1,0:T(8,128)} %bitcast.54), custom_call_target="tpu_custom_call" | custom-call | tf_op jit(solution)/shard_map/pallas_call | solution.py:236
  187.6 1.2 reshape.128
  189.4 1.8 fusion.17
  191.3 5.2 %copy.30 = f32[128,2,4096]{2,1,0:T(2,128)} copy(f32[128,2,4096]{2,0,1:T(8,128)S(1)} %fusion.17) | data formatting | bytes 8388608 | tf_op jit(solution)/shard_map/tdc,tn->dcn/dot_general | solution.py:311
  196.5 17.0 %all-to-all-start.1 = ((f32[128,2,4096]{2,1,0:T(2,128)}), f32[128,2,4096]{2,1,0:T(2,128)}, u32[]{:S(2)}, u32[]{:S(2)}) async-start(f32[128,2,4096]{2,1,0:T(2,128)} %copy.30), calls=%async_computation.1 | async-start | bytes 8388608 | tf_op jit(solution)/shard_map/all_to_all | solution.py:312
  213.5 50.6 %all-to-all-done.1 = f32[128,2,4096]{2,1,0:T(2,128)} async-done(((f32[128,2,4096]{2,1,0:T(2,128)}), f32[128,2,4096]{2,1,0:T(2,128)}, u32[]{:S(2)}, u32[]{:S(2)}) %all-to-all-start.1) | async-done | bytes 4194336 | tf_op jit(solution)/shard_map/all_to_all | solution.py:312
  264.1 6.1 %fusion = f32[64,4096]{1,0:T(8,128)S(1)} fusion(f32[128,2,4096]{2,1,0:T(2,128)} %all-to-all-done.1, s32[128,2]{0,1:T(2,128)S(1)} %multiply_add_fusion, s32[64]{0:T(128)S(1)} %multiply_add_fusion.1), kind=kOutput, calls=%fused_computation.1 | convolution fusion | flops 805584896 | bytes 5244160 | tf_op jit(solution)/shard_map/dck,dcn->kn/dot_general | solution.py:314
  270.2 2.2 reshape.130
  (65 shorter events, 5.3 us)
Async XLA Ops:
  0.6 4.3 %copy-start.8 = (s32[64]{0:T(128)S(1)}, s32[64]{0:T(128)}, u32[]{:S(2)}) copy-start(s32[64]{0:T(128)} %param.12) | copy-start | bytes 772
  15.5 11.1 %copy-start.7 = (f32[4,8]{1,0:T(4,128)S(1)}, f32[4,8]{1,0:T(4,128)}, u32[]{:S(2)}) copy-start(f32[4,8]{1,0:T(4,128)} %param.14) | copy-start | bytes 388
  15.5 11.4 %copy-start.2 = (s32[4,256,512]{2,1,0:T(8,128)S(1)}, s32[4,256,512]{2,1,0:T(8,128)}, u32[]{:S(2)}) copy-start(s32[4,256,512]{2,1,0:T(8,128)} %param.13) | copy-start | bytes 6291460
  15.5 92.1 %all-to-all-start = ((f32[128,2,4224]{2,1,0:T(2,128)}), f32[128,2,4224]{2,1,0:T(2,128)}, u32[]{:S(2)}, u32[]{:S(2)}) async-start(f32[128,2,4224]{2,1,0:T(2,128)} %reshape.125), calls=%async_computation | async-start | bytes 8650752 | tf_op jit(solution)/shard_map/all_to_all | solution.py:247
  26.9 11.5 %copy-start = (f32[4,256,512]{2,1,0:T(8,128)S(1)}, f32[4,256,512]{2,1,0:T(8,128)}, u32[]{:S(2)}) copy-start(f32[4,256,512]{2,1,0:T(8,128)} %param.9) | copy-start | bytes 6291460
  29.0 18.8 %copy-start.3 = (f32[256,512]{1,0:T(8,128)S(1)}, f32[256,512]{1,0:T(8,128)}, u32[]{:S(2)}) copy-start(f32[256,512]{1,0:T(8,128)} %param.15) | copy-start | bytes 1572868
  29.2 54.1 %collective-permute-start.4 = (f32[4,16,256]{1,2,0:T(8,128)S(1)}, f32[4,16,256]{1,2,0:T(8,128)S(1)}, u32[]{:S(2)}, u32[]{:S(2)}) collective-permute-start(f32[4,16,256]{1,2,0:T(8,128)S(1)} %get-tuple-element.33), channel_id=1, source_target_pairs={{1,0},{2,1},{3,2},{4,3},{5,4},{6,5},{7,6},{8,7},{9,8},{10,9},{11,1... | collective-permute-start | bytes 196616 | tf_op jit(solution)/shard_map/ppermute | solution.py:75
  31.5 53.7 %collective-permute-start.5 = (f32[4,16,256]{1,2,0:T(8,128)S(1)}, f32[4,16,256]{1,2,0:T(8,128)S(1)}, u32[]{:S(2)}, u32[]{:S(2)}) collective-permute-start(f32[4,16,256]{1,2,0:T(8,128)S(1)} %get-tuple-element.34), channel_id=1, source_target_pairs={{0,1},{1,2},{2,3},{3,4},{4,5},{5,6},{6,7},{7,8},{8,9},{9,10},{10,1... | collective-permute-start | bytes 196616 | tf_op jit(solution)/shard_map/ppermute | solution.py:72
  38.6 50.3 %collective-permute-start = (f32[4,16,256]{1,2,0:T(8,128)S(1)}, f32[4,16,256]{1,2,0:T(8,128)S(1)}, u32[]{:S(2)}, u32[]{:S(2)}) collective-permute-start(f32[4,16,256]{1,2,0:T(8,128)S(1)} %get-tuple-element.35), channel_id=1, source_target_pairs={{1,0},{2,1},{3,2},{4,3},{5,4},{6,5},{7,6},{8,7},{9,8},{10,9},{11,1... | collective-permute-start | bytes 196616 | tf_op jit(solution)/shard_map/ppermute | solution.py:75
  40.5 48.4 %collective-permute-start.1 = (f32[4,16,256]{1,2,0:T(8,128)S(1)}, f32[4,16,256]{1,2,0:T(8,128)S(1)}, u32[]{:S(2)}, u32[]{:S(2)}) collective-permute-start(f32[4,16,256]{1,2,0:T(8,128)S(1)} %get-tuple-element.36), channel_id=1, source_target_pairs={{0,1},{1,2},{2,3},{3,4},{4,5},{5,6},{6,7},{7,8},{8,9},{9,10},{10,1... | collective-permute-start | bytes 196616 | tf_op jit(solution)/shard_map/ppermute | solution.py:72
  48.6 81.7 %collective-permute-start.12 = (f32[1,16,256]{1,2,0:T(8,128)}, f32[1,16,256]{1,2,0:T(8,128)S(1)}, u32[]{:S(2)}, u32[]{:S(2)}) collective-permute-start(f32[1,16,256]{1,2,0:T(8,128)} %get-tuple-element.41), channel_id=1, source_target_pairs={{1,0},{2,1},{3,2},{4,3},{5,4},{6,5},{7,6},{8,7},{9,8},{10,9},{11,1... | collective-permute-start | bytes 49160 | tf_op jit(solution)/shard_map/ppermute | solution.py:75
  83.3 47.0 %collective-permute-start.13 = (f32[1,16,256]{1,2,0:T(8,128)}, f32[1,16,256]{1,2,0:T(8,128)}, u32[]{:S(2)}, u32[]{:S(2)}) collective-permute-start(f32[1,16,256]{1,2,0:T(8,128)} %get-tuple-element.42), channel_id=1, source_target_pairs={{0,1},{1,2},{2,3},{3,4},{4,5},{5,6},{6,7},{7,8},{8,9},{9,10},{10,1... | collective-permute-start | bytes 49160 | tf_op jit(solution)/shard_map/ppermute | solution.py:72
  89.7 10.1 %collective-permute-start.6 = (f32[4,16,640]{2,1,0:T(8,128)S(1)}, f32[4,16,640]{2,1,0:T(8,128)S(1)}, u32[]{:S(2)}, u32[]{:S(2)}) collective-permute-start(f32[4,16,640]{2,1,0:T(8,128)S(1)} %get-tuple-element.30), channel_id=1, source_target_pairs={{0,16},{16,32},{32,48},{48,64},{64,80},{80,96},{96,112},{1,17},{17... | collective-permute-start | bytes 491528 | tf_op jit(solution)/shard_map/ppermute | solution.py:80
  94.5 9.0 %collective-permute-start.7 = (f32[4,16,640]{2,1,0:T(8,128)S(1)}, f32[4,16,640]{2,1,0:T(8,128)S(1)}, u32[]{:S(2)}, u32[]{:S(2)}) collective-permute-start(f32[4,16,640]{2,1,0:T(8,128)S(1)} %get-tuple-element.29), channel_id=1, source_target_pairs={{16,0},{32,16},{48,32},{64,48},{80,64},{96,80},{112,96},{17,1},{33... | collective-permute-start | bytes 491528 | tf_op jit(solution)/shard_map/ppermute | solution.py:81
  97.7 6.4 %collective-permute-start.2 = (f32[4,16,640]{2,1,0:T(8,128)S(1)}, f32[4,16,640]{2,1,0:T(8,128)S(1)}, u32[]{:S(2)}, u32[]{:S(2)}) collective-permute-start(f32[4,16,640]{2,1,0:T(8,128)S(1)} %get-tuple-element.32), channel_id=1, source_target_pairs={{0,16},{16,32},{32,48},{48,64},{64,80},{80,96},{96,112},{1,17},{17... | collective-permute-start | bytes 491528 | tf_op jit(solution)/shard_map/ppermute | solution.py:80
  99.8 7.1 %collective-permute-start.3 = (f32[4,16,640]{2,1,0:T(8,128)S(1)}, f32[4,16,640]{2,1,0:T(8,128)S(1)}, u32[]{:S(2)}, u32[]{:S(2)}) collective-permute-start(f32[4,16,640]{2,1,0:T(8,128)S(1)} %get-tuple-element.31), channel_id=1, source_target_pairs={{16,0},{32,16},{48,32},{64,48},{80,64},{96,80},{112,96},{17,1},{33... | collective-permute-start | bytes 491528 | tf_op jit(solution)/shard_map/ppermute | solution.py:81
  103.5 3.4 %copy-start.1 = (f32[4,304,640]{2,1,0:T(8,128)}, f32[4,304,640]{2,1,0:T(8,128)S(1)}, u32[]{:S(2)}) copy-start(f32[4,304,640]{2,1,0:T(8,128)S(1)} %constant_dynamic-update-slice_fusion.5.r_ref) | copy-start | bytes 9338884
  120.0 24.3 %copy-start.5 = (f32[1,304,640]{2,1,0:T(8,128)S(1)}, f32[1,304,640]{2,1,0:T(8,128)}, u32[]{:S(2)}) copy-start(f32[1,304,640]{2,1,0:T(8,128)} %constant_dynamic-update-slice_fusion.19) | copy-start | bytes 2334724
  120.1 10.2 %collective-permute-start.8 = (f32[1,16,256]{1,2,0:T(8,128)S(1)}, f32[1,16,256]{1,2,0:T(8,128)S(1)}, u32[]{:S(2)}, u32[]{:S(2)}) collective-permute-start(f32[1,16,256]{1,2,0:T(8,128)S(1)} %get-tuple-element.43), channel_id=1, source_target_pairs={{1,0},{2,1},{3,2},{4,3},{5,4},{6,5},{7,6},{8,7},{9,8},{10,9},{11,1... | collective-permute-start | bytes 49160 | tf_op jit(solution)/shard_map/ppermute | solution.py:75
  122.2 9.2 %collective-permute-start.9 = (f32[1,16,256]{1,2,0:T(8,128)S(1)}, f32[1,16,256]{1,2,0:T(8,128)S(1)}, u32[]{:S(2)}, u32[]{:S(2)}) collective-permute-start(f32[1,16,256]{1,2,0:T(8,128)S(1)} %get-tuple-element.44), channel_id=1, source_target_pairs={{0,1},{1,2},{2,3},{3,4},{4,5},{5,6},{6,7},{7,8},{8,9},{9,10},{10,1... | collective-permute-start | bytes 49160 | tf_op jit(solution)/shard_map/ppermute | solution.py:72
  132.5 11.8 %collective-permute-start.14 = (f32[1,16,640]{2,1,0:T(8,128)S(1)}, f32[1,16,640]{2,1,0:T(8,128)S(1)}, u32[]{:S(2)}, u32[]{:S(2)}) collective-permute-start(f32[1,16,640]{2,1,0:T(8,128)S(1)} %get-tuple-element.38), channel_id=1, source_target_pairs={{0,16},{16,32},{32,48},{48,64},{64,80},{80,96},{96,112},{1,17},{17... | collective-permute-start | bytes 122888 | tf_op jit(solution)/shard_map/ppermute | solution.py:80
  134.7 9.7 %collective-permute-start.15 = (f32[1,16,640]{2,1,0:T(8,128)S(1)}, f32[1,16,640]{2,1,0:T(8,128)S(1)}, u32[]{:S(2)}, u32[]{:S(2)}) collective-permute-start(f32[1,16,640]{2,1,0:T(8,128)S(1)} %get-tuple-element.37), channel_id=1, source_target_pairs={{16,0},{32,16},{48,32},{64,48},{80,64},{96,80},{112,96},{17,1},{33... | collective-permute-start | bytes 122888 | tf_op jit(solution)/shard_map/ppermute | solution.py:81
  137.8 6.6 %collective-permute-start.10 = (f32[1,16,640]{2,1,0:T(8,128)S(1)}, f32[1,16,640]{2,1,0:T(8,128)S(1)}, u32[]{:S(2)}, u32[]{:S(2)}) collective-permute-start(f32[1,16,640]{2,1,0:T(8,128)S(1)} %get-tuple-element.40), channel_id=1, source_target_pairs={{0,16},{16,32},{32,48},{48,64},{64,80},{80,96},{96,112},{1,17},{17... | collective-permute-start | bytes 122888 | tf_op jit(solution)/shard_map/ppermute | solution.py:80
  142.2 4.7 %collective-permute-start.11 = (f32[1,16,640]{2,1,0:T(8,128)S(1)}, f32[1,16,640]{2,1,0:T(8,128)S(1)}, u32[]{:S(2)}, u32[]{:S(2)}) collective-permute-start(f32[1,16,640]{2,1,0:T(8,128)S(1)} %get-tuple-element.39), channel_id=1, source_target_pairs={{16,0},{32,16},{48,32},{64,48},{80,64},{96,80},{112,96},{17,1},{33... | collective-permute-start | bytes 122888 | tf_op jit(solution)/shard_map/ppermute | solution.py:81
  144.5 2.4 copy-start.6
  146.9 0.9 copy-start.4
  196.5 67.6 %all-to-all-start.1 = ((f32[128,2,4096]{2,1,0:T(2,128)}), f32[128,2,4096]{2,1,0:T(2,128)}, u32[]{:S(2)}, u32[]{:S(2)}) async-start(f32[128,2,4096]{2,1,0:T(2,128)} %copy.30), calls=%async_computation.1 | async-start | bytes 8388608 | tf_op jit(solution)/shard_map/all_to_all | solution.py:312
